TPU v7x, 256 devices: a whole 4x4x8 slice. The times are simulated.
256 devices in a mesh: ops: 16 (over z_lo, x, core), sec: 16 (over z_hi, y).
Axes of the slice: x: 4, y: 4, z: 8 (z_hi: 4, z_lo: 2; z = z_hi * 2 + z_lo), core: 2. Of those that a mesh axis runs over, the one named last changes fastest.
Arguments:
- wavefunction: float32 [16, 256, 1024], P('sec', 'ops'), may hold values from -8 to 8
- left_ops: float32 [16, 16, 256, 256], P('ops', 'sec'), may hold values from -0.375 to 0.375
- right_ops: float32 [16, 256, 256], P('ops'), may hold values from -0.375 to 0.375
- site_ops: float32 [16, 4, 4], P('ops'), may hold values from -3 to 3
- pattern: int32 [16, 16], P('ops', 'sec'), may hold values 0 or 1
- sector_sizes: int32 [16], P('sec'), may hold values from 1 to 256, 3072 in all
- owner: int32 [16], P('ops'), may hold values from 0 to 15
- slot: int32 [16], P('ops'), may hold values from 0 to 1
Outputs:
- basis: float32 [16, 256, 1024], P('sec', 'ops')
- complementary: float32 [16, 2, 256, 256], P('ops', None, 'sec')
Inputs may be any that keep to these rules, and one draw needn't show every extreme that they name: `sector_sizes`: each sector has at least one live state; some sector has all 256.
All inputs are finite; a program needn't handle non-finite values. No bound on the sum of `pattern` or of `sector_sizes` on one device may be relied on, other than what follows from the above.
Results may differ from a plain program's by a relative error of at most 0.0003.
Values sent between devices are 32-bit elements; how exact they have to be, the bound alone decides.
No kernel may reach another device: no remote copies, remote signals or barrier semaphores. Data moves between devices by JAX's collectives and lax.ppermute only.
A program may use at most 64 MiB of HBM per device.

v0:
```python
import jax
import jax.numpy as jnp
from jax import lax
from jax.sharding import PartitionSpec as P

SLOTS = 2


highest = lax.Precision.HIGHEST


def copy_for_each(shard, axis):
    copies = jnp.broadcast_to(shard, (lax.axis_size(axis), *shard.shape))
    return lax.all_to_all(copies, axis, split_axis=0, concat_axis=0, tiled=True)


def in_order(blocks, dim):
    blocks = jnp.moveaxis(blocks, 0, dim)
    shape = blocks.shape
    return blocks.reshape(*shape[:dim], shape[dim] * shape[dim + 1], *shape[dim + 2 :])


def gathered_copies(shard, axis, dim):
    blocks = copy_for_each(shard, axis)
    return in_order(blocks, dim)


def in_blocks(shard, dim, count):
    shape = shard.shape
    blocks = shard.reshape(*shape[:dim], count, shape[dim] // count, *shape[dim + 1 :])
    return jnp.moveaxis(blocks, dim, 0)


def sum_at_owner(shard, axis, dim):
    blocks = in_blocks(shard, dim, lax.axis_size(axis))
    arrived = lax.all_to_all(blocks, axis, split_axis=0, concat_axis=0, tiled=True)
    return arrived.sum(axis=0)


def rows_for(lines, count):
    spare = -lines.shape[0] % count
    if not spare:
        return lines
    return jnp.concatenate([lines, jnp.zeros((spare, *lines.shape[1:]), lines.dtype)])


def total_of(shard, axes):
    lines = shard.reshape(-1, shard.shape[-1])
    own = sum_at_owner(rows_for(lines, lax.axis_size(axes)), axes, 0)
    whole = gathered_copies(own, axes, 0)
    return whole[: len(lines)].reshape(shard.shape)


def body(wavefunction, left_ops, right_ops, site_ops, pattern, sector_sizes, owner, slot):
    ops_count = lax.axis_size("ops")
    sec_count = lax.axis_size("sec")
    row_share = wavefunction.shape[1]
    states = row_share * ops_count
    width_all = wavefunction.shape[2]
    columns = width_all // 4
    pair_count = left_ops.shape[0]
    live_all = (jnp.arange(states, dtype=jnp.int32) < sector_sizes[0]).astype(jnp.float32)
    left_block = left_ops[:, 0] * pattern[:, 0][:, None, None].astype(jnp.float32)
    row_start = lax.axis_index("ops") * row_share
    portion = gathered_copies(wavefunction, "ops", 1)
    number = portion.shape[1]
    source = (portion[0] * live_all[:, None]).reshape(number, 4, columns)
    mapped = jnp.einsum("mqc,kcd->kmqd", source, right_ops, precision=highest)
    mapped = jnp.einsum("kpq,kmqd->kmpd", site_ops, mapped, precision=highest)
    mixed_all = mapped.reshape(pair_count, number, width_all)
    total_rows = 4 * states * sec_count
    scale = jnp.sqrt(jnp.float32(total_rows))
    summed = jnp.einsum("kmn,knw->mw", left_block, mixed_all, precision=highest)
    summed = total_of(summed, "ops")
    flat = (summed * live_all[:, None]).reshape(states * 4, columns)
    local_gram = jnp.dot(flat.T, flat, precision=highest, preferred_element_type=jnp.float32)
    gram = total_of(local_gram, "sec")
    factor = jnp.linalg.cholesky(gram)
    ortho_full = jax.scipy.linalg.solve_triangular(factor, flat.T, lower=True).T
    ortho_full = ortho_full.reshape(states, width_all)
    ortho_share = lax.dynamic_slice_in_dim(ortho_full, row_start, row_share, 0)
    basis = (ortho_share * scale).reshape(1, row_share, width_all)
    frame = ortho_full.reshape(states, 4, columns)
    moved = jnp.einsum("kmn,nqd->kmqd", left_block, frame, precision=highest)
    moved = jnp.einsum("kpq,kmqd->kmpd", site_ops, moved, precision=highest)
    renorm = jnp.einsum("mpc,kmpd->kcd", frame, moved, precision=highest)
    sector_sum = sum_at_owner(renorm, "sec", 1)
    target = owner * SLOTS + slot
    select = (target[:, None] == jnp.arange(ops_count * SLOTS, dtype=jnp.int32)[None, :]).astype(
        jnp.float32
    )
    routed = jnp.einsum("kj,kcd->jcd", select, sector_sum, precision=highest)
    routed = routed.reshape(ops_count, SLOTS, sector_sum.shape[1], columns)
    complementary = sum_at_owner(routed, "ops", 0)
    return (basis, complementary)


def solution(mesh):
    placed = (
        P("sec", "ops", None),
        P("ops", "sec", None, None),
        P("ops", None, None),
        P("ops", None, None),
        P("ops", "sec"),
        P("sec"),
        P("ops"),
        P("ops"),
    )
    return jax.shard_map(
        body,
        mesh=mesh,
        in_specs=placed,
        out_specs=(P("sec", "ops", None), P("ops", None, "sec", None)),
        check_vma=False,
    )
```

profile of v0, /device:TPU:1, one launch (start us, length us, event | category | flops | bytes accessed | tf_op | source)
XLA Modules:
  0.0 214.1 jit_solution(2830286021027251761)
XLA Ops:
  0.6 2.0 broadcast_in_dim.8
  2.6 7.3 %all-to-all-start = ((f32[16,1,16,1024]{3,2,1,0:T(8,128)}), f32[16,1,16,1024]{3,2,1,0:T(8,128)S(1)}, u32[]{:S(2)}, u32[]{:S(2)}) async-start(f32[16,1,16,1024]{3,2,1,0:T(8,128)} %broadcast_in_dim.8), calls=%async_computation | async-start | bytes 2097152 | tf_op jit(solution)/shard_map/all_to_all | solution.py:14
  11.3 14.3 %all-to-all-done = f32[16,1,16,1024]{3,2,1,0:T(8,128)S(1)} async-done(((f32[16,1,16,1024]{3,2,1,0:T(8,128)}), f32[16,1,16,1024]{3,2,1,0:T(8,128)S(1)}, u32[]{:S(2)}, u32[]{:S(2)}) %all-to-all-start) | async-done | bytes 1048608 | tf_op jit(solution)/shard_map/all_to_all | solution.py:14
  26.3 1.0 fusion.4
  27.3 2.5 %convolution_bitcast_fusion.1 = f32[1,256,4,256]{3,2,1,0:T(4,128)S(1)} fusion(f32[256,4,256]{2,0,1:T(8,128)S(1)} %fusion.4, f32[1,4,4]{2,1,0:T(4,128)S(1)} %copy-done.3), kind=kOutput, calls=%fused_computation.3 | convolution fusion | flops 12582912 | bytes 2097216 | tf_op jit(solution)/shard_map/kpq,kmqd->kmpd/dot_general | solution.py:69
  30.3 1.0 fusion.22
  31.4 18.8 %all_to_all.35 = f32[16,16,1024]{2,1,0:T(8,128)S(1)} all-to-all(f32[16,16,1024]{2,1,0:T(8,128)S(1)} %fusion.22), channel_id=1, replica_groups=mesh['ops'=16,'sec'=16] {'ops'}, dimensions={0} | all-to-all | bytes 2097152 | tf_op jit(solution)/shard_map/all_to_all | solution.py:36
  50.2 1.1 broadcast_in_dim.16
  51.3 4.7 %all-to-all-start.2 = ((f32[16,16,1024]{2,1,0:T(8,128)}), f32[16,16,1024]{2,1,0:T(8,128)S(1)}, u32[]{:S(2)}, u32[]{:S(2)}) async-start(f32[16,16,1024]{2,1,0:T(8,128)} %broadcast_in_dim.16), calls=%async_computation.2 | async-start | bytes 2097152 | tf_op jit(solution)/shard_map/all_to_all | solution.py:14
  56.3 15.5 %all-to-all-done.2 = f32[16,16,1024]{2,1,0:T(8,128)S(1)} async-done(((f32[16,16,1024]{2,1,0:T(8,128)}), f32[16,16,1024]{2,1,0:T(8,128)S(1)}, u32[]{:S(2)}, u32[]{:S(2)}) %all-to-all-start.2) | async-done | bytes 1048608 | tf_op jit(solution)/shard_map/all_to_all | solution.py:14
  73.0 1.0 fusion.23
  74.0 19.9 %all_to_all.36 = f32[16,16,256]{2,1,0:T(8,128)S(1)} all-to-all(f32[16,16,256]{2,1,0:T(8,128)S(1)} %fusion.23), channel_id=1, replica_groups=mesh['ops'=16,'sec'=16] {'sec'}, dimensions={0} | all-to-all | bytes 524288 | tf_op jit(solution)/shard_map/all_to_all | solution.py:36
  93.9 0.7 broadcast_in_dim.17
  94.6 6.4 %all-to-all-start.4 = ((f32[16,16,256]{2,1,0:T(8,128)}), f32[16,16,256]{2,1,0:T(8,128)S(1)}, u32[]{:S(2)}, u32[]{:S(2)}) async-start(f32[16,16,256]{2,1,0:T(8,128)} %broadcast_in_dim.17), calls=%async_computation.4 | async-start | bytes 524288 | tf_op jit(solution)/shard_map/all_to_all | solution.py:14
  101.2 11.2 %all-to-all-done.4 = f32[16,16,256]{2,1,0:T(8,128)S(1)} async-done(((f32[16,16,256]{2,1,0:T(8,128)}), f32[16,16,256]{2,1,0:T(8,128)S(1)}, u32[]{:S(2)}, u32[]{:S(2)}) %all-to-all-start.4) | async-done | bytes 262176 | tf_op jit(solution)/shard_map/all_to_all | solution.py:14
  112.5 11.7 %cholesky.50 = f32[128,128]{1,0:T(8,128)S(1)} custom-call(f32[128,128]{1,0:T(8,128)S(1)} %cholesky.118), custom_call_target="Cholesky" | custom-call | tf_op jit(solution)/shard_map/jit(cholesky)/cholesky | solution.py:78
  124.3 9.8 %custom-call.15 = f32[1,128,128]{1,2,0:T(8,128)S(1)} custom-call(f32[1,128,128]{2,1,0:T(8,128)S(1)} %get-tuple-element.23), custom_call_target="InvertDiagBlocksLowerTriangular" | custom-call | tf_op jit(solution)/shard_map/jit(cholesky)/cholesky | solution.py:78
  134.6 11.7 %cholesky.105 = f32[128,128]{1,0:T(8,128)S(1)} custom-call(f32[128,128]{1,0:T(8,128)S(1)} %convolution_subtract_fusion.1), custom_call_target="Cholesky" | custom-call | tf_op jit(solution)/shard_map/jit(cholesky)/cholesky | solution.py:78
  146.4 0.7 compare_reduce_fusion
  148.5 4.1 %while.1 = (s32[]{:T(128)}, f32[256,256]{1,0:T(8,128)S(1)}, s32[2,2]{1,0:T(2,128)S(1)}, f32[2,128,128]{2,1,0:T(8,128)S(1)}, s32[]{:T(128)}) while((s32[]{:T(128)}, f32[256,256]{1,0:T(8,128)S(1)}, s32[2,2]{1,0:T(2,128)S(1)}, f32[2,128,128]{2,1,0:T(8,128)S(1)}, s32[]{:T(128)}) %tuple.27), condition=%wide.while_cond, body=%wide.while_body.sunk | while | flops 2 | bytes 131189 | solution.py:79
  149.1 1.4 bitcast_dynamic-update-slice_fusion.2
  151.2 1.4 bitcast_dynamic-update-slice_fusion.2
  152.6 19.9 %custom-call.16 = f32[2,128,128]{1,2,0:T(8,128)S(1)} custom-call(f32[2,128,128]{2,1,0:T(8,128)S(1)} %get-tuple-element.9), custom_call_target="InvertDiagBlocksLowerTriangular" | custom-call | tf_op jit(solution)/shard_map/jit(_solve_triangular)/triangular_solve | solution.py:79
  175.6 2.0 fusion.8
  177.6 2.5 %convolution_bitcast_fusion = f32[256,4,256]{2,1,0:T(4,128)S(1)} fusion(f32[256,4,256]{2,0,1:T(8,128)S(1)} %fusion.8, f32[1,4,4]{2,1,0:T(4,128)S(1)} %copy-done.3), kind=kOutput, calls=%fused_computation.2 | convolution fusion | flops 12582912 | bytes 2097216 | tf_op jit(solution)/shard_map/kpq,kmqd->kmpd/dot_general | solution.py:85
  180.1 1.8 fusion
  181.9 3.8 %all-to-all-start.5 = ((f32[16,1,16,256]{3,2,1,0:T(8,128)}), f32[16,1,16,256]{3,2,1,0:T(8,128)S(1)}, u32[]{:S(2)}, u32[]{:S(2)}) async-start(f32[16,1,16,256]{3,2,1,0:T(8,128)} %bitcast.30), calls=%async_computation.5 | async-start | bytes 524288 | tf_op jit(solution)/shard_map/all_to_all | solution.py:36
  187.0 8.9 %all-to-all-done.5 = f32[16,1,16,256]{3,2,1,0:T(8,128)S(1)} async-done(((f32[16,1,16,256]{3,2,1,0:T(8,128)}), f32[16,1,16,256]{3,2,1,0:T(8,128)S(1)}, u32[]{:S(2)}, u32[]{:S(2)}) %all-to-all-start.5) | async-done | bytes 262176 | tf_op jit(solution)/shard_map/all_to_all | solution.py:36
  195.9 0.9 multiply_bitcast_fusion
  196.8 7.0 %all-to-all-start.6 = ((f32[16,1,2,16,256]{4,3,2,1,0:T(8,128)}), f32[16,1,2,16,256]{4,3,2,1,0:T(8,128)S(1)}, u32[]{:S(2)}, u32[]{:S(2)}) async-start(f32[16,1,2,16,256]{4,3,2,1,0:T(8,128)} %multiply_bitcast_fusion), calls=%async_computation.6 | async-start | bytes 1048576 | tf_op jit(solution)/shard_map/all_to_all | solution.py:36
  204.8 8.7 %all-to-all-done.6 = f32[16,1,2,16,256]{4,3,2,1,0:T(8,128)S(1)} async-done(((f32[16,1,2,16,256]{4,3,2,1,0:T(8,128)}), f32[16,1,2,16,256]{4,3,2,1,0:T(8,128)S(1)}, u32[]{:S(2)}, u32[]{:S(2)}) %all-to-all-start.6) | async-done | bytes 524320 | tf_op jit(solution)/shard_map/all_to_all | solution.py:36
  213.5 0.6 reduce_sum.41
  (51 shorter events, 8.8 us)
Async XLA Ops:
  0.6 25.6 %copy-start = (f32[1,256,256]{2,1,0:T(8,128)S(1)}, f32[1,256,256]{2,1,0:T(8,128)}, u32[]{:S(2)}) copy-start(f32[1,256,256]{2,1,0:T(8,128)} %param.10) | copy-start | bytes 786436
  2.6 8.6 %copy-start.2 = (f32[1,1,256,256]{3,2,1,0:T(8,128)S(1)}, f32[1,1,256,256]{3,2,1,0:T(8,128)}, u32[]{:S(2)}) copy-start(f32[1,1,256,256]{3,2,1,0:T(8,128)} %param.9) | copy-start | bytes 786436
  2.6 23.0 %all-to-all-start = ((f32[16,1,16,1024]{3,2,1,0:T(8,128)}), f32[16,1,16,1024]{3,2,1,0:T(8,128)S(1)}, u32[]{:S(2)}, u32[]{:S(2)}) async-start(f32[16,1,16,1024]{3,2,1,0:T(8,128)} %broadcast_in_dim.8), calls=%async_computation | async-start | bytes 2097152 | tf_op jit(solution)/shard_map/all_to_all | solution.py:14
  11.3 19.0 %copy-start.1 = (f32[1,1,256,256]{3,2,1,0:T(8,128)}, f32[1,1,256,256]{3,2,1,0:T(8,128)S(1)}, u32[]{:S(2)}) copy-start(f32[1,1,256,256]{3,2,1,0:T(8,128)S(1)} %broadcast_multiply_fusion.3) | copy-start | bytes 786436
  26.2 1.0 copy-start.3
  51.3 20.5 %all-to-all-start.2 = ((f32[16,16,1024]{2,1,0:T(8,128)}), f32[16,16,1024]{2,1,0:T(8,128)S(1)}, u32[]{:S(2)}, u32[]{:S(2)}) async-start(f32[16,16,1024]{2,1,0:T(8,128)} %broadcast_in_dim.16), calls=%async_computation.2 | async-start | bytes 2097152 | tf_op jit(solution)/shard_map/all_to_all | solution.py:14
  94.6 17.7 %all-to-all-start.4 = ((f32[16,16,256]{2,1,0:T(8,128)}), f32[16,16,256]{2,1,0:T(8,128)S(1)}, u32[]{:S(2)}, u32[]{:S(2)}) async-start(f32[16,16,256]{2,1,0:T(8,128)} %broadcast_in_dim.17), calls=%async_computation.4 | async-start | bytes 524288 | tf_op jit(solution)/shard_map/all_to_all | solution.py:14
  181.9 14.0 %all-to-all-start.5 = ((f32[16,1,16,256]{3,2,1,0:T(8,128)}), f32[16,1,16,256]{3,2,1,0:T(8,128)S(1)}, u32[]{:S(2)}, u32[]{:S(2)}) async-start(f32[16,1,16,256]{3,2,1,0:T(8,128)} %bitcast.30), calls=%async_computation.5 | async-start | bytes 524288 | tf_op jit(solution)/shard_map/all_to_all | solution.py:36
  196.8 16.6 %all-to-all-start.6 = ((f32[16,1,2,16,256]{4,3,2,1,0:T(8,128)}), f32[16,1,2,16,256]{4,3,2,1,0:T(8,128)S(1)}, u32[]{:S(2)}, u32[]{:S(2)}) async-start(f32[16,1,2,16,256]{4,3,2,1,0:T(8,128)} %multiply_bitcast_fusion), calls=%async_computation.6 | async-start | bytes 1048576 | tf_op jit(solution)/shard_map/all_to_all | solution.py:36
where the time goes:
time: 215 us; the launch traced here: 214 us
  waiting for transfers between devices  58.6 us (27%)
  other arithmetic  56.9 us (26%)
  blocking collectives  38.7 us (18%)
  starting transfers between devices  29.1 us (14%)
  matrix products  14.2 us (7%)
  local copies, waits for them, and re-layouts  11.6 us (5%)
  between operations  4.95 us (2%)
    all_to_all x3, waiting for transfers between devices, copy_for_each(): return lax.all_to_all(copies, axis, split_axis=0, concat_axis=0, tiled=True)  41 us
    all_to_all x2, blocking collectives, sum_at_owner(): lax.all_to_all(blocks, axis, split_axis=0, concat_axis=0, tiled=True)  38.7 us
    another operation x6, other arithmetic, body(): factor = jnp.linalg.cholesky(gram)  34 us
    another operation x3, other arithmetic, body(): ortho_full = jax.scipy.linalg.solve_triangular(factor, flat.T, lower=True).T  19.9 us
    all_to_all x3, starting transfers between devices, copy_for_each(): return lax.all_to_all(copies, axis, split_axis=0, concat_axis=0, tiled=True)  18.3 us
    all_to_all x2, waiting for transfers between devices, sum_at_owner(): lax.all_to_all(blocks, axis, split_axis=0, concat_axis=0, tiled=True)  17.6 us
    all_to_all x2, starting transfers between devices, sum_at_owner(): lax.all_to_all(blocks, axis, split_axis=0, concat_axis=0, tiled=True)  10.8 us
    another operation x7, local copies, waits for them, and re-layouts  4.6 us
  transfers between devices with their start and end apart: 5, of which 5 were waited for; matrix products, arithmetic and copies ran while one was open for 1% of the time, Pallas kernels for 0%

commit v1 on v0

v1 whole, which is shorter than its diff:
```python
import functools

import jax
import jax.numpy as jnp
from jax import lax
from jax.experimental import pallas as pl
from jax.experimental.pallas import tpu as pltpu
from jax.sharding import PartitionSpec as P

SLOTS = 2
F32, BF16 = jnp.float32, jnp.bfloat16
HIGHEST = lax.Precision.HIGHEST
VM = pl.BlockSpec(memory_space=pltpu.VMEM)
SM = pl.BlockSpec(memory_space=pltpu.SMEM)

CORE = [(i, i ^ 1) for i in range(16)]
ZPAIR = [(i, i ^ 8) for i in range(16)]
XSHIFT = [[(i, (i & 9) | ((((i >> 1) + d) & 3) << 1)) for i in range(16)] for d in range(4)]


def other_z():
    pairs = []
    for i in range(16):
        step = 1 if i >> 3 else -1
        for s in range(16):
            t = ((((s >> 2) + step) & 3) << 2) | (s & 3)
            pairs.append((i * 16 + s, (i ^ 8) * 16 + t))
    return pairs


OTHER_Z = other_z()


def place():
    ops = lax.axis_index("ops")
    return ops, ops >> 3, (ops >> 1) & 3, ops & 1


def split(x):
    high = x.astype(BF16)
    return high, (x - high.astype(F32)).astype(BF16)


def dot3(a, b, dims=(((1,), (0,)), ((), ()))):
    def one(u, v):
        return lax.dot_general(u, v, dims, preferred_element_type=F32)

    return one(a[0], b[0]) + (one(a[0], b[1]) + one(a[1], b[0]))


NT = (((1,), (1,)), ((), ()))


def call(kernel, out, scratch, *args, specs=None, name=None):
    return pl.pallas_call(
        kernel,
        out_shape=out,
        in_specs=[VM] * len(args) if specs is None else specs,
        out_specs=jax.tree.map(lambda _: VM, out),
        scratch_shapes=scratch,
        compiler_params=pltpu.CompilerParams(vmem_limit_bytes=24 * 2**20),
        name=name,
    )(*args)


def gather(shard):
    pair = jnp.concatenate([shard, lax.ppermute(shard, "ops", ZPAIR)])
    mine = jnp.concatenate([pair, *[lax.ppermute(pair, "ops", XSHIFT[d]) for d in (1, 2, 3)]])
    return mine, lax.ppermute(mine, "ops", CORE)


def blocks(own, other, rows):
    _, z, x, c = place()
    for cc, ref in enumerate((own, other)):
        for d in range(4):
            for zz in range(2):
                index = ((z ^ zz) << 3) | (((x - d) & 3) << 1) | (c ^ cc)
                yield ref, (d * 2 + zz) * rows, index


def sigma_kernel(size, f, g, b0, b1, b2, b3, r0, r1, r2, r3, o0, o1, o2, o3, ph, pw, vh, vw, acc):
    _, z, x, c = place()
    live = size[0]
    row16 = lax.broadcasted_iota(jnp.int32, (16, 1024), 0)
    for ref, at, index in blocks(f, g, 16):
        first = pl.multiple_of(index * 16, 16)
        value = jnp.where(row16 + first < live, ref[at : at + 16, :], 0.0)
        high, low = split(value)
        ph[pl.ds(first, 16), :] = high
        pw[pl.ds(first, 16), :] = low
    pieces = [b[pl.ds(xx * 32 + pl.multiple_of(c * 16, 16), 16), :] for b in (b0, b1, b2, b3) for xx in range(4)]
    left = split(jnp.concatenate(pieces))
    u = dot3(left, (ph[...], pw[...]))
    for k, b in enumerate((b0, b1, b2, b3)):
        for p in range(4):
            total = None
            for q in range(4):
                term = b[128 + p : 129 + p, q : q + 1] * u[k * 64 : k * 64 + 64, q * 256 : q * 256 + 256]
                total = term if total is None else total + term
            high, low = split(total)
            vh[p * 64 : p * 64 + 64, k * 256 : k * 256 + 256] = high
            vw[p * 64 : p * 64 + 64, k * 256 : k * 256 + 256] = low
    right = split(jnp.concatenate([r[...] for r in (r0, r1, r2, r3)]))
    out = dot3((vh[...], vw[...]), right)
    at = lax.broadcasted_iota(jnp.int32, (256, 256), 0)
    m = z * 128 + ((at >> 4) & 3) * 32 + c * 16 + (at & 15)
    acc[...] = jnp.where(m < live, out, 0.0)
    for d, o in enumerate((o0, o1, o2, o3)):
        first = pl.multiple_of(((x + d) & 3) * 16, 16)
        for p in range(4):
            o[:, p * 256 : p * 256 + 256] = acc[pl.ds(p * 64 + first, 16), :]


def pair_kernel(f, g, left, site, out, xs, xh, xw, xt):
    ops, _, _, _ = place()
    for ref, at, index in blocks(f, g, 16):
        first = pl.multiple_of(index * 16, 16)
        value = ref[at : at + 16, :]
        xs[pl.ds(first, 16), :] = value
        high, low = split(value)
        xh[pl.ds(first, 16), :] = high
        xw[pl.ds(first, 16), :] = low
    y = dot3(split(left[...]), (xh[...], xw[...]))
    total, gram = jnp.zeros((256, 256), F32), jnp.zeros((16, 256), F32)
    first = pl.multiple_of(ops * 16, 16)
    for p in range(4):
        mixed = None
        for q in range(4):
            term = site[p, q] * y[:, q * 256 : q * 256 + 256]
            mixed = term if mixed is None else mixed + term
        x = xs[:, p * 256 : p * 256 + 256]
        xt[...] = x.T
        total = total + dot3(split(xt[...]), split(mixed))
        gram = gram + jnp.dot(xt[pl.ds(first, 16), :], x, precision=HIGHEST, preferred_element_type=F32)
    for s in range(16):
        out[s, :16, :] = total[s * 16 : s * 16 + 16, :]
        out[s, 16:, :] = gram


def route_kernel(f, g, gram, copies):
    ops, _, _, _ = place()
    slots = [jnp.zeros((16, 256), F32) for _ in range(SLOTS)]
    for ref, at, index in blocks(f, g, 40):
        gram[pl.ds(pl.multiple_of(index * 16, 16), 16), :] = ref[at + 16 : at + 32, :]
        target = ref[at + 32 : at + 33, :]
        for j in range(SLOTS):
            chosen = jnp.where(target == (ops * SLOTS + j).astype(F32), 1.0, 0.0)
            slots[j] = slots[j] + chosen * ref[at : at + 16, :]
    for s in range(16):
        for j in range(SLOTS):
            copies[s, j * 16 : j * 16 + 16, :] = slots[j]


def factor(block, size):
    count = size // 8
    lanes = lax.broadcasted_iota(jnp.int32, (8, 128), 1)
    sub = lax.broadcasted_iota(jnp.int32, (8, 128), 0)

    def spread(v):
        return jnp.broadcast_to(v, (8, 128))

    w = []
    for b in range(count):
        unit = jnp.where(lanes == sub + (size + b * 8), 1.0, 0.0)
        w.append(jnp.where(lanes < size, block[b * 8 : b * 8 + 8, :], unit))
    for b in range(count):
        t = b * 8
        col = [[spread(w[v][:, t + j : t + j + 1]) for j in range(8)] for v in range(b, count)]
        e = [[spread(col[0][j][i : i + 1, :]) if i >= j else None for j in range(8)] for i in range(8)]
        row = [spread(w[b][j : j + 1, :]) for j in range(8)]
        out = jnp.zeros((8, 128), F32)
        for j in range(8):
            inv = lax.rsqrt(e[j][j])
            row[j] = row[j] * inv
            out = jnp.where(sub == j, row[j], out)
            l = [e[i][j] * inv if i > j else None for i in range(8)]
            for i in range(j + 1, 8):
                for k in range(j + 1, i + 1):
                    e[i][k] = e[i][k] - l[i] * l[k]
            for i in range(j + 1, 8):
                row[i] = row[i] - l[i] * row[j]
            for v in range(1, count - b):
                col[v][j] = col[v][j] * inv
                for k in range(j + 1, 8):
                    col[v][k] = col[v][k] - l[k] * col[v][j]
        w[b] = out
        for v in range(1, count - b):
            rest = w[b + v]
            for j in range(8):
                rest = rest - col[v][j] * row[j]
            w[b + v] = rest
    return jnp.concatenate(w, 0)


def factor_kernel(a, x, scale, inverse, basis, u, v, size=64):
    v[...] = jnp.zeros_like(v)

    def dot(p, q):
        return jnp.dot(p, q, precision=HIGHEST, preferred_element_type=F32)

    for s in range(0, 256, size):
        low, high = s // 128 * 128, (s + size + 127) // 128 * 128
        pu = a[s : s + size, low:]
        at = [lax.broadcasted_iota(jnp.int32, (size, high), i) for i in (0, 1)]
        pv = jnp.where(at[1] == at[0] + s, 1.0, 0.0)
        if s:
            t = u[:s, low : low + 128].T[s - low : s - low + size, :]
            pu = pu - dot(t, u[:s, low:])
            pv = pv - dot(t, v[:s, :high])
        d = pu[:, :128]
        if s > low:
            d = pltpu.roll(d, 128 - (s - low), 1)
        m = pltpu.roll(factor(d, size), 128 - size, 1)[:, :size]
        u[s : s + size, low:] = dot(m, pu)
        v[s : s + size, :high] = dot(m, pv)
    inverse[...] = v[...]
    rows = jnp.concatenate([x[:, p * 256 : p * 256 + 256] for p in range(4)])
    q = dot3(split(rows), split(v[...]), NT) * scale
    for p in range(4):
        basis[:, p * 256 : p * 256 + 256] = q[p * 16 : p * 16 + 16, :]


def turn_kernel(arrived, inverse, out):
    sec = lax.axis_index("sec")
    rows = split(inverse[pl.ds(pl.multiple_of(sec * 16, 16), 16), :])
    turned = []
    for j in range(SLOTS):
        whole = jnp.concatenate([arrived[s, j * 16 : j * 16 + 16, :] for s in range(16)])
        turned.append(dot3(rows, split(whole)))
    result = dot3(split(jnp.concatenate(turned)), split(inverse[...]), NT)
    for j in range(SLOTS):
        out[j] = result[j * 16 : j * 16 + 16, :]


def body(wavefunction, left_ops, right_ops, site_ops, pattern, sector_sizes, owner, slot):
    def shape(*dims, dtype=F32):
        return jax.ShapeDtypeStruct(dims, dtype)

    def scratch(*dims, dtype=F32):
        return pltpu.VMEM(dims, dtype)

    def a2a(x, axis):
        return lax.all_to_all(x, axis, split_axis=0, concat_axis=0, tiled=True)

    z = lax.axis_index("ops") >> 3
    left, right = left_ops[0, 0], right_ops[0]
    site = site_ops[0] * pattern[0, 0].astype(F32)
    padded = jnp.pad(site, ((0, 4), (0, 252)))
    halves = left.reshape(2, 128, 256)
    kept = jnp.concatenate([lax.dynamic_index_in_dim(halves, z, 0, False), padded])
    given = jnp.concatenate([lax.dynamic_index_in_dim(halves, 1 - z, 0, False), padded])
    given = lax.ppermute(given, "ops", ZPAIR)
    right_z = lax.ppermute(right, ("ops", "sec"), OTHER_Z)
    mine, theirs = gather(wavefunction[0])
    lefts = [kept, given, lax.ppermute(kept, "ops", CORE), lax.ppermute(given, "ops", CORE)]
    rights = [right, right_z, lax.ppermute(right, "ops", CORE), lax.ppermute(right_z, "ops", CORE)]
    parts = call(
        sigma_kernel,
        [shape(16, 1024)] * 4,
        [scratch(256, 1024, dtype=BF16)] * 4 + [scratch(256, 256)],
        sector_sizes,
        mine,
        theirs,
        *lefts,
        *rights,
        specs=[SM] + [VM] * 10,
        name="sigma",
    )
    own = parts[0]
    for d in (1, 2, 3):
        own = own + lax.ppermute(parts[d], "ops", XSHIFT[d])
    mine, theirs = gather(own)
    pairs = call(
        pair_kernel,
        shape(16, 32, 256),
        [scratch(256, 1024)] + [scratch(256, 1024, dtype=BF16)] * 2 + [scratch(256, 256)],
        mine,
        theirs,
        left,
        site,
        specs=[VM, VM, VM, SM],
        name="pairs",
    )
    arrived = a2a(pairs, "sec").sum(axis=0)
    target = (owner[0] * SLOTS + slot[0]).astype(F32)
    mine, theirs = gather(jnp.concatenate([arrived, jnp.broadcast_to(target, (8, 256))]))
    gram, copies = call(route_kernel, [shape(256, 256), shape(16, 32, 256)], [], mine, theirs, name="route")
    routed = a2a(copies, "sec")
    total_rows = 4 * 256 * lax.axis_size("sec")
    inverse, basis = call(
        functools.partial(factor_outer, scale=float(total_rows) ** 0.5),
        [shape(256, 256), shape(16, 1024)],
        [scratch(256, 256), scratch(256, 256)],
        gram,
        own,
        name="factor",
    )
    out = call(turn_kernel, shape(2, 16, 256), [], routed, inverse, name="turn")
    return basis[None], out[None]


def factor_outer(a, x, inverse, basis, u, v, scale):
    factor_kernel(a, x, scale, inverse, basis, u, v)


def solution(mesh):
    placed = (
        P("sec", "ops", None),
        P("ops", "sec", None, None),
        P("ops", None, None),
        P("ops", None, None),
        P("ops", "sec"),
        P("sec"),
        P("ops"),
        P("ops"),
    )
    return jax.shard_map(
        body,
        mesh=mesh,
        in_specs=placed,
        out_specs=(P("sec", "ops", None), P("ops", None, "sec", None)),
        check_vma=False,
    )
```

time: 215 us -> 121 us (0.56)
  other arithmetic: 56.9 us -> 0.95 us
  blocking collectives: 38.7 us -> 0 us
  starting transfers between devices: 29.1 us -> 52.6 us
  Pallas kernels: 0 us -> 17.7 us
  matrix products: 14.2 us -> 0 us
  waiting for transfers between devices: 58.6 us -> 44.6 us
  local copies, waits for them, and re-layouts: 11.6 us -> 0.96 us
    another operation x10 -> x0, other arithmetic: 54 us -> none  [the longest x6 34 us: body(): factor = jnp.linalg.cholesky(gram)]
    ppermute x0 -> x24, starting transfers between devices: none -> 40.1 us  [the longest x9 11.8 us: gather(): lax.ppermute(pair, 'ops', XSHIFT[d])]
    all_to_all x2 -> x0, blocking collectives: 38.7 us -> none  [sum_at_owner(): lax.all_to_all(blocks, axis, split_axis=0, concat_axis=0, tiled=True)]
    all_to_all x5 -> x2, waiting for transfers between devices: 58.6 us -> 20.2 us  [a2a(): return lax.all_to_all(x, axis, split_axis=0, concat_axis=0, tiled=True)]
    ppermute x0 -> x24, waiting for transfers between devices: none -> 24.4 us  [the longest x9 11.5 us: gather(): lax.ppermute(pair, 'ops', XSHIFT[d])]
    pallas_call x0 -> x5, Pallas kernels: none -> 17.7 us  [call(): pl.pallas_call(kernel, out_shape=out, in_specs=[VM] * len(args) if specs...]
    all_to_all x5 -> x2, starting transfers between devices: 29.1 us -> 12.5 us  [a2a(): return lax.all_to_all(x, axis, split_axis=0, concat_axis=0, tiled=True)]
    dot_general x7 -> x0, matrix products: 11.8 us -> none  [the longest x1 2.49 us: body(): moved = jnp.einsum('kpq,kmqd->kmpd', site_ops, moved, precision=highest)]
  transfers between devices with their start and end apart: 5 -> 26, of which waited for: 5 -> 18; matrix products, arithmetic and copies ran while one was open for 1% -> 1% of each run, Pallas kernels for 0% -> 9%
where the time goes in v1:
time: 121 us; the launch traced here: 120 us
  starting transfers between devices  52.6 us (43%)
  waiting for transfers between devices  44.6 us (37%)
  Pallas kernels  17.7 us (15%)
  between operations  3.4 us (3%)
    all_to_all x2, waiting for transfers between devices, a2a(): return lax.all_to_all(x, axis, split_axis=0, concat_axis=0, tiled=True)  20.2 us
    pallas_call x5, Pallas kernels, call(): pl.pallas_call(kernel, out_shape=out, in_specs=[VM] * len(args) if specs...  17.7 us
    all_to_all x2, starting transfers between devices, a2a(): return lax.all_to_all(x, axis, split_axis=0, concat_axis=0, tiled=True)  12.5 us
    ppermute x9, starting transfers between devices, gather(): lax.ppermute(pair, 'ops', XSHIFT[d])  11.8 us
    ppermute x9, waiting for transfers between devices, gather(): lax.ppermute(pair, 'ops', XSHIFT[d])  11.5 us
    ppermute x3, starting transfers between devices, gather(): return (mine, lax.ppermute(mine, 'ops', CORE))  11.2 us
    ppermute x3, starting transfers between devices, gather(): pair = jnp.concatenate([shard, lax.ppermute(shard, 'ops', ZPAIR)])  5.42 us
    ppermute x1, starting transfers between devices, body(): right_z = lax.ppermute(right, ('ops', 'sec'), OTHER_Z)  4.67 us
  transfers between devices with their start and end apart: 26, of which 18 were waited for; matrix products, arithmetic and copies ran while one was open for 1% of the time, Pallas kernels for 9%

profile of v1, /device:TPU:1, one launch (start us, length us, event | category | flops | bytes accessed | tf_op | source)
XLA Modules:
  0.0 120.2 jit_solution(9596528534255415878)
XLA Ops:
  0.6 2.5 %collective-permute-start = (f32[16,1024]{1,0:T(8,128)}, f32[16,1024]{1,0:T(8,128)S(1)}, u32[]{:S(2)}, u32[]{:S(2)}) collective-permute-start(f32[16,1024]{1,0:T(8,128)} %bitcast.20), channel_id=1, source_target_pairs={{0,128},{16,144},{32,160},{48,176},{64,192},{80,208},{96,224},{112... | collective-permute-start | bytes 196616 | tf_op jit(solution)/shard_map/ppermute | solution.py:67
  3.2 4.7 %collective-permute-start.8 = (f32[256,256]{1,0:T(8,128)}, f32[256,256]{1,0:T(8,128)S(1)}, u32[]{:S(2)}, u32[]{:S(2)}) collective-permute-start(f32[256,256]{1,0:T(8,128)} %bitcast.17), channel_id=1, source_target_pairs={{0,140},{1,141},{2,142},{3,143},{4,128},{5,129},{6,130},{7,131},{8... | collective-permute-start | bytes 786440 | tf_op jit(solution)/shard_map/ppermute | solution.py:253
  8.7 1.3 %collective-permute-start.1 = (f32[32,1024]{1,0:T(8,128)S(1)}, f32[32,1024]{1,0:T(8,128)S(1)}, u32[]{:S(2)}, u32[]{:S(2)}) collective-permute-start(f32[32,1024]{1,0:T(8,128)S(1)} %pad_maximum_fusion), channel_id=1, source_target_pairs={{0,32},{16,48},{32,64},{48,80},{64,96},{80,112},{96,0},{112,16},{1... | collective-permute-start | bytes 393224 | tf_op jit(solution)/shard_map/ppermute | solution.py:68
  10.6 2.5 %collective-permute-start.2 = (f32[32,1024]{1,0:T(8,128)S(1)}, f32[32,1024]{1,0:T(8,128)S(1)}, u32[]{:S(2)}, u32[]{:S(2)}) collective-permute-start(f32[32,1024]{1,0:T(8,128)S(1)} %pad_maximum_fusion), channel_id=1, source_target_pairs={{0,64},{16,80},{32,96},{48,112},{64,0},{80,16},{96,32},{112,48},{1... | collective-permute-start | bytes 393224 | tf_op jit(solution)/shard_map/ppermute | solution.py:68
  13.2 1.2 collective-permute-start.3
  14.4 2.9 %collective-permute-done.2 = f32[32,1024]{1,0:T(8,128)S(1)} collective-permute-done((f32[32,1024]{1,0:T(8,128)S(1)}, f32[32,1024]{1,0:T(8,128)S(1)}, u32[]{:S(2)}, u32[]{:S(2)}) %collective-permute-start.2) | collective-permute-done | bytes 131104 | tf_op jit(solution)/shard_map/ppermute | solution.py:68
  17.3 1.3 %collective-permute-done.3 = f32[32,1024]{1,0:T(8,128)S(1)} collective-permute-done((f32[32,1024]{1,0:T(8,128)S(1)}, f32[32,1024]{1,0:T(8,128)S(1)}, u32[]{:S(2)}, u32[]{:S(2)}) %collective-permute-start.3) | collective-permute-done | bytes 131104 | tf_op jit(solution)/shard_map/ppermute | solution.py:68
  18.6 2.0 %collective-permute-start.4 = (f32[128,1024]{1,0:T(8,128)S(1)}, f32[128,1024]{1,0:T(8,128)S(1)}, u32[]{:S(2)}, u32[]{:S(2)}) collective-permute-start(f32[128,1024]{1,0:T(8,128)S(1)} %constant_dynamic-update-slice_fusion.f), channel_id=1, source_target_pairs={{0,16},{16,0},{32,48},{48,32},{64,80},{80,64},{96,112},{112,96},{1... | collective-permute-start | bytes 1572872 | tf_op jit(solution)/shard_map/ppermute | solution.py:69
  22.7 2.7 %collective-permute-done.5.b1 = f32[136,256]{1,0:T(8,128)S(1)} collective-permute-done((f32[136,256]{1,0:T(8,128)S(1)}, f32[136,256]{1,0:T(8,128)S(1)}, u32[]{:S(2)}, u32[]{:S(2)}) %collective-permute-start.5) | collective-permute-done | bytes 139296 | tf_op jit(solution)/shard_map/ppermute | solution.py:252
  25.4 1.4 %collective-permute-start.7 = (f32[136,256]{1,0:T(8,128)S(1)}, f32[136,256]{1,0:T(8,128)S(1)}, u32[]{:S(2)}, u32[]{:S(2)}) collective-permute-start(f32[136,256]{1,0:T(8,128)S(1)} %collective-permute-done.5.b1), channel_id=1, source_target_pairs={{0,16},{16,0},{32,48},{48,32},{64,80},{80,64},{96,112},{112,96},{1... | collective-permute-start | bytes 417800 | tf_op jit(solution)/shard_map/ppermute | solution.py:255
  27.9 2.2 %sigma.1 = (f32[16,1024]{1,0:T(8,128)S(1)}, f32[16,1024]{1,0:T(8,128)S(1)}, f32[16,1024]{1,0:T(8,128)S(1)}, f32[16,1024]{1,0:T(8,128)S(1)}) custom-call(s32[1]{0:T(128)S(6)} %copy.24.size, f32[128,1024]{1,0:T(8,128)S(1)} %constant_dynamic-update-slice_fusion.f, f32[128,1024]{1,0:T(8,128)S(1)} %collective-permute-done.4.g, ...), custom_call_target="tpu_custom_call" | custom-call | tf_op jit(solution)/shard_map/sigma/pallas_call | solution.py:55
  31.1 2.6 %collective-permute-start.12 = (f32[16,1024]{1,0:T(8,128)S(1)}, f32[16,1024]{1,0:T(8,128)S(1)}, u32[]{:S(2)}, u32[]{:S(2)}) collective-permute-start(f32[16,1024]{1,0:T(8,128)S(1)} %get-tuple-element.12), channel_id=1, source_target_pairs={{0,64},{16,80},{32,96},{48,112},{64,0},{80,16},{96,32},{112,48},{1... | collective-permute-start | bytes 196616 | tf_op jit(solution)/shard_map/ppermute | solution.py:271
  34.5 2.1 %collective-permute-done.12 = f32[16,1024]{1,0:T(8,128)S(1)} collective-permute-done((f32[16,1024]{1,0:T(8,128)S(1)}, f32[16,1024]{1,0:T(8,128)S(1)}, u32[]{:S(2)}, u32[]{:S(2)}) %collective-permute-start.12) | collective-permute-done | bytes 65568 | tf_op jit(solution)/shard_map/ppermute | solution.py:271
  37.3 3.1 %collective-permute-done.14 = f32[16,1024]{1,0:T(8,128)S(1)} collective-permute-done((f32[16,1024]{1,0:T(8,128)S(1)}, f32[16,1024]{1,0:T(8,128)S(1)}, u32[]{:S(2)}, u32[]{:S(2)}) %collective-permute-start.14) | collective-permute-done | bytes 65568 | tf_op jit(solution)/shard_map/ppermute | solution.py:67
  40.9 2.8 %collective-permute-start.16 = (f32[32,1024]{1,0:T(8,128)S(1)}, f32[32,1024]{1,0:T(8,128)S(1)}, u32[]{:S(2)}, u32[]{:S(2)}) collective-permute-start(f32[32,1024]{1,0:T(8,128)S(1)} %pad_maximum_fusion.1), channel_id=1, source_target_pairs={{0,64},{16,80},{32,96},{48,112},{64,0},{80,16},{96,32},{112,48},{1... | collective-permute-start | bytes 393224 | tf_op jit(solution)/shard_map/ppermute | solution.py:68
  43.8 1.7 %collective-permute-done.15 = f32[32,1024]{1,0:T(8,128)S(1)} collective-permute-done((f32[32,1024]{1,0:T(8,128)S(1)}, f32[32,1024]{1,0:T(8,128)S(1)}, u32[]{:S(2)}, u32[]{:S(2)}) %collective-permute-start.15) | collective-permute-done | bytes 131104 | tf_op jit(solution)/shard_map/ppermute | solution.py:68
  45.5 2.0 %collective-permute-done.16 = f32[32,1024]{1,0:T(8,128)S(1)} collective-permute-done((f32[32,1024]{1,0:T(8,128)S(1)}, f32[32,1024]{1,0:T(8,128)S(1)}, u32[]{:S(2)}, u32[]{:S(2)}) %collective-permute-start.16) | collective-permute-done | bytes 131104 | tf_op jit(solution)/shard_map/ppermute | solution.py:68
  47.9 4.3 %collective-permute-start.18 = (f32[128,1024]{1,0:T(8,128)S(1)}, f32[128,1024]{1,0:T(8,128)S(1)}, u32[]{:S(2)}, u32[]{:S(2)}) collective-permute-start(f32[128,1024]{1,0:T(8,128)S(1)} %constant_dynamic-update-slice_fusion.5.f), channel_id=1, source_target_pairs={{0,16},{16,0},{32,48},{48,32},{64,80},{80,64},{96,112},{112,96},{1... | collective-permute-start | bytes 1572872 | tf_op jit(solution)/shard_map/ppermute | solution.py:69
  52.2 1.5 %collective-permute-done.18.g = f32[128,1024]{1,0:T(8,128)S(1)} collective-permute-done((f32[128,1024]{1,0:T(8,128)S(1)}, f32[128,1024]{1,0:T(8,128)S(1)}, u32[]{:S(2)}, u32[]{:S(2)}) %collective-permute-start.18) | collective-permute-done | bytes 524320 | tf_op jit(solution)/shard_map/ppermute | solution.py:69
  53.7 3.3 %pairs.1 = f32[16,32,256]{2,1,0:T(8,128)} custom-call(f32[128,1024]{1,0:T(8,128)S(1)} %constant_dynamic-update-slice_fusion.5.f, f32[128,1024]{1,0:T(8,128)S(1)} %collective-permute-done.18.g, f32[256,256]{1,0:T(8,128)S(1)} %bitcast.16, f32[4,4]{1,0:T(4,128)S(1)} %multiply_bitcast_fusion.site), custom_call_target="tpu_custom_call" | custom-call | tf_op jit(solution)/shard_map/pairs/pallas_call | solution.py:55
  57.1 8.0 %all-to-all-start = ((f32[16,32,256]{2,1,0:T(8,128)}), f32[16,32,256]{2,1,0:T(8,128)S(1)}, u32[]{:S(2)}, u32[]{:S(2)}) async-start(f32[16,32,256]{2,1,0:T(8,128)} %pairs.1), calls=%async_computation | async-start | bytes 1048576 | tf_op jit(solution)/shard_map/all_to_all | solution.py:243
  66.4 14.0 %all-to-all-done = f32[16,32,256]{2,1,0:T(8,128)S(1)} async-done(((f32[16,32,256]{2,1,0:T(8,128)}), f32[16,32,256]{2,1,0:T(8,128)S(1)}, u32[]{:S(2)}, u32[]{:S(2)}) %all-to-all-start) | async-done | bytes 524320 | tf_op jit(solution)/shard_map/all_to_all | solution.py:243
  80.5 2.8 %collective-permute-start.19 = (f32[40,256]{1,0:T(8,128)S(1)}, f32[40,256]{1,0:T(8,128)S(1)}, u32[]{:S(2)}, u32[]{:S(2)}) collective-permute-start(f32[40,256]{1,0:T(8,128)S(1)} %concatenate.37), channel_id=1, source_target_pairs={{0,128},{16,144},{32,160},{48,176},{64,192},{80,208},{96,224},{112... | collective-permute-start | bytes 122888 | tf_op jit(solution)/shard_map/ppermute | solution.py:67
  83.3 1.4 %collective-permute-done.19 = f32[40,256]{1,0:T(8,128)S(1)} collective-permute-done((f32[40,256]{1,0:T(8,128)S(1)}, f32[40,256]{1,0:T(8,128)S(1)}, u32[]{:S(2)}, u32[]{:S(2)}) %collective-permute-start.19) | collective-permute-done | bytes 40992 | tf_op jit(solution)/shard_map/ppermute | solution.py:67
  85.1 2.9 %collective-permute-start.21 = (f32[80,256]{1,0:T(8,128)S(1)}, f32[80,256]{1,0:T(8,128)S(1)}, u32[]{:S(2)}, u32[]{:S(2)}) collective-permute-start(f32[80,256]{1,0:T(8,128)S(1)} %pad_maximum_fusion.2), channel_id=1, source_target_pairs={{0,64},{16,80},{32,96},{48,112},{64,0},{80,16},{96,32},{112,48},{1... | collective-permute-start | bytes 245768 | tf_op jit(solution)/shard_map/ppermute | solution.py:68
  88.1 1.2 collective-permute-done.20
  89.3 1.5 %collective-permute-done.21 = f32[80,256]{1,0:T(8,128)S(1)} collective-permute-done((f32[80,256]{1,0:T(8,128)S(1)}, f32[80,256]{1,0:T(8,128)S(1)}, u32[]{:S(2)}, u32[]{:S(2)}) %collective-permute-start.21) | collective-permute-done | bytes 81952 | tf_op jit(solution)/shard_map/ppermute | solution.py:68
  91.3 4.9 %collective-permute-start.23 = (f32[320,256]{1,0:T(8,128)S(1)}, f32[320,256]{1,0:T(8,128)S(1)}, u32[]{:S(2)}, u32[]{:S(2)}) collective-permute-start(f32[320,256]{1,0:T(8,128)S(1)} %constant_dynamic-update-slice_fusion.10.f), channel_id=1, source_target_pairs={{0,16},{16,0},{32,48},{48,32},{64,80},{80,64},{96,112},{112,96},{1... | collective-permute-start | bytes 983048 | tf_op jit(solution)/shard_map/ppermute | solution.py:69
  96.2 1.3 %collective-permute-done.23.g = f32[320,256]{1,0:T(8,128)S(1)} collective-permute-done((f32[320,256]{1,0:T(8,128)S(1)}, f32[320,256]{1,0:T(8,128)S(1)}, u32[]{:S(2)}, u32[]{:S(2)}) %collective-permute-start.23) | collective-permute-done | bytes 327712 | tf_op jit(solution)/shard_map/ppermute | solution.py:69
  98.3 4.5 %all-to-all-start.1 = ((f32[16,32,256]{2,1,0:T(8,128)}), f32[16,32,256]{2,1,0:T(8,128)S(1)}, u32[]{:S(2)}, u32[]{:S(2)}) async-start(f32[16,32,256]{2,1,0:T(8,128)} %get-tuple-element.16), calls=%async_computation.1 | async-start | bytes 1048576 | tf_op jit(solution)/shard_map/all_to_all | solution.py:243
  102.8 10.3 %factor.1 = (f32[256,256]{1,0:T(8,128)S(1)}, f32[16,1024]{1,0:T(8,128)}) custom-call(f32[256,256]{1,0:T(8,128)S(1)} %get-tuple-element.14.a, f32[16,1024]{1,0:T(8,128)S(1)} %get-tuple-element.19.x), custom_call_target="tpu_custom_call" | custom-call | tf_op jit(solution)/shard_map/factor/pallas_call | solution.py:55
  113.1 6.1 %all-to-all-done.1.arrived = f32[16,32,256]{2,1,0:T(8,128)S(1)} async-done(((f32[16,32,256]{2,1,0:T(8,128)}), f32[16,32,256]{2,1,0:T(8,128)S(1)}, u32[]{:S(2)}, u32[]{:S(2)}) %all-to-all-start.1) | async-done | bytes 524320 | tf_op jit(solution)/shard_map/all_to_all | solution.py:243
  (58 shorter events, 9.8 us)
Async XLA Ops:
  0.6 7.2 %collective-permute-start = (f32[16,1024]{1,0:T(8,128)}, f32[16,1024]{1,0:T(8,128)S(1)}, u32[]{:S(2)}, u32[]{:S(2)}) collective-permute-start(f32[16,1024]{1,0:T(8,128)} %bitcast.20), channel_id=1, source_target_pairs={{0,128},{16,144},{32,160},{48,176},{64,192},{80,208},{96,224},{112... | collective-permute-start | bytes 196616 | tf_op jit(solution)/shard_map/ppermute | solution.py:67
  3.2 6.8 %copy-start.2 = (f32[1,16,1024]{2,1,0:T(8,128)S(1)}, f32[1,16,1024]{2,1,0:T(8,128)}, u32[]{:S(2)}) copy-start(f32[1,16,1024]{2,1,0:T(8,128)} %param.8) | copy-start | bytes 196612
  3.2 19.0 %collective-permute-start.8 = (f32[256,256]{1,0:T(8,128)}, f32[256,256]{1,0:T(8,128)S(1)}, u32[]{:S(2)}, u32[]{:S(2)}) collective-permute-start(f32[256,256]{1,0:T(8,128)} %bitcast.17), channel_id=1, source_target_pairs={{0,140},{1,141},{2,142},{3,143},{4,128},{5,129},{6,130},{7,131},{8... | collective-permute-start | bytes 786440 | tf_op jit(solution)/shard_map/ppermute | solution.py:253
  8.7 5.7 %collective-permute-start.1 = (f32[32,1024]{1,0:T(8,128)S(1)}, f32[32,1024]{1,0:T(8,128)S(1)}, u32[]{:S(2)}, u32[]{:S(2)}) collective-permute-start(f32[32,1024]{1,0:T(8,128)S(1)} %pad_maximum_fusion), channel_id=1, source_target_pairs={{0,32},{16,48},{32,64},{48,80},{64,96},{80,112},{96,0},{112,16},{1... | collective-permute-start | bytes 393224 | tf_op jit(solution)/shard_map/ppermute | solution.py:68
  10.6 6.7 %collective-permute-start.2 = (f32[32,1024]{1,0:T(8,128)S(1)}, f32[32,1024]{1,0:T(8,128)S(1)}, u32[]{:S(2)}, u32[]{:S(2)}) collective-permute-start(f32[32,1024]{1,0:T(8,128)S(1)} %pad_maximum_fusion), channel_id=1, source_target_pairs={{0,64},{16,80},{32,96},{48,112},{64,0},{80,16},{96,32},{112,48},{1... | collective-permute-start | bytes 393224 | tf_op jit(solution)/shard_map/ppermute | solution.py:68
  13.2 5.4 %collective-permute-start.3 = (f32[32,1024]{1,0:T(8,128)S(1)}, f32[32,1024]{1,0:T(8,128)S(1)}, u32[]{:S(2)}, u32[]{:S(2)}) collective-permute-start(f32[32,1024]{1,0:T(8,128)S(1)} %pad_maximum_fusion), channel_id=1, source_target_pairs={{0,96},{16,112},{32,0},{48,16},{64,32},{80,48},{96,64},{112,80},{1... | collective-permute-start | bytes 393224 | tf_op jit(solution)/shard_map/ppermute | solution.py:68
  14.4 6.2 %copy-start = (f32[1,1,256,256]{3,2,1,0:T(8,128)S(1)}, f32[1,1,256,256]{3,2,1,0:T(8,128)}, u32[]{:S(2)}) copy-start(f32[1,1,256,256]{3,2,1,0:T(8,128)} %param.9) | copy-start | bytes 786436
  18.6 2.0 %copy-start.3 = (f32[1,4,4]{2,1,0:T(4,128)S(1)}, f32[1,4,4]{2,1,0:T(4,128)}, u32[]{:S(2)}) copy-start(f32[1,4,4]{2,1,0:T(4,128)} %param.11) | copy-start | bytes 196
  18.6 9.2 %collective-permute-start.4 = (f32[128,1024]{1,0:T(8,128)S(1)}, f32[128,1024]{1,0:T(8,128)S(1)}, u32[]{:S(2)}, u32[]{:S(2)}) collective-permute-start(f32[128,1024]{1,0:T(8,128)S(1)} %constant_dynamic-update-slice_fusion.f), channel_id=1, source_target_pairs={{0,16},{16,0},{32,48},{48,32},{64,80},{80,64},{96,112},{112,96},{1... | collective-permute-start | bytes 1572872 | tf_op jit(solution)/shard_map/ppermute | solution.py:69
  20.6 1.0 copy-start.1
  20.7 4.7 %collective-permute-start.5 = (f32[136,256]{1,0:T(8,128)S(1)}, f32[136,256]{1,0:T(8,128)S(1)}, u32[]{:S(2)}, u32[]{:S(2)}) collective-permute-start(f32[136,256]{1,0:T(8,128)S(1)} %get-tuple-element.22), channel_id=1, source_target_pairs={{0,128},{16,144},{32,160},{48,176},{64,192},{80,208},{96,224},{112... | collective-permute-start | bytes 417800 | tf_op jit(solution)/shard_map/ppermute | solution.py:252
  21.6 5.9 %collective-permute-start.9 = (f32[256,256]{1,0:T(8,128)S(1)}, f32[256,256]{1,0:T(8,128)S(1)}, u32[]{:S(2)}, u32[]{:S(2)}) collective-permute-start(f32[256,256]{1,0:T(8,128)S(1)} %bitcast.18), channel_id=1, source_target_pairs={{0,16},{16,0},{32,48},{48,32},{64,80},{80,64},{96,112},{112,96},{1... | collective-permute-start | bytes 786440 | tf_op jit(solution)/shard_map/ppermute | solution.py:256
  22.2 5.7 %collective-permute-start.10 = (f32[256,256]{1,0:T(8,128)S(1)}, f32[256,256]{1,0:T(8,128)S(1)}, u32[]{:S(2)}, u32[]{:S(2)}) collective-permute-start(f32[256,256]{1,0:T(8,128)S(1)} %collective-permute-done.8.r1), channel_id=1, source_target_pairs={{0,16},{16,0},{32,48},{48,32},{64,80},{80,64},{96,112},{112,96},{1... | collective-permute-start | bytes 786440 | tf_op jit(solution)/shard_map/ppermute | solution.py:256
  22.2 5.3 %collective-permute-start.6 = (f32[136,256]{1,0:T(8,128)S(1)}, f32[136,256]{1,0:T(8,128)S(1)}, u32[]{:S(2)}, u32[]{:S(2)}) collective-permute-start(f32[136,256]{1,0:T(8,128)S(1)} %get-tuple-element.23.b0), channel_id=1, source_target_pairs={{0,16},{16,0},{32,48},{48,32},{64,80},{80,64},{96,112},{112,96},{1... | collective-permute-start | bytes 417800 | tf_op jit(solution)/shard_map/ppermute | solution.py:255
  25.4 2.4 %collective-permute-start.7 = (f32[136,256]{1,0:T(8,128)S(1)}, f32[136,256]{1,0:T(8,128)S(1)}, u32[]{:S(2)}, u32[]{:S(2)}) collective-permute-start(f32[136,256]{1,0:T(8,128)S(1)} %collective-permute-done.5.b1), channel_id=1, source_target_pairs={{0,16},{16,0},{32,48},{48,32},{64,80},{80,64},{96,112},{112,96},{1... | collective-permute-start | bytes 417800 | tf_op jit(solution)/shard_map/ppermute | solution.py:255
  30.1 4.5 %collective-permute-start.11 = (f32[16,1024]{1,0:T(8,128)S(1)}, f32[16,1024]{1,0:T(8,128)S(1)}, u32[]{:S(2)}, u32[]{:S(2)}) collective-permute-start(f32[16,1024]{1,0:T(8,128)S(1)} %get-tuple-element.11), channel_id=1, source_target_pairs={{0,32},{16,48},{32,64},{48,80},{64,96},{80,112},{96,0},{112,16},{1... | collective-permute-start | bytes 196616 | tf_op jit(solution)/shard_map/ppermute | solution.py:271
  31.1 5.5 %collective-permute-start.12 = (f32[16,1024]{1,0:T(8,128)S(1)}, f32[16,1024]{1,0:T(8,128)S(1)}, u32[]{:S(2)}, u32[]{:S(2)}) collective-permute-start(f32[16,1024]{1,0:T(8,128)S(1)} %get-tuple-element.12), channel_id=1, source_target_pairs={{0,64},{16,80},{32,96},{48,112},{64,0},{80,16},{96,32},{112,48},{1... | collective-permute-start | bytes 196616 | tf_op jit(solution)/shard_map/ppermute | solution.py:271
  33.7 3.5 %collective-permute-start.13 = (f32[16,1024]{1,0:T(8,128)S(1)}, f32[16,1024]{1,0:T(8,128)S(1)}, u32[]{:S(2)}, u32[]{:S(2)}) collective-permute-start(f32[16,1024]{1,0:T(8,128)S(1)} %get-tuple-element.13), channel_id=1, source_target_pairs={{0,96},{16,112},{32,0},{48,16},{64,32},{80,48},{96,64},{112,80},{1... | collective-permute-start | bytes 196616 | tf_op jit(solution)/shard_map/ppermute | solution.py:271
  37.2 3.2 %collective-permute-start.14 = (f32[16,1024]{1,0:T(8,128)S(1)}, f32[16,1024]{1,0:T(8,128)S(1)}, u32[]{:S(2)}, u32[]{:S(2)}) collective-permute-start(f32[16,1024]{1,0:T(8,128)S(1)} %get-tuple-element.19.x), channel_id=1, source_target_pairs={{0,128},{16,144},{32,160},{48,176},{64,192},{80,208},{96,224},{112... | collective-permute-start | bytes 196616 | tf_op jit(solution)/shard_map/ppermute | solution.py:67
  40.4 5.1 %collective-permute-start.15 = (f32[32,1024]{1,0:T(8,128)S(1)}, f32[32,1024]{1,0:T(8,128)S(1)}, u32[]{:S(2)}, u32[]{:S(2)}) collective-permute-start(f32[32,1024]{1,0:T(8,128)S(1)} %pad_maximum_fusion.1), channel_id=1, source_target_pairs={{0,32},{16,48},{32,64},{48,80},{64,96},{80,112},{96,0},{112,16},{1... | collective-permute-start | bytes 393224 | tf_op jit(solution)/shard_map/ppermute | solution.py:68
  40.9 6.6 %collective-permute-start.16 = (f32[32,1024]{1,0:T(8,128)S(1)}, f32[32,1024]{1,0:T(8,128)S(1)}, u32[]{:S(2)}, u32[]{:S(2)}) collective-permute-start(f32[32,1024]{1,0:T(8,128)S(1)} %pad_maximum_fusion.1), channel_id=1, source_target_pairs={{0,64},{16,80},{32,96},{48,112},{64,0},{80,16},{96,32},{112,48},{1... | collective-permute-start | bytes 393224 | tf_op jit(solution)/shard_map/ppermute | solution.py:68
  43.7 4.1 %collective-permute-start.17 = (f32[32,1024]{1,0:T(8,128)S(1)}, f32[32,1024]{1,0:T(8,128)S(1)}, u32[]{:S(2)}, u32[]{:S(2)}) collective-permute-start(f32[32,1024]{1,0:T(8,128)S(1)} %pad_maximum_fusion.1), channel_id=1, source_target_pairs={{0,96},{16,112},{32,0},{48,16},{64,32},{80,48},{96,64},{112,80},{1... | collective-permute-start | bytes 393224 | tf_op jit(solution)/shard_map/ppermute | solution.py:68
  47.9 5.9 %collective-permute-start.18 = (f32[128,1024]{1,0:T(8,128)S(1)}, f32[128,1024]{1,0:T(8,128)S(1)}, u32[]{:S(2)}, u32[]{:S(2)}) collective-permute-start(f32[128,1024]{1,0:T(8,128)S(1)} %constant_dynamic-update-slice_fusion.5.f), channel_id=1, source_target_pairs={{0,16},{16,0},{32,48},{48,32},{64,80},{80,64},{96,112},{112,96},{1... | collective-permute-start | bytes 1572872 | tf_op jit(solution)/shard_map/ppermute | solution.py:69
  57.1 23.3 %all-to-all-start = ((f32[16,32,256]{2,1,0:T(8,128)}), f32[16,32,256]{2,1,0:T(8,128)S(1)}, u32[]{:S(2)}, u32[]{:S(2)}) async-start(f32[16,32,256]{2,1,0:T(8,128)} %pairs.1), calls=%async_computation | async-start | bytes 1048576 | tf_op jit(solution)/shard_map/all_to_all | solution.py:243
  80.5 4.2 %collective-permute-start.19 = (f32[40,256]{1,0:T(8,128)S(1)}, f32[40,256]{1,0:T(8,128)S(1)}, u32[]{:S(2)}, u32[]{:S(2)}) collective-permute-start(f32[40,256]{1,0:T(8,128)S(1)} %concatenate.37), channel_id=1, source_target_pairs={{0,128},{16,144},{32,160},{48,176},{64,192},{80,208},{96,224},{112... | collective-permute-start | bytes 122888 | tf_op jit(solution)/shard_map/ppermute | solution.py:67
  84.7 4.6 %collective-permute-start.20 = (f32[80,256]{1,0:T(8,128)S(1)}, f32[80,256]{1,0:T(8,128)S(1)}, u32[]{:S(2)}, u32[]{:S(2)}) collective-permute-start(f32[80,256]{1,0:T(8,128)S(1)} %pad_maximum_fusion.2), channel_id=1, source_target_pairs={{0,32},{16,48},{32,64},{48,80},{64,96},{80,112},{96,0},{112,16},{1... | collective-permute-start | bytes 245768 | tf_op jit(solution)/shard_map/ppermute | solution.py:68
  85.1 5.6 %collective-permute-start.21 = (f32[80,256]{1,0:T(8,128)S(1)}, f32[80,256]{1,0:T(8,128)S(1)}, u32[]{:S(2)}, u32[]{:S(2)}) collective-permute-start(f32[80,256]{1,0:T(8,128)S(1)} %pad_maximum_fusion.2), channel_id=1, source_target_pairs={{0,64},{16,80},{32,96},{48,112},{64,0},{80,16},{96,32},{112,48},{1... | collective-permute-start | bytes 245768 | tf_op jit(solution)/shard_map/ppermute | solution.py:68
  88.0 3.3 %collective-permute-start.22 = (f32[80,256]{1,0:T(8,128)S(1)}, f32[80,256]{1,0:T(8,128)S(1)}, u32[]{:S(2)}, u32[]{:S(2)}) collective-permute-start(f32[80,256]{1,0:T(8,128)S(1)} %pad_maximum_fusion.2), channel_id=1, source_target_pairs={{0,96},{16,112},{32,0},{48,16},{64,32},{80,48},{96,64},{112,80},{1... | collective-permute-start | bytes 245768 | tf_op jit(solution)/shard_map/ppermute | solution.py:68
  91.3 6.1 %collective-permute-start.23 = (f32[320,256]{1,0:T(8,128)S(1)}, f32[320,256]{1,0:T(8,128)S(1)}, u32[]{:S(2)}, u32[]{:S(2)}) collective-permute-start(f32[320,256]{1,0:T(8,128)S(1)} %constant_dynamic-update-slice_fusion.10.f), channel_id=1, source_target_pairs={{0,16},{16,0},{32,48},{48,32},{64,80},{80,64},{96,112},{112,96},{1... | collective-permute-start | bytes 983048 | tf_op jit(solution)/shard_map/ppermute | solution.py:69
  98.3 20.9 %all-to-all-start.1 = ((f32[16,32,256]{2,1,0:T(8,128)}), f32[16,32,256]{2,1,0:T(8,128)S(1)}, u32[]{:S(2)}, u32[]{:S(2)}) async-start(f32[16,32,256]{2,1,0:T(8,128)} %get-tuple-element.16), calls=%async_computation.1 | async-start | bytes 1048576 | tf_op jit(solution)/shard_map/all_to_all | solution.py:243

commit v2 on v1

v2 whole, which is shorter than its diff:
```python
import functools

import jax
import jax.numpy as jnp
from jax import lax
from jax.experimental import pallas as pl
from jax.experimental.pallas import tpu as pltpu
from jax.sharding import PartitionSpec as P


SLOTS = 2
HALF = 4_000_000_000
F32, BF16 = jnp.float32, jnp.bfloat16
HIGHEST = lax.Precision.HIGHEST
VM = pl.BlockSpec(memory_space=pltpu.VMEM)
SM = pl.BlockSpec(memory_space=pltpu.SMEM)


def swap(mask):
    return [(i, i ^ mask) for i in range(16)]


CORE, ZPAIR = swap(1), swap(8)
NEAR = (1, 3, 2)


def exchange(parts, axis, unit):
    got = {}
    for d in NEAR:
        got[d] = lax.ppermute(parts[d], axis, swap(d * unit))
    return got


def other_z():
    pairs = []
    for i in range(16):
        step = 1 if i >> 3 else -1
        for s in range(16):
            t = ((((s >> 2) + step) & 3) << 2) | (s & 3)
            pairs.append((i * 16 + s, (i ^ 8) * 16 + t))
    return pairs


OTHER_Z = other_z()


def place():
    ops = lax.axis_index("ops")
    return ops, ops >> 3, (ops >> 1) & 3, ops & 1


def split(x):
    high = x.astype(BF16)
    return high, (x - high.astype(F32)).astype(BF16)


def dot3(a, b, dims=(((1,), (0,)), ((), ()))):
    def one(u, v):
        return lax.dot_general(u, v, dims, preferred_element_type=F32)

    return one(a[0], b[0]) + (one(a[0], b[1]) + one(a[1], b[0]))


NT = (((1,), (1,)), ((), ()))


def call(kernel, out, scratch, *args, specs=None, flops=0):
    return pl.pallas_call(
        kernel,
        out_shape=out,
        in_specs=[VM] * len(args) if specs is None else specs,
        out_specs=jax.tree.map(lambda _: VM, out),
        scratch_shapes=scratch,
        compiler_params=pltpu.CompilerParams(vmem_limit_bytes=24 * 2**20),
        cost_estimate=pl.CostEstimate(flops=flops or 200_000_000, bytes_accessed=1_000_000, transcendentals=0),
    )(*args)


def gather_pair(shard):
    return jnp.concatenate([shard, lax.ppermute(shard, "ops", ZPAIR)])


def gather_rest(pair):
    got = exchange([pair] * 4, "ops", 2)
    mine = jnp.concatenate([pair, got[1], got[2], got[3]])
    return mine, lax.ppermute(mine, "ops", CORE)


def blocks(own, other, rows):
    _, z, x, c = place()
    for cc, ref in enumerate((own, other)):
        for d in range(4):
            for zz in range(2):
                index = ((z ^ zz) << 3) | ((x ^ d) << 1) | (c ^ cc)
                yield ref, (d * 2 + zz) * rows, index


def prep_kernel(left, site, x, kept, given, copy):
    _, z, _, _ = place()
    low, high = left[:, :128], left[:, 128:]
    kept[:256, :] = jnp.where(z == 0, low, high)
    given[:256, :] = jnp.where(z == 0, high, low)
    kept[256:, :] = site[...]
    given[256:, :] = site[...]
    copy[...] = x[...]


def sigma_kernel(size, f, g, b0, b1, b2, b3, r0, r1, r2, r3, o0, o1, o2, o3, ph, pw, vh, vw, acc):
    _, z, x, c = place()
    live = size[0]
    row16 = lax.broadcasted_iota(jnp.int32, (16, 1024), 0)
    for cc, ref in enumerate((f, g)):
        for d in range(4):
            first = pl.multiple_of(((x ^ d) << 5) | ((c ^ cc) << 4), 16)
            value = jnp.where(row16 + (z * 128 + first) < live, ref[d * 16 : d * 16 + 16, :], 0.0)
            high, low = split(value)
            ph[pl.ds(first, 16), :] = high
            pw[pl.ds(first, 16), :] = low
    lefts = (b0, b1, b2, b3)
    pieces = [b[pl.ds(pl.multiple_of((i * 2 + c) * 16, 16), 16), :] for b in lefts for i in range(8)]
    u = dot3(split(jnp.concatenate(pieces)), (ph[...], pw[...]))
    for k, b in enumerate(lefts):
        for p in range(4):
            total = None
            for q in range(4):
                term = b[256 + p : 257 + p, q : q + 1] * u[k * 128 : k * 128 + 128, q * 256 : q * 256 + 256]
                total = term if total is None else total + term
            high, low = split(total)
            vh[p * 128 : p * 128 + 128, k * 256 : k * 256 + 256] = high
            vw[p * 128 : p * 128 + 128, k * 256 : k * 256 + 256] = low
    out = dot3((vh[...], vw[...]), split(jnp.concatenate([r[...] for r in (r0, r1, r2, r3)])))
    at = lax.broadcasted_iota(jnp.int32, (512, 256), 0)
    m = ((at >> 4) & 7) * 32 + c * 16 + (at & 15)
    acc[...] = jnp.where(m < live, out, 0.0)
    for d, o in enumerate((o0, o1, o2, o3)):
        for zz in range(2):
            first = ((z ^ zz) << 6) | ((x ^ d) << 4)
            for p in range(4):
                o[zz * 16 : zz * 16 + 16, p * 256 : p * 256 + 256] = acc[pl.ds(pl.multiple_of(p * 128 + first, 16), 16), :]


def sec_place():
    sec = lax.axis_index("sec")
    return sec, sec >> 2, sec & 3


def pair_kernel(f, g, left, site, o0, o1, o2, o3, xs, xh, xw, xt, acc):
    ops, _, _, _ = place()
    _, zh, y0 = sec_place()
    for ref, at, index in blocks(f, g, 16):
        first = pl.multiple_of(index * 16, 16)
        value = ref[at : at + 16, :]
        xs[pl.ds(first, 16), :] = value
        high, low = split(value)
        xh[pl.ds(first, 16), :] = high
        xw[pl.ds(first, 16), :] = low
    y = dot3(split(left[...]), (xh[...], xw[...]))
    total, gram = jnp.zeros((256, 256), F32), jnp.zeros((16, 256), F32)
    first = pl.multiple_of(ops * 16, 16)
    for p in range(4):
        mixed = None
        for q in range(4):
            term = site[p, q] * y[:, q * 256 : q * 256 + 256]
            mixed = term if mixed is None else mixed + term
        x = xs[:, p * 256 : p * 256 + 256]
        xt[...] = x.T
        total = total + dot3(split(xt[...]), split(mixed))
        gram = gram + jnp.dot(xt[pl.ds(first, 16), :], x, precision=HIGHEST, preferred_element_type=F32)
    acc[...] = total
    for d, o in enumerate((o0, o1, o2, o3)):
        for h in range(4):
            s = ((zh ^ h) << 2) | (y0 ^ d)
            o[h * 16 : h * 16 + 16, :] = acc[pl.ds(pl.multiple_of(s * 16, 16), 16), :]
        o[64:, :] = gram


def row_kernel(a, b, c, d, o0, o1, o2, o3):
    total = a[...] + b[...] + (c[...] + d[...])
    for h, o in enumerate((o0, o1, o2, o3)):
        o[:16, :] = total[h * 16 : h * 16 + 16, :]
        o[16:, :] = total[64:, :]


def route_kernel(f, g, gram, out, tmp):
    ops, _, _, _ = place()
    for ref, at, index in blocks(f, g, 40):
        gram[pl.ds(pl.multiple_of(index * 16, 16), 16), :] = ref[at + 16 : at + 32, :]
        tmp[pl.ds(pl.multiple_of(index * 24, 8), 16), :] = ref[at : at + 16, :]
        tmp[pl.ds(pl.multiple_of(index * 24, 8) + 16, 8), :] = ref[at + 32 : at + 40, :]
    for j in range(SLOTS):
        total = jnp.zeros((16, 256), F32)
        for k in range(16):
            target = tmp[k * 24 + 16 : k * 24 + 17, :]
            chosen = jnp.where(target == (ops * SLOTS + j).astype(F32), 1.0, 0.0)
            total = total + chosen * tmp[k * 24 : k * 24 + 16, :]
        out[j * 16 : j * 16 + 16, :] = total


def factor(block, size):
    count = size // 8
    lanes = lax.broadcasted_iota(jnp.int32, (8, 128), 1)
    sub = lax.broadcasted_iota(jnp.int32, (8, 128), 0)

    def spread(v):
        return jnp.broadcast_to(v, (8, 128))

    w = []
    for b in range(count):
        unit = jnp.where(lanes == sub + (size + b * 8), 1.0, 0.0)
        w.append(jnp.where(lanes < size, block[b * 8 : b * 8 + 8, :], unit))
    for b in range(count):
        t = b * 8
        col = [[spread(w[v][:, t + j : t + j + 1]) for j in range(8)] for v in range(b, count)]
        e = [[spread(col[0][j][i : i + 1, :]) if i >= j else None for j in range(8)] for i in range(8)]
        row = [spread(w[b][j : j + 1, :]) for j in range(8)]
        out = jnp.zeros((8, 128), F32)
        for j in range(8):
            inv = lax.rsqrt(e[j][j])
            row[j] = row[j] * inv
            out = jnp.where(sub == j, row[j], out)
            l = [e[i][j] * inv if i > j else None for i in range(8)]
            for i in range(j + 1, 8):
                for k in range(j + 1, i + 1):
                    e[i][k] = e[i][k] - l[i] * l[k]
            for i in range(j + 1, 8):
                row[i] = row[i] - l[i] * row[j]
            for v in range(1, count - b):
                col[v][j] = col[v][j] * inv
                for k in range(j + 1, 8):
                    col[v][k] = col[v][k] - l[k] * col[v][j]
        w[b] = out
        for v in range(1, count - b):
            rest = w[b + v]
            for j in range(8):
                rest = rest - col[v][j] * row[j]
            w[b + v] = rest
    return jnp.concatenate(w, 0)


def factor_steps(a, u, v, first, last, size=64):
    def dot(p, q):
        return jnp.dot(p, q, precision=HIGHEST, preferred_element_type=F32)

    for s in range(first, last, size):
        low, high = s // 128 * 128, (s + size + 127) // 128 * 128
        pu = a[s : s + size, low:]
        at = [lax.broadcasted_iota(jnp.int32, (size, high), i) for i in (0, 1)]
        pv = jnp.where(at[1] == at[0] + s, 1.0, 0.0)
        if s:
            t = u[:s, low : low + 128].T[s - low : s - low + size, :]
            pu = pu - dot(t, u[:s, low:])
            pv = pv - dot(t, v[:s, :high])
        d = pu[:, :128]
        if s > low:
            d = pltpu.roll(d, 128 - (s - low), 1)
        m = pltpu.roll(factor(d, size), 128 - size, 1)[:, :size]
        u[s : s + size, low:] = dot(m, pu)
        v[s : s + size, :high] = dot(m, pv)


def factor_first(a, u, v):
    factor_steps(a, u, v, 0, 128)


def factor_second(a, u0, v0, v, u):
    u[:128, :] = u0[...]
    v[:128, :128] = v0[...]
    v[:128, 128:] = jnp.zeros((128, 128), F32)
    factor_steps(a, u, v, 128, 256)


def basis_kernel(x, inverse, basis, scale):
    rows = jnp.concatenate([x[:, p * 256 : p * 256 + 256] for p in range(4)])
    q = dot3(split(rows), split(inverse[...]), NT) * scale
    for p in range(4):
        basis[:, p * 256 : p * 256 + 256] = q[p * 16 : p * 16 + 16, :]


def left_kernel(near, far, inverse, o0, o1, o2, o3, ch, cw, acc):
    _, zh, y0 = sec_place()
    ch[...] = jnp.zeros_like(ch)
    cw[...] = jnp.zeros_like(cw)
    for h, r, at in ((0, near, 0), (1, near, 32), (3, far, 0), (2, far, 32)):
        first = pl.multiple_of(((zh ^ h) << 6) | (y0 << 4), 16)
        for j in range(SLOTS):
            high, low = split(r[at + j * 16 : at + j * 16 + 16, :])
            ch[pl.ds(first, 16), j * 256 : j * 256 + 256] = high
            cw[pl.ds(first, 16), j * 256 : j * 256 + 256] = low
    rows = split(inverse[pl.ds(pl.multiple_of(zh * 64, 64), 64), :])
    acc[...] = dot3(rows, (ch[...], cw[...]))
    for d, o in enumerate((o0, o1, o2, o3)):
        first = pl.multiple_of((y0 ^ d) << 4, 16)
        for j in range(SLOTS):
            o[j * 16 : j * 16 + 16, :] = acc[pl.ds(first, 16), j * 256 : j * 256 + 256]


def right_kernel(a, b, c, d, inverse, out):
    total = a[...] + b[...] + (c[...] + d[...])
    result = dot3(split(total), split(inverse[...]), NT)
    for j in range(SLOTS):
        out[j] = result[j * 16 : j * 16 + 16, :]


def step(wavefunction, left_ops, right_ops, site_ops, pattern, sector_sizes, owner, slot):
    def shape(*dims, dtype=F32):
        return jax.ShapeDtypeStruct(dims, dtype)

    def scratch(*dims, dtype=F32):
        return pltpu.VMEM(dims, dtype)

    left, right = left_ops[0, 0], right_ops[0]
    site = site_ops[0] * pattern[0, 0].astype(F32)
    right_z = lax.ppermute(right, ("ops", "sec"), OTHER_Z)
    kept, given, shard = call(
        prep_kernel,
        [shape(264, 128), shape(264, 128), shape(16, 1024)],
        [],
        left,
        jnp.pad(site, ((0, 4), (0, 124))),
        wavefunction[0],
    )
    given = lax.ppermute(given, "ops", ZPAIR)
    got = exchange([wavefunction[0]] * 4, "ops", 2)
    mine = jnp.concatenate([shard, got[1], got[2], got[3]])
    parts = call(
        sigma_kernel,
        [shape(32, 1024)] * 4,
        [scratch(128, 1024, dtype=BF16)] * 2 + [scratch(512, 1024, dtype=BF16)] * 2 + [scratch(512, 256)],
        sector_sizes,
        mine,
        lax.ppermute(mine, "ops", CORE),
        kept,
        given,
        lax.ppermute(kept, "ops", CORE),
        lax.ppermute(given, "ops", CORE),
        right,
        right_z,
        lax.ppermute(right, "ops", CORE),
        lax.ppermute(right_z, "ops", CORE),
        specs=[SM] + [VM] * 10,
    )
    got = exchange(parts, "ops", 2)
    total = parts[0] + got[1] + (got[2] + got[3])
    other = lax.ppermute(total, "ops", ZPAIR)
    pair = jnp.concatenate([total[:16] + other[16:], total[16:] + other[:16]])
    own = pair[:16]
    parts = call(
        pair_kernel,
        [shape(80, 256)] * 4,
        [scratch(256, 1024)] + [scratch(256, 1024, dtype=BF16)] * 2 + [scratch(256, 256)] * 2,
        *gather_rest(pair),
        left,
        site,
        specs=[VM] * 3 + [SM],
    )
    got = exchange(parts, "sec", 1)
    parts = call(row_kernel, [shape(32, 256)] * 4, [], parts[0], got[1], got[2], got[3])
    got = exchange(parts, "sec", 4)
    arrived = parts[0] + got[1] + (got[2] + got[3])
    target = (owner[0] * SLOTS + slot[0]).astype(F32)
    packed = jnp.concatenate([arrived, jnp.broadcast_to(target, (8, 256))])
    gram, routed = call(
        route_kernel, [shape(256, 256), shape(32, 256)], [scratch(384, 256)], *gather_rest(gather_pair(packed))
    )
    other = lax.ppermute(routed, "sec", swap(4))
    upper, begun = call(factor_first, [shape(128, 256), shape(128, 128)], [], gram, flops=HALF)
    near, upper, begun = lax.optimization_barrier((jnp.concatenate([routed, other]), upper, begun))
    far = lax.ppermute(near, "sec", swap(12))
    inverse = call(factor_second, shape(256, 256), [scratch(256, 256)], gram, upper, begun, flops=HALF)
    parts = call(
        left_kernel, [shape(32, 256)] * 4, [scratch(256, 512, dtype=BF16)] * 2 + [scratch(64, 512)], near, far, inverse
    )
    got = exchange(parts, "sec", 1)
    total_rows = 4 * 256 * lax.axis_size("sec")
    basis = call(functools.partial(basis_kernel, scale=float(total_rows) ** 0.5), shape(16, 1024), [], own, inverse)
    out = call(right_kernel, shape(2, 16, 256), [], parts[0], got[1], got[2], got[3], inverse)
    return basis[None], out[None]


def solution(mesh):
    placed = (
        P("sec", "ops", None),
        P("ops", "sec", None, None),
        P("ops", None, None),
        P("ops", None, None),
        P("ops", "sec"),
        P("sec"),
        P("ops"),
        P("ops"),
    )
    return jax.shard_map(
        step,
        mesh=mesh,
        in_specs=placed,
        out_specs=(P("sec", "ops", None), P("ops", None, "sec", None)),
        check_vma=False,
    )
```

time: 121 us -> 115 us (0.950)
  waiting for transfers between devices: 44.6 us -> 36.7 us
  local copies, waits for them, and re-layouts: 0.96 us -> 2.57 us
    all_to_all x2 -> x0, waiting for transfers between devices: 20.2 us -> none  [a2a(): return lax.all_to_all(x, axis, split_axis=0, concat_axis=0, tiled=True)]
    ppermute x24 -> x34, starting transfers between devices: 40.1 us -> 53.3 us  [the longest x21 30.1 us: exchange(): got[d] = lax.ppermute(parts[d], axis, swap(d * unit))]
    all_to_all x2 -> x0, starting transfers between devices: 12.5 us -> none  [a2a(): return lax.all_to_all(x, axis, split_axis=0, concat_axis=0, tiled=True)]
    ppermute x24 -> x34, waiting for transfers between devices: 24.4 us -> 36.7 us  [the longest x21 24.6 us: exchange(): got[d] = lax.ppermute(parts[d], axis, swap(d * unit))]
    unnamed x20 -> x19, local copies, waits for them, and re-layouts: 0.91 us -> 2.53 us
    pallas_call x5 -> x10, Pallas kernels: 17.7 us -> 17.8 us  [call(): pl.pallas_call(kernel, out_shape=out, in_specs=[VM] * len(args) if specs...]
  transfers between devices with their start and end apart: 26 -> 34, of which waited for: 18 -> 19; matrix products, arithmetic and copies ran while one was open for 1% -> 0% of each run, Pallas kernels for 9% -> 9%
where the time goes in v2:
time: 115 us; the launch traced here: 114 us
  starting transfers between devices  53.3 us (46%)
  waiting for transfers between devices  36.7 us (32%)
  Pallas kernels  17.8 us (15%)
  between operations  3.56 us (3%)
  local copies, waits for them, and re-layouts  2.57 us (2%)
    ppermute x21, starting transfers between devices, exchange(): got[d] = lax.ppermute(parts[d], axis, swap(d * unit))  30.1 us
    ppermute x21, waiting for transfers between devices, exchange(): got[d] = lax.ppermute(parts[d], axis, swap(d * unit))  24.6 us
    pallas_call x10, Pallas kernels, call(): pl.pallas_call(kernel, out_shape=out, in_specs=[VM] * len(args) if specs...  17.8 us
    ppermute x2, starting transfers between devices, gather_rest(): return (mine, lax.ppermute(mine, 'ops', CORE))  8.58 us
    ppermute x1, starting transfers between devices, step(): right_z = lax.ppermute(right, ('ops', 'sec'), OTHER_Z)  5.73 us
    ppermute x1, waiting for transfers between devices, step(): other = lax.ppermute(total, 'ops', ZPAIR)  3.8 us
    ppermute x2, waiting for transfers between devices, gather_rest(): return (mine, lax.ppermute(mine, 'ops', CORE))  2.79 us
    ppermute x1, waiting for transfers between devices, step(): given = lax.ppermute(given, 'ops', ZPAIR)  2.76 us
  transfers between devices with their start and end apart: 34, of which 19 were waited for; matrix products, arithmetic and copies ran while one was open for 0% of the time, Pallas kernels for 9%

profile of v2, /device:TPU:1, one launch (start us, length us, event | category | flops | bytes accessed | tf_op | source)
XLA Modules:
  0.0 114.1 jit_solution(1062340256747578668)
XLA Ops:
  0.6 2.1 %collective-permute-start = (f32[16,1024]{1,0:T(8,128)}, f32[16,1024]{1,0:T(8,128)S(1)}, u32[]{:S(2)}, u32[]{:S(2)}) collective-permute-start(f32[16,1024]{1,0:T(8,128)} %bitcast.14), channel_id=1, source_target_pairs={{0,32},{16,48},{32,0},{48,16},{64,96},{80,112},{96,64},{112,80},{1... | collective-permute-start | bytes 196616 | tf_op jit(solution)/shard_map/ppermute | solution.py:30
  2.7 2.5 %collective-permute-start.1 = (f32[16,1024]{1,0:T(8,128)}, f32[16,1024]{1,0:T(8,128)S(1)}, u32[]{:S(2)}, u32[]{:S(2)}) collective-permute-start(f32[16,1024]{1,0:T(8,128)} %bitcast.15), channel_id=1, source_target_pairs={{0,64},{16,80},{32,96},{48,112},{64,0},{80,16},{96,32},{112,48},{1... | collective-permute-start | bytes 196616 | tf_op jit(solution)/shard_map/ppermute | solution.py:30
  5.2 5.7 %collective-permute-start.7 = (f32[256,256]{1,0:T(8,128)}, f32[256,256]{1,0:T(8,128)S(1)}, u32[]{:S(2)}, u32[]{:S(2)}) collective-permute-start(f32[256,256]{1,0:T(8,128)} %bitcast.9), channel_id=1, source_target_pairs={{0,140},{1,141},{2,142},{3,143},{4,128},{5,129},{6,130},{7,131},{8... | collective-permute-start | bytes 786440 | tf_op jit(solution)/shard_map/ppermute | solution.py:313
  11.0 1.8 %collective-permute-start.8 = (f32[256,256]{1,0:T(8,128)}, f32[256,256]{1,0:T(8,128)S(1)}, u32[]{:S(2)}, u32[]{:S(2)}) collective-permute-start(f32[256,256]{1,0:T(8,128)} %bitcast.10), channel_id=1, source_target_pairs={{0,16},{16,0},{32,48},{48,32},{64,80},{80,64},{96,112},{112,96},{1... | collective-permute-start | bytes 786440 | tf_op jit(solution)/shard_map/ppermute | solution.py:338
  16.3 2.1 %collective-permute-start.9 = (f32[256,256]{1,0:T(8,128)S(1)}, f32[256,256]{1,0:T(8,128)S(1)}, u32[]{:S(2)}, u32[]{:S(2)}) collective-permute-start(f32[256,256]{1,0:T(8,128)S(1)} %collective-permute-done.7.r1), channel_id=1, source_target_pairs={{0,16},{16,0},{32,48},{48,32},{64,80},{80,64},{96,112},{112,96},{1... | collective-permute-start | bytes 786440 | tf_op jit(solution)/shard_map/ppermute | solution.py:339
  18.4 2.8 %collective-permute-done.4.b1 = f32[264,128]{1,0:T(8,128)S(1)} collective-permute-done((f32[264,128]{1,0:T(8,128)S(1)}, f32[264,128]{1,0:T(8,128)S(1)}, u32[]{:S(2)}, u32[]{:S(2)}) %collective-permute-start.4) | collective-permute-done | bytes 135200 | tf_op jit(solution)/shard_map/ppermute | solution.py:322
  23.1 3.7 %shard_map.96 = (f32[32,1024]{1,0:T(8,128)S(1)}, f32[32,1024]{1,0:T(8,128)S(1)}, f32[32,1024]{1,0:T(8,128)S(1)}, f32[32,1024]{1,0:T(8,128)S(1)}) custom-call(s32[1]{0:T(128)S(6)} %copy.23.size, f32[64,1024]{1,0:T(8,128)S(1)} %constant_dynamic-update-slice_fusion.f, f32[64,1024]{1,0:T(8,128)S(1)} %collective-permute-done.3.g, ...), custom_call_target="tpu_custom_call" | custom-call | flops 200000000 | bytes 1000000 | tf_op jit(solution)/shard_map/pallas_call | solution.py:68
  26.8 3.7 %collective-permute-start.11 = (f32[32,1024]{1,0:T(8,128)S(1)}, f32[32,1024]{1,0:T(8,128)S(1)}, u32[]{:S(2)}, u32[]{:S(2)}) collective-permute-start(f32[32,1024]{1,0:T(8,128)S(1)} %get-tuple-element.33), channel_id=1, source_target_pairs={{0,64},{16,80},{32,96},{48,112},{64,0},{80,16},{96,32},{112,48},{1... | collective-permute-start | bytes 393224 | tf_op jit(solution)/shard_map/ppermute | solution.py:30
  31.5 5.1 %collective-permute-done.11 = f32[32,1024]{1,0:T(8,128)S(1)} collective-permute-done((f32[32,1024]{1,0:T(8,128)S(1)}, f32[32,1024]{1,0:T(8,128)S(1)}, u32[]{:S(2)}, u32[]{:S(2)}) %collective-permute-start.11) | collective-permute-done | bytes 131104 | tf_op jit(solution)/shard_map/ppermute | solution.py:30
  36.6 2.5 %collective-permute-done.12 = f32[32,1024]{1,0:T(8,128)S(1)} collective-permute-done((f32[32,1024]{1,0:T(8,128)S(1)}, f32[32,1024]{1,0:T(8,128)S(1)}, u32[]{:S(2)}, u32[]{:S(2)}) %collective-permute-start.12) | collective-permute-done | bytes 131104 | tf_op jit(solution)/shard_map/ppermute | solution.py:30
  39.3 3.8 %collective-permute-done.13 = f32[32,1024]{1,0:T(8,128)S(1)} collective-permute-done((f32[32,1024]{1,0:T(8,128)S(1)}, f32[32,1024]{1,0:T(8,128)S(1)}, u32[]{:S(2)}, u32[]{:S(2)}) %collective-permute-start.13) | collective-permute-done | bytes 131104 | tf_op jit(solution)/shard_map/ppermute | solution.py:344
  44.6 2.5 %collective-permute-start.16 = (f32[32,1024]{1,0:T(8,128)S(1)}, f32[32,1024]{1,0:T(8,128)S(1)}, u32[]{:S(2)}, u32[]{:S(2)}) collective-permute-start(f32[32,1024]{1,0:T(8,128)S(1)} %pad_maximum_fusion), channel_id=1, source_target_pairs={{0,96},{16,112},{32,64},{48,80},{64,32},{80,48},{96,0},{112,16},{1... | collective-permute-start | bytes 393224 | tf_op jit(solution)/shard_map/ppermute | solution.py:30
  47.1 2.1 %collective-permute-done.15 = f32[32,1024]{1,0:T(8,128)S(1)} collective-permute-done((f32[32,1024]{1,0:T(8,128)S(1)}, f32[32,1024]{1,0:T(8,128)S(1)}, u32[]{:S(2)}, u32[]{:S(2)}) %collective-permute-start.15) | collective-permute-done | bytes 131104 | tf_op jit(solution)/shard_map/ppermute | solution.py:30
  50.4 3.3 %collective-permute-start.17 = (f32[128,1024]{1,0:T(8,128)S(1)}, f32[128,1024]{1,0:T(8,128)S(1)}, u32[]{:S(2)}, u32[]{:S(2)}) collective-permute-start(f32[128,1024]{1,0:T(8,128)S(1)} %constant_dynamic-update-slice_fusion.4.f), channel_id=1, source_target_pairs={{0,16},{16,0},{32,48},{48,32},{64,80},{80,64},{96,112},{112,96},{1... | collective-permute-start | bytes 1572872 | tf_op jit(solution)/shard_map/ppermute | solution.py:86
  53.7 1.5 %collective-permute-done.17.g = f32[128,1024]{1,0:T(8,128)S(1)} collective-permute-done((f32[128,1024]{1,0:T(8,128)S(1)}, f32[128,1024]{1,0:T(8,128)S(1)}, u32[]{:S(2)}, u32[]{:S(2)}) %collective-permute-start.17) | collective-permute-done | bytes 524320 | tf_op jit(solution)/shard_map/ppermute | solution.py:86
  55.2 2.6 %shard_map.97 = (f32[80,256]{1,0:T(8,128)S(1)}, f32[80,256]{1,0:T(8,128)S(1)}, f32[80,256]{1,0:T(8,128)S(1)}, f32[80,256]{1,0:T(8,128)S(1)}) custom-call(f32[128,1024]{1,0:T(8,128)S(1)} %constant_dynamic-update-slice_fusion.4.f, f32[128,1024]{1,0:T(8,128)S(1)} %collective-permute-done.17.g, f32[256,256]{1,0:T(8,128)S(1)} %bitcast.13, ...), custom_call_target="tpu_custom_call" | custom-call | flops 200000000 | bytes 1000000 | tf_op jit(solution)/shard_map/pallas_call | solution.py:68
  57.8 1.4 %collective-permute-start.18 = (f32[80,256]{1,0:T(8,128)S(1)}, f32[80,256]{1,0:T(8,128)S(1)}, u32[]{:S(2)}, u32[]{:S(2)}) collective-permute-start(f32[80,256]{1,0:T(8,128)S(1)} %get-tuple-element.36), channel_id=1, source_target_pairs={{0,1},{1,0},{2,3},{3,2},{4,5},{5,4},{6,7},{7,6},{8,9},{9,8},{10,11... | collective-permute-start | bytes 245768 | tf_op jit(solution)/shard_map/ppermute | solution.py:30
  59.2 2.6 %collective-permute-start.19 = (f32[80,256]{1,0:T(8,128)S(1)}, f32[80,256]{1,0:T(8,128)S(1)}, u32[]{:S(2)}, u32[]{:S(2)}) collective-permute-start(f32[80,256]{1,0:T(8,128)S(1)} %get-tuple-element.37), channel_id=1, source_target_pairs={{0,2},{1,3},{2,0},{3,1},{4,6},{5,7},{6,4},{7,5},{8,10},{9,11},{10,... | collective-permute-start | bytes 245768 | tf_op jit(solution)/shard_map/ppermute | solution.py:30
  61.8 3.9 %collective-permute-done.19.c = f32[80,256]{1,0:T(8,128)S(1)} collective-permute-done((f32[80,256]{1,0:T(8,128)S(1)}, f32[80,256]{1,0:T(8,128)S(1)}, u32[]{:S(2)}, u32[]{:S(2)}) %collective-permute-start.19) | collective-permute-done | bytes 81952 | tf_op jit(solution)/shard_map/ppermute | solution.py:30
  65.7 2.0 %collective-permute-done.20.d = f32[80,256]{1,0:T(8,128)S(1)} collective-permute-done((f32[80,256]{1,0:T(8,128)S(1)}, f32[80,256]{1,0:T(8,128)S(1)}, u32[]{:S(2)}, u32[]{:S(2)}) %collective-permute-start.20) | collective-permute-done | bytes 81952 | tf_op jit(solution)/shard_map/ppermute | solution.py:30
  68.3 2.8 %collective-permute-start.22 = (f32[32,256]{1,0:T(8,128)S(1)}, f32[32,256]{1,0:T(8,128)S(1)}, u32[]{:S(2)}, u32[]{:S(2)}) collective-permute-start(f32[32,256]{1,0:T(8,128)S(1)} %get-tuple-element.41), channel_id=1, source_target_pairs={{0,8},{1,9},{2,10},{3,11},{4,12},{5,13},{6,14},{7,15},{8,0},{9,1},... | collective-permute-start | bytes 98312 | tf_op jit(solution)/shard_map/ppermute | solution.py:30
  71.1 2.4 %collective-permute-start.23 = (f32[32,256]{1,0:T(8,128)S(1)}, f32[32,256]{1,0:T(8,128)S(1)}, u32[]{:S(2)}, u32[]{:S(2)}) collective-permute-start(f32[32,256]{1,0:T(8,128)S(1)} %get-tuple-element.42), channel_id=1, source_target_pairs={{0,12},{1,13},{2,14},{3,15},{4,8},{5,9},{6,10},{7,11},{8,4},{9,5},... | collective-permute-start | bytes 98312 | tf_op jit(solution)/shard_map/ppermute | solution.py:30
  77.0 2.3 %collective-permute-done.24 = f32[40,256]{1,0:T(8,128)S(1)} collective-permute-done((f32[40,256]{1,0:T(8,128)S(1)}, f32[40,256]{1,0:T(8,128)S(1)}, u32[]{:S(2)}, u32[]{:S(2)}) %collective-permute-start.24) | collective-permute-done | bytes 40992 | tf_op jit(solution)/shard_map/ppermute | solution.py:80
  79.4 3.5 %collective-permute-start.26 = (f32[80,256]{1,0:T(8,128)S(1)}, f32[80,256]{1,0:T(8,128)S(1)}, u32[]{:S(2)}, u32[]{:S(2)}) collective-permute-start(f32[80,256]{1,0:T(8,128)S(1)} %pad_maximum_fusion.1), channel_id=1, source_target_pairs={{0,64},{16,80},{32,96},{48,112},{64,0},{80,16},{96,32},{112,48},{1... | collective-permute-start | bytes 245768 | tf_op jit(solution)/shard_map/ppermute | solution.py:30
  83.2 2.4 %collective-permute-done.26 = f32[80,256]{1,0:T(8,128)S(1)} collective-permute-done((f32[80,256]{1,0:T(8,128)S(1)}, f32[80,256]{1,0:T(8,128)S(1)}, u32[]{:S(2)}, u32[]{:S(2)}) %collective-permute-start.26) | collective-permute-done | bytes 81952 | tf_op jit(solution)/shard_map/ppermute | solution.py:30
  85.6 1.8 %collective-permute-done.27 = f32[80,256]{1,0:T(8,128)S(1)} collective-permute-done((f32[80,256]{1,0:T(8,128)S(1)}, f32[80,256]{1,0:T(8,128)S(1)}, u32[]{:S(2)}, u32[]{:S(2)}) %collective-permute-start.27) | collective-permute-done | bytes 81952 | tf_op jit(solution)/shard_map/ppermute | solution.py:30
  87.4 5.3 %collective-permute-start.28 = (f32[320,256]{1,0:T(8,128)S(1)}, f32[320,256]{1,0:T(8,128)S(1)}, u32[]{:S(2)}, u32[]{:S(2)}) collective-permute-start(f32[320,256]{1,0:T(8,128)S(1)} %constant_dynamic-update-slice_fusion.9.f), channel_id=1, source_target_pairs={{0,16},{16,0},{32,48},{48,32},{64,80},{80,64},{96,112},{112,96},{1... | collective-permute-start | bytes 983048 | tf_op jit(solution)/shard_map/ppermute | solution.py:86
  95.4 4.5 %shard_map.100 = (f32[128,256]{1,0:T(8,128)S(1)}, f32[128,128]{1,0:T(8,128)S(1)}) custom-call(f32[256,256]{1,0:T(8,128)S(1)} %get-tuple-element.43.a), custom_call_target="tpu_custom_call" | custom-call | flops 4000000000 | bytes 1000000 | tf_op jit(solution)/shard_map/pallas_call | solution.py:68
  99.9 2.0 %collective-permute-start.30 = (f32[64,256]{1,0:T(8,128)S(1)}, f32[64,256]{1,0:T(8,128)S(1)}, u32[]{:S(2)}, u32[]{:S(2)}) collective-permute-start(f32[64,256]{1,0:T(8,128)S(1)} %pad_maximum_fusion.2.near), channel_id=1, source_target_pairs={{0,12},{1,13},{2,14},{3,15},{4,8},{5,9},{6,10},{7,11},{8,4},{9,5},... | collective-permute-start | bytes 196616 | tf_op jit(solution)/shard_map/ppermute | solution.py:368
  101.9 4.8 %shard_map.101.inverse = f32[256,256]{1,0:T(8,128)S(1)} custom-call(f32[256,256]{1,0:T(8,128)S(1)} %get-tuple-element.43.a, f32[128,256]{1,0:T(8,128)S(1)} %get-tuple-element.47.u0, f32[128,128]{1,0:T(8,128)S(1)} %get-tuple-element.48.v0), custom_call_target="tpu_custom_call" | custom-call | flops 4000000000 | bytes 1000000 | tf_op jit(solution)/shard_map/pallas_call | solution.py:68
  107.1 1.7 %collective-permute-start.32 = (f32[32,256]{1,0:T(8,128)S(1)}, f32[32,256]{1,0:T(8,128)S(1)}, u32[]{:S(2)}, u32[]{:S(2)}) collective-permute-start(f32[32,256]{1,0:T(8,128)S(1)} %get-tuple-element.52), channel_id=1, source_target_pairs={{0,2},{1,3},{2,0},{3,1},{4,6},{5,7},{6,4},{7,5},{8,10},{9,11},{10,... | collective-permute-start | bytes 98312 | tf_op jit(solution)/shard_map/ppermute | solution.py:30
  108.8 2.2 %collective-permute-start.33 = (f32[32,256]{1,0:T(8,128)S(1)}, f32[32,256]{1,0:T(8,128)S(1)}, u32[]{:S(2)}, u32[]{:S(2)}) collective-permute-start(f32[32,256]{1,0:T(8,128)S(1)} %get-tuple-element.53), channel_id=1, source_target_pairs={{0,3},{1,2},{2,1},{3,0},{4,7},{5,6},{6,5},{7,4},{8,11},{9,10},{10,... | collective-permute-start | bytes 98312 | tf_op jit(solution)/shard_map/ppermute | solution.py:30
  (79 shorter events, 17.3 us)
Async XLA Ops:
  0.6 15.3 %collective-permute-start = (f32[16,1024]{1,0:T(8,128)}, f32[16,1024]{1,0:T(8,128)S(1)}, u32[]{:S(2)}, u32[]{:S(2)}) collective-permute-start(f32[16,1024]{1,0:T(8,128)} %bitcast.14), channel_id=1, source_target_pairs={{0,32},{16,48},{32,0},{48,16},{64,96},{80,112},{96,64},{112,80},{1... | collective-permute-start | bytes 196616 | tf_op jit(solution)/shard_map/ppermute | solution.py:30
  2.7 13.3 %collective-permute-start.1 = (f32[16,1024]{1,0:T(8,128)}, f32[16,1024]{1,0:T(8,128)S(1)}, u32[]{:S(2)}, u32[]{:S(2)}) collective-permute-start(f32[16,1024]{1,0:T(8,128)} %bitcast.15), channel_id=1, source_target_pairs={{0,64},{16,80},{32,96},{48,112},{64,0},{80,16},{96,32},{112,48},{1... | collective-permute-start | bytes 196616 | tf_op jit(solution)/shard_map/ppermute | solution.py:30
  5.2 10.9 %collective-permute-start.2 = (f32[16,1024]{1,0:T(8,128)}, f32[16,1024]{1,0:T(8,128)S(1)}, u32[]{:S(2)}, u32[]{:S(2)}) collective-permute-start(f32[16,1024]{1,0:T(8,128)} %bitcast.16), channel_id=1, source_target_pairs={{0,96},{16,112},{32,64},{48,80},{64,32},{80,48},{96,0},{112,16},{1... | collective-permute-start | bytes 196616 | tf_op jit(solution)/shard_map/ppermute | solution.py:30
  5.2 11.1 %collective-permute-start.7 = (f32[256,256]{1,0:T(8,128)}, f32[256,256]{1,0:T(8,128)S(1)}, u32[]{:S(2)}, u32[]{:S(2)}) collective-permute-start(f32[256,256]{1,0:T(8,128)} %bitcast.9), channel_id=1, source_target_pairs={{0,140},{1,141},{2,142},{3,143},{4,128},{5,129},{6,130},{7,131},{8... | collective-permute-start | bytes 786440 | tf_op jit(solution)/shard_map/ppermute | solution.py:313
  11.0 11.8 %collective-permute-start.8 = (f32[256,256]{1,0:T(8,128)}, f32[256,256]{1,0:T(8,128)S(1)}, u32[]{:S(2)}, u32[]{:S(2)}) collective-permute-start(f32[256,256]{1,0:T(8,128)} %bitcast.10), channel_id=1, source_target_pairs={{0,16},{16,0},{32,48},{48,32},{64,80},{80,64},{96,112},{112,96},{1... | collective-permute-start | bytes 786440 | tf_op jit(solution)/shard_map/ppermute | solution.py:338
  16.0 5.2 %collective-permute-start.4 = (f32[264,128]{1,0:T(8,128)S(1)}, f32[264,128]{1,0:T(8,128)S(1)}, u32[]{:S(2)}, u32[]{:S(2)}) collective-permute-start(f32[264,128]{1,0:T(8,128)S(1)} %get-tuple-element.30), channel_id=1, source_target_pairs={{0,128},{16,144},{32,160},{48,176},{64,192},{80,208},{96,224},{112... | collective-permute-start | bytes 405512 | tf_op jit(solution)/shard_map/ppermute | solution.py:322
  16.1 6.9 %collective-permute-start.3 = (f32[64,1024]{1,0:T(8,128)S(1)}, f32[64,1024]{1,0:T(8,128)S(1)}, u32[]{:S(2)}, u32[]{:S(2)}) collective-permute-start(f32[64,1024]{1,0:T(8,128)S(1)} %constant_dynamic-update-slice_fusion.f), channel_id=1, source_target_pairs={{0,16},{16,0},{32,48},{48,32},{64,80},{80,64},{96,112},{112,96},{1... | collective-permute-start | bytes 786440 | tf_op jit(solution)/shard_map/ppermute | solution.py:331
  16.3 6.7 %collective-permute-start.9 = (f32[256,256]{1,0:T(8,128)S(1)}, f32[256,256]{1,0:T(8,128)S(1)}, u32[]{:S(2)}, u32[]{:S(2)}) collective-permute-start(f32[256,256]{1,0:T(8,128)S(1)} %collective-permute-done.7.r1), channel_id=1, source_target_pairs={{0,16},{16,0},{32,48},{48,32},{64,80},{80,64},{96,112},{112,96},{1... | collective-permute-start | bytes 786440 | tf_op jit(solution)/shard_map/ppermute | solution.py:339
  18.4 4.3 %collective-permute-start.5 = (f32[264,128]{1,0:T(8,128)S(1)}, f32[264,128]{1,0:T(8,128)S(1)}, u32[]{:S(2)}, u32[]{:S(2)}) collective-permute-start(f32[264,128]{1,0:T(8,128)S(1)} %get-tuple-element.29.b0), channel_id=1, source_target_pairs={{0,16},{16,0},{32,48},{48,32},{64,80},{80,64},{96,112},{112,96},{1... | collective-permute-start | bytes 405512 | tf_op jit(solution)/shard_map/ppermute | solution.py:334
  26.7 4.8 %collective-permute-start.10 = (f32[32,1024]{1,0:T(8,128)S(1)}, f32[32,1024]{1,0:T(8,128)S(1)}, u32[]{:S(2)}, u32[]{:S(2)}) collective-permute-start(f32[32,1024]{1,0:T(8,128)S(1)} %get-tuple-element.32), channel_id=1, source_target_pairs={{0,32},{16,48},{32,0},{48,16},{64,96},{80,112},{96,64},{112,80},{1... | collective-permute-start | bytes 393224 | tf_op jit(solution)/shard_map/ppermute | solution.py:30
  26.8 9.7 %collective-permute-start.11 = (f32[32,1024]{1,0:T(8,128)S(1)}, f32[32,1024]{1,0:T(8,128)S(1)}, u32[]{:S(2)}, u32[]{:S(2)}) collective-permute-start(f32[32,1024]{1,0:T(8,128)S(1)} %get-tuple-element.33), channel_id=1, source_target_pairs={{0,64},{16,80},{32,96},{48,112},{64,0},{80,16},{96,32},{112,48},{1... | collective-permute-start | bytes 393224 | tf_op jit(solution)/shard_map/ppermute | solution.py:30
  30.5 8.6 %collective-permute-start.12 = (f32[32,1024]{1,0:T(8,128)S(1)}, f32[32,1024]{1,0:T(8,128)S(1)}, u32[]{:S(2)}, u32[]{:S(2)}) collective-permute-start(f32[32,1024]{1,0:T(8,128)S(1)} %get-tuple-element.34), channel_id=1, source_target_pairs={{0,96},{16,112},{32,64},{48,80},{64,32},{80,48},{96,0},{112,16},{1... | collective-permute-start | bytes 393224 | tf_op jit(solution)/shard_map/ppermute | solution.py:30
  39.2 3.9 %collective-permute-start.13 = (f32[32,1024]{1,0:T(8,128)S(1)}, f32[32,1024]{1,0:T(8,128)S(1)}, u32[]{:S(2)}, u32[]{:S(2)}) collective-permute-start(f32[32,1024]{1,0:T(8,128)S(1)} %add_add_fusion), channel_id=1, source_target_pairs={{0,128},{16,144},{32,160},{48,176},{64,192},{80,208},{96,224},{112... | collective-permute-start | bytes 393224 | tf_op jit(solution)/shard_map/ppermute | solution.py:344
  43.1 4.0 %collective-permute-start.14 = (f32[32,1024]{1,0:T(8,128)S(1)}, f32[32,1024]{1,0:T(8,128)S(1)}, u32[]{:S(2)}, u32[]{:S(2)}) collective-permute-start(f32[32,1024]{1,0:T(8,128)S(1)} %pad_maximum_fusion), channel_id=1, source_target_pairs={{0,32},{16,48},{32,0},{48,16},{64,96},{80,112},{96,64},{112,80},{1... | collective-permute-start | bytes 393224 | tf_op jit(solution)/shard_map/ppermute | solution.py:30
  43.2 5.9 %collective-permute-start.15 = (f32[32,1024]{1,0:T(8,128)S(1)}, f32[32,1024]{1,0:T(8,128)S(1)}, u32[]{:S(2)}, u32[]{:S(2)}) collective-permute-start(f32[32,1024]{1,0:T(8,128)S(1)} %pad_maximum_fusion), channel_id=1, source_target_pairs={{0,64},{16,80},{32,96},{48,112},{64,0},{80,16},{96,32},{112,48},{1... | collective-permute-start | bytes 393224 | tf_op jit(solution)/shard_map/ppermute | solution.py:30
  44.6 5.8 %collective-permute-start.16 = (f32[32,1024]{1,0:T(8,128)S(1)}, f32[32,1024]{1,0:T(8,128)S(1)}, u32[]{:S(2)}, u32[]{:S(2)}) collective-permute-start(f32[32,1024]{1,0:T(8,128)S(1)} %pad_maximum_fusion), channel_id=1, source_target_pairs={{0,96},{16,112},{32,64},{48,80},{64,32},{80,48},{96,0},{112,16},{1... | collective-permute-start | bytes 393224 | tf_op jit(solution)/shard_map/ppermute | solution.py:30
  50.4 4.8 %collective-permute-start.17 = (f32[128,1024]{1,0:T(8,128)S(1)}, f32[128,1024]{1,0:T(8,128)S(1)}, u32[]{:S(2)}, u32[]{:S(2)}) collective-permute-start(f32[128,1024]{1,0:T(8,128)S(1)} %constant_dynamic-update-slice_fusion.4.f), channel_id=1, source_target_pairs={{0,16},{16,0},{32,48},{48,32},{64,80},{80,64},{96,112},{112,96},{1... | collective-permute-start | bytes 1572872 | tf_op jit(solution)/shard_map/ppermute | solution.py:86
  57.8 4.0 %collective-permute-start.18 = (f32[80,256]{1,0:T(8,128)S(1)}, f32[80,256]{1,0:T(8,128)S(1)}, u32[]{:S(2)}, u32[]{:S(2)}) collective-permute-start(f32[80,256]{1,0:T(8,128)S(1)} %get-tuple-element.36), channel_id=1, source_target_pairs={{0,1},{1,0},{2,3},{3,2},{4,5},{5,4},{6,7},{7,6},{8,9},{9,8},{10,11... | collective-permute-start | bytes 245768 | tf_op jit(solution)/shard_map/ppermute | solution.py:30
  59.2 6.5 %collective-permute-start.19 = (f32[80,256]{1,0:T(8,128)S(1)}, f32[80,256]{1,0:T(8,128)S(1)}, u32[]{:S(2)}, u32[]{:S(2)}) collective-permute-start(f32[80,256]{1,0:T(8,128)S(1)} %get-tuple-element.37), channel_id=1, source_target_pairs={{0,2},{1,3},{2,0},{3,1},{4,6},{5,7},{6,4},{7,5},{8,10},{9,11},{10,... | collective-permute-start | bytes 245768 | tf_op jit(solution)/shard_map/ppermute | solution.py:30
  61.8 5.9 %collective-permute-start.20 = (f32[80,256]{1,0:T(8,128)S(1)}, f32[80,256]{1,0:T(8,128)S(1)}, u32[]{:S(2)}, u32[]{:S(2)}) collective-permute-start(f32[80,256]{1,0:T(8,128)S(1)} %get-tuple-element.38), channel_id=1, source_target_pairs={{0,3},{1,2},{2,1},{3,0},{4,7},{5,6},{6,5},{7,4},{8,11},{9,10},{10,... | collective-permute-start | bytes 245768 | tf_op jit(solution)/shard_map/ppermute | solution.py:30
  67.8 7.0 %collective-permute-start.21 = (f32[32,256]{1,0:T(8,128)S(1)}, f32[32,256]{1,0:T(8,128)S(1)}, u32[]{:S(2)}, u32[]{:S(2)}) collective-permute-start(f32[32,256]{1,0:T(8,128)S(1)} %get-tuple-element.40), channel_id=1, source_target_pairs={{0,4},{1,5},{2,6},{3,7},{4,0},{5,1},{6,2},{7,3},{8,12},{9,13},{10,... | collective-permute-start | bytes 98312 | tf_op jit(solution)/shard_map/ppermute | solution.py:30
  68.3 6.8 %collective-permute-start.22 = (f32[32,256]{1,0:T(8,128)S(1)}, f32[32,256]{1,0:T(8,128)S(1)}, u32[]{:S(2)}, u32[]{:S(2)}) collective-permute-start(f32[32,256]{1,0:T(8,128)S(1)} %get-tuple-element.41), channel_id=1, source_target_pairs={{0,8},{1,9},{2,10},{3,11},{4,12},{5,13},{6,14},{7,15},{8,0},{9,1},... | collective-permute-start | bytes 98312 | tf_op jit(solution)/shard_map/ppermute | solution.py:30
  71.1 5.2 %collective-permute-start.23 = (f32[32,256]{1,0:T(8,128)S(1)}, f32[32,256]{1,0:T(8,128)S(1)}, u32[]{:S(2)}, u32[]{:S(2)}) collective-permute-start(f32[32,256]{1,0:T(8,128)S(1)} %get-tuple-element.42), channel_id=1, source_target_pairs={{0,12},{1,13},{2,14},{3,15},{4,8},{5,9},{6,10},{7,11},{8,4},{9,5},... | collective-permute-start | bytes 98312 | tf_op jit(solution)/shard_map/ppermute | solution.py:30
  79.3 4.0 %collective-permute-start.25 = (f32[80,256]{1,0:T(8,128)S(1)}, f32[80,256]{1,0:T(8,128)S(1)}, u32[]{:S(2)}, u32[]{:S(2)}) collective-permute-start(f32[80,256]{1,0:T(8,128)S(1)} %pad_maximum_fusion.1), channel_id=1, source_target_pairs={{0,32},{16,48},{32,0},{48,16},{64,96},{80,112},{96,64},{112,80},{1... | collective-permute-start | bytes 245768 | tf_op jit(solution)/shard_map/ppermute | solution.py:30
  79.4 6.2 %collective-permute-start.26 = (f32[80,256]{1,0:T(8,128)S(1)}, f32[80,256]{1,0:T(8,128)S(1)}, u32[]{:S(2)}, u32[]{:S(2)}) collective-permute-start(f32[80,256]{1,0:T(8,128)S(1)} %pad_maximum_fusion.1), channel_id=1, source_target_pairs={{0,64},{16,80},{32,96},{48,112},{64,0},{80,16},{96,32},{112,48},{1... | collective-permute-start | bytes 245768 | tf_op jit(solution)/shard_map/ppermute | solution.py:30
  82.9 4.5 %collective-permute-start.27 = (f32[80,256]{1,0:T(8,128)S(1)}, f32[80,256]{1,0:T(8,128)S(1)}, u32[]{:S(2)}, u32[]{:S(2)}) collective-permute-start(f32[80,256]{1,0:T(8,128)S(1)} %pad_maximum_fusion.1), channel_id=1, source_target_pairs={{0,96},{16,112},{32,64},{48,80},{64,32},{80,48},{96,0},{112,16},{1... | collective-permute-start | bytes 245768 | tf_op jit(solution)/shard_map/ppermute | solution.py:30
  87.4 6.6 %collective-permute-start.28 = (f32[320,256]{1,0:T(8,128)S(1)}, f32[320,256]{1,0:T(8,128)S(1)}, u32[]{:S(2)}, u32[]{:S(2)}) collective-permute-start(f32[320,256]{1,0:T(8,128)S(1)} %constant_dynamic-update-slice_fusion.9.f), channel_id=1, source_target_pairs={{0,16},{16,0},{32,48},{48,32},{64,80},{80,64},{96,112},{112,96},{1... | collective-permute-start | bytes 983048 | tf_op jit(solution)/shard_map/ppermute | solution.py:86
  94.1 5.8 %collective-permute-start.29 = (f32[32,256]{1,0:T(8,128)S(1)}, f32[32,256]{1,0:T(8,128)S(1)}, u32[]{:S(2)}, u32[]{:S(2)}) collective-permute-start(f32[32,256]{1,0:T(8,128)S(1)} %get-tuple-element.44), channel_id=1, source_target_pairs={{0,4},{1,5},{2,6},{3,7},{4,0},{5,1},{6,2},{7,3},{8,12},{9,13},{10,... | collective-permute-start | bytes 98312 | tf_op jit(solution)/shard_map/ppermute | solution.py:365
  99.9 6.8 %collective-permute-start.30 = (f32[64,256]{1,0:T(8,128)S(1)}, f32[64,256]{1,0:T(8,128)S(1)}, u32[]{:S(2)}, u32[]{:S(2)}) collective-permute-start(f32[64,256]{1,0:T(8,128)S(1)} %pad_maximum_fusion.2.near), channel_id=1, source_target_pairs={{0,12},{1,13},{2,14},{3,15},{4,8},{5,9},{6,10},{7,11},{8,4},{9,5},... | collective-permute-start | bytes 196616 | tf_op jit(solution)/shard_map/ppermute | solution.py:368
  107.0 4.9 %collective-permute-start.31 = (f32[32,256]{1,0:T(8,128)S(1)}, f32[32,256]{1,0:T(8,128)S(1)}, u32[]{:S(2)}, u32[]{:S(2)}) collective-permute-start(f32[32,256]{1,0:T(8,128)S(1)} %get-tuple-element.51), channel_id=1, source_target_pairs={{0,1},{1,0},{2,3},{3,2},{4,5},{5,4},{6,7},{7,6},{8,9},{9,8},{10,11... | collective-permute-start | bytes 98312 | tf_op jit(solution)/shard_map/ppermute | solution.py:30
  107.1 4.8 %collective-permute-start.32 = (f32[32,256]{1,0:T(8,128)S(1)}, f32[32,256]{1,0:T(8,128)S(1)}, u32[]{:S(2)}, u32[]{:S(2)}) collective-permute-start(f32[32,256]{1,0:T(8,128)S(1)} %get-tuple-element.52), channel_id=1, source_target_pairs={{0,2},{1,3},{2,0},{3,1},{4,6},{5,7},{6,4},{7,5},{8,10},{9,11},{10,... | collective-permute-start | bytes 98312 | tf_op jit(solution)/shard_map/ppermute | solution.py:30
  108.8 4.4 %collective-permute-start.33 = (f32[32,256]{1,0:T(8,128)S(1)}, f32[32,256]{1,0:T(8,128)S(1)}, u32[]{:S(2)}, u32[]{:S(2)}) collective-permute-start(f32[32,256]{1,0:T(8,128)S(1)} %get-tuple-element.53), channel_id=1, source_target_pairs={{0,3},{1,2},{2,1},{3,0},{4,7},{5,6},{6,5},{7,4},{8,11},{9,10},{10,... | collective-permute-start | bytes 98312 | tf_op jit(solution)/shard_map/ppermute | solution.py:30
  (7 other events, 22.5 us)

commit v3 on v2

--- a/solution.py
+++ b/solution.py
@@ -29,19 +29,6 @@
     for d in NEAR:
         got[d] = lax.ppermute(parts[d], axis, swap(d * unit))
     return got
-
-
-def other_z():
-    pairs = []
-    for i in range(16):
-        step = 1 if i >> 3 else -1
-        for s in range(16):
-            t = ((((s >> 2) + step) & 3) << 2) | (s & 3)
-            pairs.append((i * 16 + s, (i ^ 8) * 16 + t))
-    return pairs
-
-
-OTHER_Z = other_z()
 
 
 def place():
@@ -95,28 +82,29 @@
                 yield ref, (d * 2 + zz) * rows, index
 
 
-def prep_kernel(left, site, x, kept, given, copy):
-    _, z, _, _ = place()
-    low, high = left[:, :128], left[:, 128:]
-    kept[:256, :] = jnp.where(z == 0, low, high)
-    given[:256, :] = jnp.where(z == 0, high, low)
-    kept[256:, :] = site[...]
-    given[256:, :] = site[...]
+def prep_kernel(left, site, pattern, x, packed, copy):
+    packed[:256, :] = left[...]
+    row, lane = (lax.broadcasted_iota(jnp.int32, (8, 256), i) for i in (0, 1))
+    values = jnp.zeros((8, 256), F32)
+    scale = pattern[0, 0].astype(F32)
+    for p in range(4):
+        for q in range(4):
+            values = jnp.where((row == p) & (lane == q), site[p, q] * scale, values)
+    packed[256:, :] = values
     copy[...] = x[...]
 
 
-def sigma_kernel(size, f, g, b0, b1, b2, b3, r0, r1, r2, r3, o0, o1, o2, o3, ph, pw, vh, vw, acc):
+def sigma_kernel(size, f, g, b0, b1, r0, r1, o0, o1, o2, o3, ph, pw, vh, vw, acc):
     _, z, x, c = place()
     live = size[0]
     row16 = lax.broadcasted_iota(jnp.int32, (16, 1024), 0)
-    for cc, ref in enumerate((f, g)):
-        for d in range(4):
-            first = pl.multiple_of(((x ^ d) << 5) | ((c ^ cc) << 4), 16)
-            value = jnp.where(row16 + (z * 128 + first) < live, ref[d * 16 : d * 16 + 16, :], 0.0)
-            high, low = split(value)
-            ph[pl.ds(first, 16), :] = high
-            pw[pl.ds(first, 16), :] = low
-    lefts = (b0, b1, b2, b3)
+    for ref, at, index in blocks(f, g, 16):
+        first = pl.multiple_of(index * 16, 16)
+        value = jnp.where(row16 + first < live, ref[at : at + 16, :], 0.0)
+        high, low = split(value)
+        ph[pl.ds(first, 16), :] = high
+        pw[pl.ds(first, 16), :] = low
+    lefts = (b0, b1)
     pieces = [b[pl.ds(pl.multiple_of((i * 2 + c) * 16, 16), 16), :] for b in lefts for i in range(8)]
     u = dot3(split(jnp.concatenate(pieces)), (ph[...], pw[...]))
     for k, b in enumerate(lefts):
@@ -128,7 +116,7 @@
             high, low = split(total)
             vh[p * 128 : p * 128 + 128, k * 256 : k * 256 + 256] = high
             vw[p * 128 : p * 128 + 128, k * 256 : k * 256 + 256] = low
-    out = dot3((vh[...], vw[...]), split(jnp.concatenate([r[...] for r in (r0, r1, r2, r3)])))
+    out = dot3((vh[...], vw[...]), split(jnp.concatenate([r0[...], r1[...]])))
     at = lax.broadcasted_iota(jnp.int32, (512, 256), 0)
     m = ((at >> 4) & 7) * 32 + c * 16 + (at & 15)
     acc[...] = jnp.where(m < live, out, 0.0)
@@ -162,10 +150,12 @@
         for q in range(4):
             term = site[p, q] * y[:, q * 256 : q * 256 + 256]
             mixed = term if mixed is None else mixed + term
-        x = xs[:, p * 256 : p * 256 + 256]
-        xt[...] = x.T
+        at = slice(p * 256, p * 256 + 256)
+        xt[...] = xs[:, at].T
         total = total + dot3(split(xt[...]), split(mixed))
-        gram = gram + jnp.dot(xt[pl.ds(first, 16), :], x, precision=HIGHEST, preferred_element_type=F32)
+        rows, right = split(xt[pl.ds(first, 16), :]), (xh[:, at], xw[:, at])
+        low = jnp.dot(rows[1], right[1], preferred_element_type=F32)
+        gram = gram + (dot3(rows, right) + low)
     acc[...] = total
     for d, o in enumerate((o0, o1, o2, o3)):
         for h in range(4):
@@ -174,11 +164,12 @@
         o[64:, :] = gram
 
 
-def row_kernel(a, b, c, d, o0, o1, o2, o3):
+def row_kernel(a, b, c, d, kept, given):
     total = a[...] + b[...] + (c[...] + d[...])
-    for h, o in enumerate((o0, o1, o2, o3)):
-        o[:16, :] = total[h * 16 : h * 16 + 16, :]
-        o[16:, :] = total[64:, :]
+    for o, order in ((kept, (0, 3)), (given, (1, 2))):
+        for n, h in enumerate(order):
+            o[n * 16 : n * 16 + 16, :] = total[h * 16 : h * 16 + 16, :]
+        o[32:, :] = total[64:, :]
 
 
 def route_kernel(f, g, gram, out, tmp):
@@ -310,34 +301,35 @@
 
     left, right = left_ops[0, 0], right_ops[0]
     site = site_ops[0] * pattern[0, 0].astype(F32)
-    right_z = lax.ppermute(right, ("ops", "sec"), OTHER_Z)
-    kept, given, shard = call(
+    other = lax.ppermute(wavefunction[0], "ops", ZPAIR)
+    packed, shard = call(
         prep_kernel,
-        [shape(264, 128), shape(264, 128), shape(16, 1024)],
+        [shape(264, 256), shape(16, 1024)],
         [],
         left,
-        jnp.pad(site, ((0, 4), (0, 124))),
+        site_ops[0],
+        pattern,
         wavefunction[0],
-    )
-    given = lax.ppermute(given, "ops", ZPAIR)
-    got = exchange([wavefunction[0]] * 4, "ops", 2)
-    mine = jnp.concatenate([shard, got[1], got[2], got[3]])
+        specs=[VM, SM, SM, VM],
+    )
+    given = lax.ppermute(packed, "ops", CORE)
+    right_given = lax.ppermute(right, "ops", CORE)
+    pair = jnp.concatenate([shard, other])
+    got = exchange([pair] * 4, "ops", 2)
+    mine = jnp.concatenate([pair, got[1], got[2], got[3]])
+    mine, given, right_given = lax.optimization_barrier((mine, given, right_given))
     parts = call(
         sigma_kernel,
         [shape(32, 1024)] * 4,
-        [scratch(128, 1024, dtype=BF16)] * 2 + [scratch(512, 1024, dtype=BF16)] * 2 + [scratch(512, 256)],
+        [scratch(256, 1024, dtype=BF16)] * 2 + [scratch(512, 512, dtype=BF16)] * 2 + [scratch(512, 256)],
         sector_sizes,
         mine,
         lax.ppermute(mine, "ops", CORE),
-        kept,
+        packed,
         given,
-        lax.ppermute(kept, "ops", CORE),
-        lax.ppermute(given, "ops", CORE),
         right,
-        right_z,
-        lax.ppermute(right, "ops", CORE),
-        lax.ppermute(right_z, "ops", CORE),
-        specs=[SM] + [VM] * 10,
+        right_given,
+        specs=[SM] + [VM] * 6,
     )
     got = exchange(parts, "ops", 2)
     total = parts[0] + got[1] + (got[2] + got[3])
@@ -347,16 +339,18 @@
     parts = call(
         pair_kernel,
         [shape(80, 256)] * 4,
-        [scratch(256, 1024)] + [scratch(256, 1024, dtype=BF16)] * 2 + [scratch(256, 256)] * 2,
+        [scratch(256, 1024)]
+        + [scratch(256, 1024, dtype=BF16)] * 2
+        + [scratch(256, 256)] * 2,
         *gather_rest(pair),
         left,
         site,
         specs=[VM] * 3 + [SM],
     )
     got = exchange(parts, "sec", 1)
-    parts = call(row_kernel, [shape(32, 256)] * 4, [], parts[0], got[1], got[2], got[3])
-    got = exchange(parts, "sec", 4)
-    arrived = parts[0] + got[1] + (got[2] + got[3])
+    kept, given = call(row_kernel, [shape(48, 256)] * 2, [], parts[0], got[1], got[2], got[3])
+    half = kept + lax.ppermute(given, "sec", swap(4))
+    arrived = jnp.concatenate([half[:16], half[32:]]) + lax.ppermute(half[16:], "sec", swap(12))
     target = (owner[0] * SLOTS + slot[0]).astype(F32)
     packed = jnp.concatenate([arrived, jnp.broadcast_to(target, (8, 256))])
     gram, routed = call(

time: 115 us -> 115 us (level)
  waiting for transfers between devices: 36.7 us -> 39.4 us
  Pallas kernels: 17.8 us -> 16.5 us
    ppermute x21 -> x18, starting transfers between devices: 30.1 us -> 24.4 us  [exchange(): got[d] = lax.ppermute(parts[d], axis, swap(d * unit))]
    ppermute x21 -> x18, waiting for transfers between devices: 24.6 us -> 28.1 us  [exchange(): got[d] = lax.ppermute(parts[d], axis, swap(d * unit))]
    ppermute x6 -> x5, waiting for transfers between devices: 3.19 us -> 1.75 us  [the longest x1 1.3 us: step(): lax.ppermute(half[16:], 'sec', swap(12))]
    pallas_call x10, Pallas kernels: 17.8 us -> 16.5 us  [call(): pl.pallas_call(kernel, out_shape=out, in_specs=[VM] * len(args) if specs...]
    ppermute x1, starting transfers between devices: 1.96 us -> 3.34 us  [step(): far = lax.ppermute(near, 'sec', swap(12))]
    ppermute x6 -> x5, starting transfers between devices: 10.6 us -> 11.5 us  [the longest x1 4.39 us: step(): lax.ppermute(half[16:], 'sec', swap(12))]
  transfers between devices with their start and end apart: 34 -> 30, of which waited for: 19 -> 19; matrix products, arithmetic and copies ran while one was open for 0% -> 0% of each run, Pallas kernels for 9% -> 9%
where the time goes in v3:
time: 115 us; the launch traced here: 114 us
  starting transfers between devices  52.4 us (46%)
  waiting for transfers between devices  39.4 us (34%)
  Pallas kernels  16.5 us (14%)
  between operations  3.51 us (3%)
  local copies, waits for them, and re-layouts  2.6 us (2%)
    ppermute x18, waiting for transfers between devices, exchange(): got[d] = lax.ppermute(parts[d], axis, swap(d * unit))  28.1 us
    ppermute x18, starting transfers between devices, exchange(): got[d] = lax.ppermute(parts[d], axis, swap(d * unit))  24.4 us
    pallas_call x10, Pallas kernels, call(): pl.pallas_call(kernel, out_shape=out, in_specs=[VM] * len(args) if specs...  16.5 us
    ppermute x2, starting transfers between devices, gather_rest(): return (mine, lax.ppermute(mine, 'ops', CORE))  9.27 us
    ppermute x1, starting transfers between devices, step(): lax.ppermute(half[16:], 'sec', swap(12))  4.39 us
    ppermute x1, waiting for transfers between devices, step(): other = lax.ppermute(total, 'ops', ZPAIR)  3.58 us
    ppermute x1, starting transfers between devices, step(): far = lax.ppermute(near, 'sec', swap(12))  3.34 us
    ppermute x1, starting transfers between devices, step(): half = kept + lax.ppermute(given, 'sec', swap(4))  3.07 us
  transfers between devices with their start and end apart: 30, of which 19 were waited for; matrix products, arithmetic and copies ran while one was open for 0% of the time, Pallas kernels for 9%

profile of v3, /device:TPU:1, one launch (start us, length us, event | category | flops | bytes accessed | tf_op | source)
XLA Modules:
  0.0 114.4 jit_solution(17258782259194491207)
XLA Ops:
  0.6 2.5 %collective-permute-start = (f32[16,1024]{1,0:T(8,128)}, f32[16,1024]{1,0:T(8,128)S(1)}, u32[]{:S(2)}, u32[]{:S(2)}) collective-permute-start(f32[16,1024]{1,0:T(8,128)} %bitcast.14), channel_id=1, source_target_pairs={{0,128},{16,144},{32,160},{48,176},{64,192},{80,208},{96,224},{112... | collective-permute-start | bytes 196616 | tf_op jit(solution)/shard_map/ppermute | solution.py:304
  8.3 2.5 %collective-permute-start.2 = (f32[32,1024]{1,0:T(8,128)S(1)}, f32[32,1024]{1,0:T(8,128)S(1)}, u32[]{:S(2)}, u32[]{:S(2)}) collective-permute-start(f32[32,1024]{1,0:T(8,128)S(1)} %get-tuple-element.60), channel_id=1, source_target_pairs={{0,64},{16,80},{32,96},{48,112},{64,0},{80,16},{96,32},{112,48},{1... | collective-permute-start | bytes 393224 | tf_op jit(solution)/shard_map/ppermute | solution.py:30
  10.7 1.5 %collective-permute-start.4 = (f32[264,256]{1,0:T(8,128)S(1)}, f32[264,256]{1,0:T(8,128)S(1)}, u32[]{:S(2)}, u32[]{:S(2)}) collective-permute-start(f32[264,256]{1,0:T(8,128)S(1)} %get-tuple-element.29.b0), channel_id=1, source_target_pairs={{0,16},{16,0},{32,48},{48,32},{64,80},{80,64},{96,112},{112,96},{1... | collective-permute-start | bytes 811016 | tf_op jit(solution)/shard_map/ppermute | solution.py:315
  12.9 2.9 %collective-permute-done.2 = f32[32,1024]{1,0:T(8,128)S(1)} collective-permute-done((f32[32,1024]{1,0:T(8,128)S(1)}, f32[32,1024]{1,0:T(8,128)S(1)}, u32[]{:S(2)}, u32[]{:S(2)}) %collective-permute-start.2) | collective-permute-done | bytes 131104 | tf_op jit(solution)/shard_map/ppermute | solution.py:30
  15.9 4.4 %collective-permute-done.3 = f32[32,1024]{1,0:T(8,128)S(1)} collective-permute-done((f32[32,1024]{1,0:T(8,128)S(1)}, f32[32,1024]{1,0:T(8,128)S(1)}, u32[]{:S(2)}, u32[]{:S(2)}) %collective-permute-start.3) | collective-permute-done | bytes 131104 | tf_op jit(solution)/shard_map/ppermute | solution.py:30
  22.4 1.6 %shard_map.96 = (f32[32,1024]{1,0:T(8,128)S(1)}, f32[32,1024]{1,0:T(8,128)S(1)}, f32[32,1024]{1,0:T(8,128)S(1)}, f32[32,1024]{1,0:T(8,128)S(1)}) custom-call(s32[1]{0:T(128)S(6)} %copy.25.size, f32[128,1024]{1,0:T(8,128)S(1)} %constant_dynamic-update-slice_fusion.2.f, f32[128,1024]{1,0:T(8,128)S(1)} %collective-permute-done.6.g, ...), custom_call_target="tpu_custom_call" | custom-call | flops 200000000 | bytes 1000000 | tf_op jit(solution)/shard_map/pallas_call | solution.py:55
  24.1 1.9 %collective-permute-start.8 = (f32[32,1024]{1,0:T(8,128)S(1)}, f32[32,1024]{1,0:T(8,128)S(1)}, u32[]{:S(2)}, u32[]{:S(2)}) collective-permute-start(f32[32,1024]{1,0:T(8,128)S(1)} %get-tuple-element.35), channel_id=1, source_target_pairs={{0,64},{16,80},{32,96},{48,112},{64,0},{80,16},{96,32},{112,48},{1... | collective-permute-start | bytes 393224 | tf_op jit(solution)/shard_map/ppermute | solution.py:30
  26.0 2.0 %collective-permute-start.9 = (f32[32,1024]{1,0:T(8,128)S(1)}, f32[32,1024]{1,0:T(8,128)S(1)}, u32[]{:S(2)}, u32[]{:S(2)}) collective-permute-start(f32[32,1024]{1,0:T(8,128)S(1)} %get-tuple-element.36), channel_id=1, source_target_pairs={{0,96},{16,112},{32,64},{48,80},{64,32},{80,48},{96,0},{112,16},{1... | collective-permute-start | bytes 393224 | tf_op jit(solution)/shard_map/ppermute | solution.py:30
  28.8 3.3 %collective-permute-done.8 = f32[32,1024]{1,0:T(8,128)S(1)} collective-permute-done((f32[32,1024]{1,0:T(8,128)S(1)}, f32[32,1024]{1,0:T(8,128)S(1)}, u32[]{:S(2)}, u32[]{:S(2)}) %collective-permute-start.8) | collective-permute-done | bytes 131104 | tf_op jit(solution)/shard_map/ppermute | solution.py:30
  32.0 2.5 %collective-permute-done.9 = f32[32,1024]{1,0:T(8,128)S(1)} collective-permute-done((f32[32,1024]{1,0:T(8,128)S(1)}, f32[32,1024]{1,0:T(8,128)S(1)}, u32[]{:S(2)}, u32[]{:S(2)}) %collective-permute-start.9) | collective-permute-done | bytes 131104 | tf_op jit(solution)/shard_map/ppermute | solution.py:30
  34.9 3.6 %collective-permute-done.10 = f32[32,1024]{1,0:T(8,128)S(1)} collective-permute-done((f32[32,1024]{1,0:T(8,128)S(1)}, f32[32,1024]{1,0:T(8,128)S(1)}, u32[]{:S(2)}, u32[]{:S(2)}) %collective-permute-start.10) | collective-permute-done | bytes 131104 | tf_op jit(solution)/shard_map/ppermute | solution.py:336
  38.7 3.1 %collective-permute-start.12 = (f32[32,1024]{1,0:T(8,128)S(1)}, f32[32,1024]{1,0:T(8,128)S(1)}, u32[]{:S(2)}, u32[]{:S(2)}) collective-permute-start(f32[32,1024]{1,0:T(8,128)S(1)} %pad_maximum_fusion), channel_id=1, source_target_pairs={{0,64},{16,80},{32,96},{48,112},{64,0},{80,16},{96,32},{112,48},{1... | collective-permute-start | bytes 393224 | tf_op jit(solution)/shard_map/ppermute | solution.py:30
  42.5 3.2 %collective-permute-done.12 = f32[32,1024]{1,0:T(8,128)S(1)} collective-permute-done((f32[32,1024]{1,0:T(8,128)S(1)}, f32[32,1024]{1,0:T(8,128)S(1)}, u32[]{:S(2)}, u32[]{:S(2)}) %collective-permute-start.12) | collective-permute-done | bytes 131104 | tf_op jit(solution)/shard_map/ppermute | solution.py:30
  45.8 1.5 %collective-permute-done.13 = f32[32,1024]{1,0:T(8,128)S(1)} collective-permute-done((f32[32,1024]{1,0:T(8,128)S(1)}, f32[32,1024]{1,0:T(8,128)S(1)}, u32[]{:S(2)}, u32[]{:S(2)}) %collective-permute-start.13) | collective-permute-done | bytes 131104 | tf_op jit(solution)/shard_map/ppermute | solution.py:30
  47.3 3.4 %collective-permute-start.14 = (f32[128,1024]{1,0:T(8,128)S(1)}, f32[128,1024]{1,0:T(8,128)S(1)}, u32[]{:S(2)}, u32[]{:S(2)}) collective-permute-start(f32[128,1024]{1,0:T(8,128)S(1)} %constant_dynamic-update-slice_fusion.7.f), channel_id=1, source_target_pairs={{0,16},{16,0},{32,48},{48,32},{64,80},{80,64},{96,112},{112,96},{1... | collective-permute-start | bytes 1572872 | tf_op jit(solution)/shard_map/ppermute | solution.py:73
  50.8 1.5 %collective-permute-done.14.g = f32[128,1024]{1,0:T(8,128)S(1)} collective-permute-done((f32[128,1024]{1,0:T(8,128)S(1)}, f32[128,1024]{1,0:T(8,128)S(1)}, u32[]{:S(2)}, u32[]{:S(2)}) %collective-permute-start.14) | collective-permute-done | bytes 524320 | tf_op jit(solution)/shard_map/ppermute | solution.py:73
  52.3 2.7 %shard_map.97 = (f32[80,256]{1,0:T(8,128)S(1)}, f32[80,256]{1,0:T(8,128)S(1)}, f32[80,256]{1,0:T(8,128)S(1)}, f32[80,256]{1,0:T(8,128)S(1)}) custom-call(f32[128,1024]{1,0:T(8,128)S(1)} %constant_dynamic-update-slice_fusion.7.f, f32[128,1024]{1,0:T(8,128)S(1)} %collective-permute-done.14.g, f32[256,256]{1,0:T(8,128)S(1)} %bitcast.12, ...), custom_call_target="tpu_custom_call" | custom-call | flops 200000000 | bytes 1000000 | tf_op jit(solution)/shard_map/pallas_call | solution.py:55
  55.0 1.6 %collective-permute-start.15 = (f32[80,256]{1,0:T(8,128)S(1)}, f32[80,256]{1,0:T(8,128)S(1)}, u32[]{:S(2)}, u32[]{:S(2)}) collective-permute-start(f32[80,256]{1,0:T(8,128)S(1)} %get-tuple-element.38), channel_id=1, source_target_pairs={{0,1},{1,0},{2,3},{3,2},{4,5},{5,4},{6,7},{7,6},{8,9},{9,8},{10,11... | collective-permute-start | bytes 245768 | tf_op jit(solution)/shard_map/ppermute | solution.py:30
  56.6 2.6 %collective-permute-start.16 = (f32[80,256]{1,0:T(8,128)S(1)}, f32[80,256]{1,0:T(8,128)S(1)}, u32[]{:S(2)}, u32[]{:S(2)}) collective-permute-start(f32[80,256]{1,0:T(8,128)S(1)} %get-tuple-element.39), channel_id=1, source_target_pairs={{0,2},{1,3},{2,0},{3,1},{4,6},{5,7},{6,4},{7,5},{8,10},{9,11},{10,... | collective-permute-start | bytes 245768 | tf_op jit(solution)/shard_map/ppermute | solution.py:30
  59.2 3.9 %collective-permute-done.16.c = f32[80,256]{1,0:T(8,128)S(1)} collective-permute-done((f32[80,256]{1,0:T(8,128)S(1)}, f32[80,256]{1,0:T(8,128)S(1)}, u32[]{:S(2)}, u32[]{:S(2)}) %collective-permute-start.16) | collective-permute-done | bytes 81952 | tf_op jit(solution)/shard_map/ppermute | solution.py:30
  63.1 2.0 %collective-permute-done.17.d = f32[80,256]{1,0:T(8,128)S(1)} collective-permute-done((f32[80,256]{1,0:T(8,128)S(1)}, f32[80,256]{1,0:T(8,128)S(1)}, u32[]{:S(2)}, u32[]{:S(2)}) %collective-permute-start.17) | collective-permute-done | bytes 81952 | tf_op jit(solution)/shard_map/ppermute | solution.py:30
  65.2 3.1 %collective-permute-start.18 = (f32[48,256]{1,0:T(8,128)S(1)}, f32[48,256]{1,0:T(8,128)S(1)}, u32[]{:S(2)}, u32[]{:S(2)}) collective-permute-start(f32[48,256]{1,0:T(8,128)S(1)} %get-tuple-element.42), channel_id=1, source_target_pairs={{0,4},{1,5},{2,6},{3,7},{4,0},{5,1},{6,2},{7,3},{8,12},{9,13},{10,... | collective-permute-start | bytes 147464 | tf_op jit(solution)/shard_map/ppermute | solution.py:352
  70.0 4.4 %collective-permute-start.19 = (f32[32,256]{1,0:T(8,128)S(1)}, f32[32,256]{1,0:T(8,128)S(1)}, u32[]{:S(2)}, u32[]{:S(2)}) collective-permute-start(f32[32,256]{1,0:T(8,128)S(1)} %slice.34), channel_id=1, source_target_pairs={{0,12},{1,13},{2,14},{3,15},{4,8},{5,9},{6,10},{7,11},{8,4},{9,5},... | collective-permute-start | bytes 98312 | tf_op jit(solution)/shard_map/ppermute | solution.py:353
  76.5 2.3 %collective-permute-done.20 = f32[40,256]{1,0:T(8,128)S(1)} collective-permute-done((f32[40,256]{1,0:T(8,128)S(1)}, f32[40,256]{1,0:T(8,128)S(1)}, u32[]{:S(2)}, u32[]{:S(2)}) %collective-permute-start.20) | collective-permute-done | bytes 40992 | tf_op jit(solution)/shard_map/ppermute | solution.py:67
  80.4 2.3 %collective-permute-start.23 = (f32[80,256]{1,0:T(8,128)S(1)}, f32[80,256]{1,0:T(8,128)S(1)}, u32[]{:S(2)}, u32[]{:S(2)}) collective-permute-start(f32[80,256]{1,0:T(8,128)S(1)} %pad_maximum_fusion.1), channel_id=1, source_target_pairs={{0,96},{16,112},{32,64},{48,80},{64,32},{80,48},{96,0},{112,16},{1... | collective-permute-start | bytes 245768 | tf_op jit(solution)/shard_map/ppermute | solution.py:30
  84.9 5.8 %collective-permute-start.24 = (f32[320,256]{1,0:T(8,128)S(1)}, f32[320,256]{1,0:T(8,128)S(1)}, u32[]{:S(2)}, u32[]{:S(2)}) collective-permute-start(f32[320,256]{1,0:T(8,128)S(1)} %constant_dynamic-update-slice_fusion.12.f), channel_id=1, source_target_pairs={{0,16},{16,0},{32,48},{48,32},{64,80},{80,64},{96,112},{112,96},{1... | collective-permute-start | bytes 983048 | tf_op jit(solution)/shard_map/ppermute | solution.py:73
  92.1 2.2 %collective-permute-start.25 = (f32[32,256]{1,0:T(8,128)S(1)}, f32[32,256]{1,0:T(8,128)S(1)}, u32[]{:S(2)}, u32[]{:S(2)}) collective-permute-start(f32[32,256]{1,0:T(8,128)S(1)} %get-tuple-element.44), channel_id=1, source_target_pairs={{0,4},{1,5},{2,6},{3,7},{4,0},{5,1},{6,2},{7,3},{8,12},{9,13},{10,... | collective-permute-start | bytes 98312 | tf_op jit(solution)/shard_map/ppermute | solution.py:359
  94.3 4.5 %shard_map.100 = (f32[128,256]{1,0:T(8,128)S(1)}, f32[128,128]{1,0:T(8,128)S(1)}) custom-call(f32[256,256]{1,0:T(8,128)S(1)} %get-tuple-element.43.a), custom_call_target="tpu_custom_call" | custom-call | flops 4000000000 | bytes 1000000 | tf_op jit(solution)/shard_map/pallas_call | solution.py:55
  98.8 3.3 %collective-permute-start.26 = (f32[64,256]{1,0:T(8,128)S(1)}, f32[64,256]{1,0:T(8,128)S(1)}, u32[]{:S(2)}, u32[]{:S(2)}) collective-permute-start(f32[64,256]{1,0:T(8,128)S(1)} %pad_maximum_fusion.2.near), channel_id=1, source_target_pairs={{0,12},{1,13},{2,14},{3,15},{4,8},{5,9},{6,10},{7,11},{8,4},{9,5},... | collective-permute-start | bytes 196616 | tf_op jit(solution)/shard_map/ppermute | solution.py:362
  102.2 4.8 %shard_map.101.inverse = f32[256,256]{1,0:T(8,128)S(1)} custom-call(f32[256,256]{1,0:T(8,128)S(1)} %get-tuple-element.43.a, f32[128,256]{1,0:T(8,128)S(1)} %get-tuple-element.47.u0, f32[128,128]{1,0:T(8,128)S(1)} %get-tuple-element.48.v0), custom_call_target="tpu_custom_call" | custom-call | flops 4000000000 | bytes 1000000 | tf_op jit(solution)/shard_map/pallas_call | solution.py:55
  107.5 1.8 %collective-permute-start.28 = (f32[32,256]{1,0:T(8,128)S(1)}, f32[32,256]{1,0:T(8,128)S(1)}, u32[]{:S(2)}, u32[]{:S(2)}) collective-permute-start(f32[32,256]{1,0:T(8,128)S(1)} %get-tuple-element.52), channel_id=1, source_target_pairs={{0,2},{1,3},{2,0},{3,1},{4,6},{5,7},{6,4},{7,5},{8,10},{9,11},{10,... | collective-permute-start | bytes 98312 | tf_op jit(solution)/shard_map/ppermute | solution.py:30
  109.2 2.1 %collective-permute-start.29 = (f32[32,256]{1,0:T(8,128)S(1)}, f32[32,256]{1,0:T(8,128)S(1)}, u32[]{:S(2)}, u32[]{:S(2)}) collective-permute-start(f32[32,256]{1,0:T(8,128)S(1)} %get-tuple-element.53), channel_id=1, source_target_pairs={{0,3},{1,2},{2,1},{3,0},{4,7},{5,6},{6,5},{7,4},{8,11},{9,10},{10,... | collective-permute-start | bytes 98312 | tf_op jit(solution)/shard_map/ppermute | solution.py:30
  (74 shorter events, 20.0 us)
Async XLA Ops:
  0.6 6.3 %collective-permute-start = (f32[16,1024]{1,0:T(8,128)}, f32[16,1024]{1,0:T(8,128)S(1)}, u32[]{:S(2)}, u32[]{:S(2)}) collective-permute-start(f32[16,1024]{1,0:T(8,128)} %bitcast.14), channel_id=1, source_target_pairs={{0,128},{16,144},{32,160},{48,176},{64,192},{80,208},{96,224},{112... | collective-permute-start | bytes 196616 | tf_op jit(solution)/shard_map/ppermute | solution.py:304
  6.9 5.3 %copy-start = (f32[1,256,256]{2,1,0:T(8,128)S(1)}, f32[1,256,256]{2,1,0:T(8,128)}, u32[]{:S(2)}) copy-start(f32[1,256,256]{2,1,0:T(8,128)} %param.10) | copy-start | bytes 786436
  7.0 6.0 %collective-permute-start.1 = (f32[32,1024]{1,0:T(8,128)S(1)}, f32[32,1024]{1,0:T(8,128)S(1)}, u32[]{:S(2)}, u32[]{:S(2)}) collective-permute-start(f32[32,1024]{1,0:T(8,128)S(1)} %get-tuple-element.60), channel_id=1, source_target_pairs={{0,32},{16,48},{32,0},{48,16},{64,96},{80,112},{96,64},{112,80},{1... | collective-permute-start | bytes 393224 | tf_op jit(solution)/shard_map/ppermute | solution.py:30
  8.3 7.6 %collective-permute-start.2 = (f32[32,1024]{1,0:T(8,128)S(1)}, f32[32,1024]{1,0:T(8,128)S(1)}, u32[]{:S(2)}, u32[]{:S(2)}) collective-permute-start(f32[32,1024]{1,0:T(8,128)S(1)} %get-tuple-element.60), channel_id=1, source_target_pairs={{0,64},{16,80},{32,96},{48,112},{64,0},{80,16},{96,32},{112,48},{1... | collective-permute-start | bytes 393224 | tf_op jit(solution)/shard_map/ppermute | solution.py:30
  10.7 9.6 %collective-permute-start.4 = (f32[264,256]{1,0:T(8,128)S(1)}, f32[264,256]{1,0:T(8,128)S(1)}, u32[]{:S(2)}, u32[]{:S(2)}) collective-permute-start(f32[264,256]{1,0:T(8,128)S(1)} %get-tuple-element.29.b0), channel_id=1, source_target_pairs={{0,16},{16,0},{32,48},{48,32},{64,80},{80,64},{96,112},{112,96},{1... | collective-permute-start | bytes 811016 | tf_op jit(solution)/shard_map/ppermute | solution.py:315
  12.2 8.0 %collective-permute-start.5 = (f32[256,256]{1,0:T(8,128)S(1)}, f32[256,256]{1,0:T(8,128)S(1)}, u32[]{:S(2)}, u32[]{:S(2)}) collective-permute-start(f32[256,256]{1,0:T(8,128)S(1)} %bitcast.9), channel_id=1, source_target_pairs={{0,16},{16,0},{32,48},{48,32},{64,80},{80,64},{96,112},{112,96},{1... | collective-permute-start | bytes 786440 | tf_op jit(solution)/shard_map/ppermute | solution.py:316
  12.2 8.0 %collective-permute-start.3 = (f32[32,1024]{1,0:T(8,128)S(1)}, f32[32,1024]{1,0:T(8,128)S(1)}, u32[]{:S(2)}, u32[]{:S(2)}) collective-permute-start(f32[32,1024]{1,0:T(8,128)S(1)} %get-tuple-element.60), channel_id=1, source_target_pairs={{0,96},{16,112},{32,64},{48,80},{64,32},{80,48},{96,0},{112,16},{1... | collective-permute-start | bytes 393224 | tf_op jit(solution)/shard_map/ppermute | solution.py:30
  20.3 2.1 %collective-permute-start.6 = (f32[128,1024]{1,0:T(8,128)S(1)}, f32[128,1024]{1,0:T(8,128)S(1)}, u32[]{:S(2)}, u32[]{:S(2)}) collective-permute-start(f32[128,1024]{1,0:T(8,128)S(1)} %constant_dynamic-update-slice_fusion.2.f), channel_id=1, source_target_pairs={{0,16},{16,0},{32,48},{48,32},{64,80},{80,64},{96,112},{112,96},{1... | collective-permute-start | bytes 1572872 | tf_op jit(solution)/shard_map/ppermute | solution.py:327
  24.0 4.8 %collective-permute-start.7 = (f32[32,1024]{1,0:T(8,128)S(1)}, f32[32,1024]{1,0:T(8,128)S(1)}, u32[]{:S(2)}, u32[]{:S(2)}) collective-permute-start(f32[32,1024]{1,0:T(8,128)S(1)} %get-tuple-element.34), channel_id=1, source_target_pairs={{0,32},{16,48},{32,0},{48,16},{64,96},{80,112},{96,64},{112,80},{1... | collective-permute-start | bytes 393224 | tf_op jit(solution)/shard_map/ppermute | solution.py:30
  24.1 7.9 %collective-permute-start.8 = (f32[32,1024]{1,0:T(8,128)S(1)}, f32[32,1024]{1,0:T(8,128)S(1)}, u32[]{:S(2)}, u32[]{:S(2)}) collective-permute-start(f32[32,1024]{1,0:T(8,128)S(1)} %get-tuple-element.35), channel_id=1, source_target_pairs={{0,64},{16,80},{32,96},{48,112},{64,0},{80,16},{96,32},{112,48},{1... | collective-permute-start | bytes 393224 | tf_op jit(solution)/shard_map/ppermute | solution.py:30
  26.0 8.6 %collective-permute-start.9 = (f32[32,1024]{1,0:T(8,128)S(1)}, f32[32,1024]{1,0:T(8,128)S(1)}, u32[]{:S(2)}, u32[]{:S(2)}) collective-permute-start(f32[32,1024]{1,0:T(8,128)S(1)} %get-tuple-element.36), channel_id=1, source_target_pairs={{0,96},{16,112},{32,64},{48,80},{64,32},{80,48},{96,0},{112,16},{1... | collective-permute-start | bytes 393224 | tf_op jit(solution)/shard_map/ppermute | solution.py:30
  34.6 3.9 %collective-permute-start.10 = (f32[32,1024]{1,0:T(8,128)S(1)}, f32[32,1024]{1,0:T(8,128)S(1)}, u32[]{:S(2)}, u32[]{:S(2)}) collective-permute-start(f32[32,1024]{1,0:T(8,128)S(1)} %add_add_fusion), channel_id=1, source_target_pairs={{0,128},{16,144},{32,160},{48,176},{64,192},{80,208},{96,224},{112... | collective-permute-start | bytes 393224 | tf_op jit(solution)/shard_map/ppermute | solution.py:336
  38.6 3.9 %collective-permute-start.11 = (f32[32,1024]{1,0:T(8,128)S(1)}, f32[32,1024]{1,0:T(8,128)S(1)}, u32[]{:S(2)}, u32[]{:S(2)}) collective-permute-start(f32[32,1024]{1,0:T(8,128)S(1)} %pad_maximum_fusion), channel_id=1, source_target_pairs={{0,32},{16,48},{32,0},{48,16},{64,96},{80,112},{96,64},{112,80},{1... | collective-permute-start | bytes 393224 | tf_op jit(solution)/shard_map/ppermute | solution.py:30
  38.7 7.1 %collective-permute-start.12 = (f32[32,1024]{1,0:T(8,128)S(1)}, f32[32,1024]{1,0:T(8,128)S(1)}, u32[]{:S(2)}, u32[]{:S(2)}) collective-permute-start(f32[32,1024]{1,0:T(8,128)S(1)} %pad_maximum_fusion), channel_id=1, source_target_pairs={{0,64},{16,80},{32,96},{48,112},{64,0},{80,16},{96,32},{112,48},{1... | collective-permute-start | bytes 393224 | tf_op jit(solution)/shard_map/ppermute | solution.py:30
  41.8 5.5 %collective-permute-start.13 = (f32[32,1024]{1,0:T(8,128)S(1)}, f32[32,1024]{1,0:T(8,128)S(1)}, u32[]{:S(2)}, u32[]{:S(2)}) collective-permute-start(f32[32,1024]{1,0:T(8,128)S(1)} %pad_maximum_fusion), channel_id=1, source_target_pairs={{0,96},{16,112},{32,64},{48,80},{64,32},{80,48},{96,0},{112,16},{1... | collective-permute-start | bytes 393224 | tf_op jit(solution)/shard_map/ppermute | solution.py:30
  42.5 9.8 %copy-start.2 = (f32[1,1,256,256]{3,2,1,0:T(8,128)S(1)}, f32[1,1,256,256]{3,2,1,0:T(8,128)}, u32[]{:S(2)}) copy-start(f32[1,1,256,256]{3,2,1,0:T(8,128)} %param.9) | copy-start | bytes 786436
  47.3 5.0 %collective-permute-start.14 = (f32[128,1024]{1,0:T(8,128)S(1)}, f32[128,1024]{1,0:T(8,128)S(1)}, u32[]{:S(2)}, u32[]{:S(2)}) collective-permute-start(f32[128,1024]{1,0:T(8,128)S(1)} %constant_dynamic-update-slice_fusion.7.f), channel_id=1, source_target_pairs={{0,16},{16,0},{32,48},{48,32},{64,80},{80,64},{96,112},{112,96},{1... | collective-permute-start | bytes 1572872 | tf_op jit(solution)/shard_map/ppermute | solution.py:73
  55.0 4.2 %collective-permute-start.15 = (f32[80,256]{1,0:T(8,128)S(1)}, f32[80,256]{1,0:T(8,128)S(1)}, u32[]{:S(2)}, u32[]{:S(2)}) collective-permute-start(f32[80,256]{1,0:T(8,128)S(1)} %get-tuple-element.38), channel_id=1, source_target_pairs={{0,1},{1,0},{2,3},{3,2},{4,5},{5,4},{6,7},{7,6},{8,9},{9,8},{10,11... | collective-permute-start | bytes 245768 | tf_op jit(solution)/shard_map/ppermute | solution.py:30
  56.6 6.5 %collective-permute-start.16 = (f32[80,256]{1,0:T(8,128)S(1)}, f32[80,256]{1,0:T(8,128)S(1)}, u32[]{:S(2)}, u32[]{:S(2)}) collective-permute-start(f32[80,256]{1,0:T(8,128)S(1)} %get-tuple-element.39), channel_id=1, source_target_pairs={{0,2},{1,3},{2,0},{3,1},{4,6},{5,7},{6,4},{7,5},{8,10},{9,11},{10,... | collective-permute-start | bytes 245768 | tf_op jit(solution)/shard_map/ppermute | solution.py:30
  59.2 5.9 %collective-permute-start.17 = (f32[80,256]{1,0:T(8,128)S(1)}, f32[80,256]{1,0:T(8,128)S(1)}, u32[]{:S(2)}, u32[]{:S(2)}) collective-permute-start(f32[80,256]{1,0:T(8,128)S(1)} %get-tuple-element.40), channel_id=1, source_target_pairs={{0,3},{1,2},{2,1},{3,0},{4,7},{5,6},{6,5},{7,4},{8,11},{9,10},{10,... | collective-permute-start | bytes 245768 | tf_op jit(solution)/shard_map/ppermute | solution.py:30
  65.2 4.8 %collective-permute-start.18 = (f32[48,256]{1,0:T(8,128)S(1)}, f32[48,256]{1,0:T(8,128)S(1)}, u32[]{:S(2)}, u32[]{:S(2)}) collective-permute-start(f32[48,256]{1,0:T(8,128)S(1)} %get-tuple-element.42), channel_id=1, source_target_pairs={{0,4},{1,5},{2,6},{3,7},{4,0},{5,1},{6,2},{7,3},{8,12},{9,13},{10,... | collective-permute-start | bytes 147464 | tf_op jit(solution)/shard_map/ppermute | solution.py:352
  70.0 5.7 %collective-permute-start.19 = (f32[32,256]{1,0:T(8,128)S(1)}, f32[32,256]{1,0:T(8,128)S(1)}, u32[]{:S(2)}, u32[]{:S(2)}) collective-permute-start(f32[32,256]{1,0:T(8,128)S(1)} %slice.34), channel_id=1, source_target_pairs={{0,12},{1,13},{2,14},{3,15},{4,8},{5,9},{6,10},{7,11},{8,4},{9,5},... | collective-permute-start | bytes 98312 | tf_op jit(solution)/shard_map/ppermute | solution.py:353
  75.7 3.0 %collective-permute-start.20 = (f32[40,256]{1,0:T(8,128)S(1)}, f32[40,256]{1,0:T(8,128)S(1)}, u32[]{:S(2)}, u32[]{:S(2)}) collective-permute-start(f32[40,256]{1,0:T(8,128)S(1)} %concatenate.36), channel_id=1, source_target_pairs={{0,128},{16,144},{32,160},{48,176},{64,192},{80,208},{96,224},{112... | collective-permute-start | bytes 122888 | tf_op jit(solution)/shard_map/ppermute | solution.py:67
  78.8 4.0 %collective-permute-start.21 = (f32[80,256]{1,0:T(8,128)S(1)}, f32[80,256]{1,0:T(8,128)S(1)}, u32[]{:S(2)}, u32[]{:S(2)}) collective-permute-start(f32[80,256]{1,0:T(8,128)S(1)} %pad_maximum_fusion.1), channel_id=1, source_target_pairs={{0,32},{16,48},{32,0},{48,16},{64,96},{80,112},{96,64},{112,80},{1... | collective-permute-start | bytes 245768 | tf_op jit(solution)/shard_map/ppermute | solution.py:30
  78.9 4.9 %collective-permute-start.22 = (f32[80,256]{1,0:T(8,128)S(1)}, f32[80,256]{1,0:T(8,128)S(1)}, u32[]{:S(2)}, u32[]{:S(2)}) collective-permute-start(f32[80,256]{1,0:T(8,128)S(1)} %pad_maximum_fusion.1), channel_id=1, source_target_pairs={{0,64},{16,80},{32,96},{48,112},{64,0},{80,16},{96,32},{112,48},{1... | collective-permute-start | bytes 245768 | tf_op jit(solution)/shard_map/ppermute | solution.py:30
  80.4 4.5 %collective-permute-start.23 = (f32[80,256]{1,0:T(8,128)S(1)}, f32[80,256]{1,0:T(8,128)S(1)}, u32[]{:S(2)}, u32[]{:S(2)}) collective-permute-start(f32[80,256]{1,0:T(8,128)S(1)} %pad_maximum_fusion.1), channel_id=1, source_target_pairs={{0,96},{16,112},{32,64},{48,80},{64,32},{80,48},{96,0},{112,16},{1... | collective-permute-start | bytes 245768 | tf_op jit(solution)/shard_map/ppermute | solution.py:30
  84.9 7.1 %collective-permute-start.24 = (f32[320,256]{1,0:T(8,128)S(1)}, f32[320,256]{1,0:T(8,128)S(1)}, u32[]{:S(2)}, u32[]{:S(2)}) collective-permute-start(f32[320,256]{1,0:T(8,128)S(1)} %constant_dynamic-update-slice_fusion.12.f), channel_id=1, source_target_pairs={{0,16},{16,0},{32,48},{48,32},{64,80},{80,64},{96,112},{112,96},{1... | collective-permute-start | bytes 983048 | tf_op jit(solution)/shard_map/ppermute | solution.py:73
  92.1 6.7 %collective-permute-start.25 = (f32[32,256]{1,0:T(8,128)S(1)}, f32[32,256]{1,0:T(8,128)S(1)}, u32[]{:S(2)}, u32[]{:S(2)}) collective-permute-start(f32[32,256]{1,0:T(8,128)S(1)} %get-tuple-element.44), channel_id=1, source_target_pairs={{0,4},{1,5},{2,6},{3,7},{4,0},{5,1},{6,2},{7,3},{8,12},{9,13},{10,... | collective-permute-start | bytes 98312 | tf_op jit(solution)/shard_map/ppermute | solution.py:359
  98.8 8.2 %collective-permute-start.26 = (f32[64,256]{1,0:T(8,128)S(1)}, f32[64,256]{1,0:T(8,128)S(1)}, u32[]{:S(2)}, u32[]{:S(2)}) collective-permute-start(f32[64,256]{1,0:T(8,128)S(1)} %pad_maximum_fusion.2.near), channel_id=1, source_target_pairs={{0,12},{1,13},{2,14},{3,15},{4,8},{5,9},{6,10},{7,11},{8,4},{9,5},... | collective-permute-start | bytes 196616 | tf_op jit(solution)/shard_map/ppermute | solution.py:362
  107.4 4.9 %collective-permute-start.27 = (f32[32,256]{1,0:T(8,128)S(1)}, f32[32,256]{1,0:T(8,128)S(1)}, u32[]{:S(2)}, u32[]{:S(2)}) collective-permute-start(f32[32,256]{1,0:T(8,128)S(1)} %get-tuple-element.51), channel_id=1, source_target_pairs={{0,1},{1,0},{2,3},{3,2},{4,5},{5,4},{6,7},{7,6},{8,9},{9,8},{10,11... | collective-permute-start | bytes 98312 | tf_op jit(solution)/shard_map/ppermute | solution.py:30
  107.5 4.8 %collective-permute-start.28 = (f32[32,256]{1,0:T(8,128)S(1)}, f32[32,256]{1,0:T(8,128)S(1)}, u32[]{:S(2)}, u32[]{:S(2)}) collective-permute-start(f32[32,256]{1,0:T(8,128)S(1)} %get-tuple-element.52), channel_id=1, source_target_pairs={{0,2},{1,3},{2,0},{3,1},{4,6},{5,7},{6,4},{7,5},{8,10},{9,11},{10,... | collective-permute-start | bytes 98312 | tf_op jit(solution)/shard_map/ppermute | solution.py:30
  109.2 4.3 %collective-permute-start.29 = (f32[32,256]{1,0:T(8,128)S(1)}, f32[32,256]{1,0:T(8,128)S(1)}, u32[]{:S(2)}, u32[]{:S(2)}) collective-permute-start(f32[32,256]{1,0:T(8,128)S(1)} %get-tuple-element.53), channel_id=1, source_target_pairs={{0,3},{1,2},{2,1},{3,0},{4,7},{5,6},{6,5},{7,4},{8,11},{9,10},{10,... | collective-permute-start | bytes 98312 | tf_op jit(solution)/shard_map/ppermute | solution.py:30
  (3 other events, 2.5 us)

commit v4 on v3

--- a/solution.py
+++ b/solution.py
@@ -22,6 +22,9 @@
 
 CORE, ZPAIR = swap(1), swap(8)
 NEAR = (1, 3, 2)
+
+
+BOTH = [(i * 16 + j, (i ^ 8) * 16 + (j ^ 12)) for i in range(16) for j in range(16)]
 
 
 def exchange(parts, axis, unit):
@@ -61,10 +64,6 @@
         compiler_params=pltpu.CompilerParams(vmem_limit_bytes=24 * 2**20),
         cost_estimate=pl.CostEstimate(flops=flops or 200_000_000, bytes_accessed=1_000_000, transcendentals=0),
     )(*args)
-
-
-def gather_pair(shard):
-    return jnp.concatenate([shard, lax.ppermute(shard, "ops", ZPAIR)])
 
 
 def gather_rest(pair):
@@ -350,12 +349,13 @@
     got = exchange(parts, "sec", 1)
     kept, given = call(row_kernel, [shape(48, 256)] * 2, [], parts[0], got[1], got[2], got[3])
     half = kept + lax.ppermute(given, "sec", swap(4))
-    arrived = jnp.concatenate([half[:16], half[32:]]) + lax.ppermute(half[16:], "sec", swap(12))
-    target = (owner[0] * SLOTS + slot[0]).astype(F32)
-    packed = jnp.concatenate([arrived, jnp.broadcast_to(target, (8, 256))])
-    gram, routed = call(
-        route_kernel, [shape(256, 256), shape(32, 256)], [scratch(384, 256)], *gather_rest(gather_pair(packed))
-    )
+    target = jnp.broadcast_to((owner[0] * SLOTS + slot[0]).astype(F32), (8, 256))
+    own_rows = jnp.concatenate([half[:16], half[32:], target])
+    peer_rows = lax.ppermute(own_rows, "ops", ZPAIR)
+    owed = lax.ppermute(half[16:], "sec", swap(12))
+    peer_owed = lax.ppermute(half[16:], ("ops", "sec"), BOTH)
+    pair = jnp.concatenate([own_rows[:32] + owed, own_rows[32:], peer_rows[:32] + peer_owed, peer_rows[32:]])
+    gram, routed = call(route_kernel, [shape(256, 256), shape(32, 256)], [scratch(384, 256)], *gather_rest(pair))
     other = lax.ppermute(routed, "sec", swap(4))
     upper, begun = call(factor_first, [shape(128, 256), shape(128, 128)], [], gram, flops=HALF)
     near, upper, begun = lax.optimization_barrier((jnp.concatenate([routed, other]), upper, begun))

time: 115 us -> 113 us (0.983)
  starting transfers between devices: 52.4 us -> 50.9 us
  waiting for transfers between devices: 39.4 us -> 38.1 us
    ppermute x1, starting transfers between devices: 3.34 us -> 1.02 us  [step(): far = lax.ppermute(near, 'sec', swap(12))]
    ppermute x2 -> x3, waiting for transfers between devices: 3.56 us -> 2.67 us  [the longest x1 2.65 us: step(): peer_owed = lax.ppermute(half[16:], ('ops', 'sec'), BOTH)]
    ppermute x2 -> x3, starting transfers between devices: 5.14 us -> 5.67 us  [the longest x1 4.39 us: step(): owed = lax.ppermute(half[16:], 'sec', swap(12))]
    unnamed x19 -> x18, local copies, waits for them, and re-layouts: 2.55 us -> 2.54 us
  transfers between devices with their start and end apart: 30 -> 31, of which waited for: 19 -> 18; matrix products, arithmetic and copies ran while one was open for 0% -> 0% of each run, Pallas kernels for 9% -> 10%
where the time goes in v4:
time: 113 us; the launch traced here: 112 us
  starting transfers between devices  50.9 us (45%)
  waiting for transfers between devices  38.1 us (34%)
  Pallas kernels  16.4 us (15%)
  between operations  3.54 us (3%)
  local copies, waits for them, and re-layouts  2.6 us (2%)
    ppermute x18, waiting for transfers between devices, exchange(): got[d] = lax.ppermute(parts[d], axis, swap(d * unit))  27.7 us
    ppermute x18, starting transfers between devices, exchange(): got[d] = lax.ppermute(parts[d], axis, swap(d * unit))  24.4 us
    pallas_call x10, Pallas kernels, call(): pl.pallas_call(kernel, out_shape=out, in_specs=[VM] * len(args) if specs...  16.4 us
    ppermute x2, starting transfers between devices, gather_rest(): return (mine, lax.ppermute(mine, 'ops', CORE))  8.77 us
    ppermute x1, starting transfers between devices, step(): owed = lax.ppermute(half[16:], 'sec', swap(12))  4.39 us
    ppermute x1, waiting for transfers between devices, step(): other = lax.ppermute(total, 'ops', ZPAIR)  3.58 us
    ppermute x1, starting transfers between devices, step(): half = kept + lax.ppermute(given, 'sec', swap(4))  3.07 us
    ppermute x1, starting transfers between devices, step(): other = lax.ppermute(routed, 'sec', swap(4))  3 us
  transfers between devices with their start and end apart: 31, of which 18 were waited for; matrix products, arithmetic and copies ran while one was open for 0% of the time, Pallas kernels for 10%

profile of v4, /device:TPU:1, one launch (start us, length us, event | category | flops | bytes accessed | tf_op | source)
XLA Modules:
  0.0 111.6 jit_solution(16046624707346064024)
XLA Ops:
  0.6 2.5 %collective-permute-start = (f32[16,1024]{1,0:T(8,128)}, f32[16,1024]{1,0:T(8,128)S(1)}, u32[]{:S(2)}, u32[]{:S(2)}) collective-permute-start(f32[16,1024]{1,0:T(8,128)} %bitcast.14), channel_id=1, source_target_pairs={{0,128},{16,144},{32,160},{48,176},{64,192},{80,208},{96,224},{112... | collective-permute-start | bytes 196616 | tf_op jit(solution)/shard_map/ppermute | solution.py:303
  8.3 2.5 %collective-permute-start.2 = (f32[32,1024]{1,0:T(8,128)S(1)}, f32[32,1024]{1,0:T(8,128)S(1)}, u32[]{:S(2)}, u32[]{:S(2)}) collective-permute-start(f32[32,1024]{1,0:T(8,128)S(1)} %get-tuple-element.62), channel_id=1, source_target_pairs={{0,64},{16,80},{32,96},{48,112},{64,0},{80,16},{96,32},{112,48},{1... | collective-permute-start | bytes 393224 | tf_op jit(solution)/shard_map/ppermute | solution.py:33
  10.7 1.5 %collective-permute-start.4 = (f32[264,256]{1,0:T(8,128)S(1)}, f32[264,256]{1,0:T(8,128)S(1)}, u32[]{:S(2)}, u32[]{:S(2)}) collective-permute-start(f32[264,256]{1,0:T(8,128)S(1)} %get-tuple-element.29.b0), channel_id=1, source_target_pairs={{0,16},{16,0},{32,48},{48,32},{64,80},{80,64},{96,112},{112,96},{1... | collective-permute-start | bytes 811016 | tf_op jit(solution)/shard_map/ppermute | solution.py:314
  12.9 2.9 %collective-permute-done.2 = f32[32,1024]{1,0:T(8,128)S(1)} collective-permute-done((f32[32,1024]{1,0:T(8,128)S(1)}, f32[32,1024]{1,0:T(8,128)S(1)}, u32[]{:S(2)}, u32[]{:S(2)}) %collective-permute-start.2) | collective-permute-done | bytes 131104 | tf_op jit(solution)/shard_map/ppermute | solution.py:33
  15.9 4.4 %collective-permute-done.3 = f32[32,1024]{1,0:T(8,128)S(1)} collective-permute-done((f32[32,1024]{1,0:T(8,128)S(1)}, f32[32,1024]{1,0:T(8,128)S(1)}, u32[]{:S(2)}, u32[]{:S(2)}) %collective-permute-start.3) | collective-permute-done | bytes 131104 | tf_op jit(solution)/shard_map/ppermute | solution.py:33
  22.4 1.6 %shard_map.96 = (f32[32,1024]{1,0:T(8,128)S(1)}, f32[32,1024]{1,0:T(8,128)S(1)}, f32[32,1024]{1,0:T(8,128)S(1)}, f32[32,1024]{1,0:T(8,128)S(1)}) custom-call(s32[1]{0:T(128)S(6)} %copy.26.size, f32[128,1024]{1,0:T(8,128)S(1)} %constant_dynamic-update-slice_fusion.2.f, f32[128,1024]{1,0:T(8,128)S(1)} %collective-permute-done.6.g, ...), custom_call_target="tpu_custom_call" | custom-call | flops 200000000 | bytes 1000000 | tf_op jit(solution)/shard_map/pallas_call | solution.py:58
  24.1 1.9 %collective-permute-start.8 = (f32[32,1024]{1,0:T(8,128)S(1)}, f32[32,1024]{1,0:T(8,128)S(1)}, u32[]{:S(2)}, u32[]{:S(2)}) collective-permute-start(f32[32,1024]{1,0:T(8,128)S(1)} %get-tuple-element.35), channel_id=1, source_target_pairs={{0,64},{16,80},{32,96},{48,112},{64,0},{80,16},{96,32},{112,48},{1... | collective-permute-start | bytes 393224 | tf_op jit(solution)/shard_map/ppermute | solution.py:33
  26.0 2.0 %collective-permute-start.9 = (f32[32,1024]{1,0:T(8,128)S(1)}, f32[32,1024]{1,0:T(8,128)S(1)}, u32[]{:S(2)}, u32[]{:S(2)}) collective-permute-start(f32[32,1024]{1,0:T(8,128)S(1)} %get-tuple-element.36), channel_id=1, source_target_pairs={{0,96},{16,112},{32,64},{48,80},{64,32},{80,48},{96,0},{112,16},{1... | collective-permute-start | bytes 393224 | tf_op jit(solution)/shard_map/ppermute | solution.py:33
  28.8 3.3 %collective-permute-done.8 = f32[32,1024]{1,0:T(8,128)S(1)} collective-permute-done((f32[32,1024]{1,0:T(8,128)S(1)}, f32[32,1024]{1,0:T(8,128)S(1)}, u32[]{:S(2)}, u32[]{:S(2)}) %collective-permute-start.8) | collective-permute-done | bytes 131104 | tf_op jit(solution)/shard_map/ppermute | solution.py:33
  32.0 2.5 %collective-permute-done.9 = f32[32,1024]{1,0:T(8,128)S(1)} collective-permute-done((f32[32,1024]{1,0:T(8,128)S(1)}, f32[32,1024]{1,0:T(8,128)S(1)}, u32[]{:S(2)}, u32[]{:S(2)}) %collective-permute-start.9) | collective-permute-done | bytes 131104 | tf_op jit(solution)/shard_map/ppermute | solution.py:33
  34.9 3.6 %collective-permute-done.10 = f32[32,1024]{1,0:T(8,128)S(1)} collective-permute-done((f32[32,1024]{1,0:T(8,128)S(1)}, f32[32,1024]{1,0:T(8,128)S(1)}, u32[]{:S(2)}, u32[]{:S(2)}) %collective-permute-start.10) | collective-permute-done | bytes 131104 | tf_op jit(solution)/shard_map/ppermute | solution.py:335
  38.7 3.1 %collective-permute-start.12 = (f32[32,1024]{1,0:T(8,128)S(1)}, f32[32,1024]{1,0:T(8,128)S(1)}, u32[]{:S(2)}, u32[]{:S(2)}) collective-permute-start(f32[32,1024]{1,0:T(8,128)S(1)} %pad_maximum_fusion), channel_id=1, source_target_pairs={{0,64},{16,80},{32,96},{48,112},{64,0},{80,16},{96,32},{112,48},{1... | collective-permute-start | bytes 393224 | tf_op jit(solution)/shard_map/ppermute | solution.py:33
  42.5 3.2 %collective-permute-done.12 = f32[32,1024]{1,0:T(8,128)S(1)} collective-permute-done((f32[32,1024]{1,0:T(8,128)S(1)}, f32[32,1024]{1,0:T(8,128)S(1)}, u32[]{:S(2)}, u32[]{:S(2)}) %collective-permute-start.12) | collective-permute-done | bytes 131104 | tf_op jit(solution)/shard_map/ppermute | solution.py:33
  45.8 1.5 %collective-permute-done.13 = f32[32,1024]{1,0:T(8,128)S(1)} collective-permute-done((f32[32,1024]{1,0:T(8,128)S(1)}, f32[32,1024]{1,0:T(8,128)S(1)}, u32[]{:S(2)}, u32[]{:S(2)}) %collective-permute-start.13) | collective-permute-done | bytes 131104 | tf_op jit(solution)/shard_map/ppermute | solution.py:33
  47.3 3.4 %collective-permute-start.14 = (f32[128,1024]{1,0:T(8,128)S(1)}, f32[128,1024]{1,0:T(8,128)S(1)}, u32[]{:S(2)}, u32[]{:S(2)}) collective-permute-start(f32[128,1024]{1,0:T(8,128)S(1)} %constant_dynamic-update-slice_fusion.7.f), channel_id=1, source_target_pairs={{0,16},{16,0},{32,48},{48,32},{64,80},{80,64},{96,112},{112,96},{1... | collective-permute-start | bytes 1572872 | tf_op jit(solution)/shard_map/ppermute | solution.py:72
  50.8 1.5 %collective-permute-done.14.g = f32[128,1024]{1,0:T(8,128)S(1)} collective-permute-done((f32[128,1024]{1,0:T(8,128)S(1)}, f32[128,1024]{1,0:T(8,128)S(1)}, u32[]{:S(2)}, u32[]{:S(2)}) %collective-permute-start.14) | collective-permute-done | bytes 524320 | tf_op jit(solution)/shard_map/ppermute | solution.py:72
  52.3 2.7 %shard_map.97 = (f32[80,256]{1,0:T(8,128)S(1)}, f32[80,256]{1,0:T(8,128)S(1)}, f32[80,256]{1,0:T(8,128)S(1)}, f32[80,256]{1,0:T(8,128)S(1)}) custom-call(f32[128,1024]{1,0:T(8,128)S(1)} %constant_dynamic-update-slice_fusion.7.f, f32[128,1024]{1,0:T(8,128)S(1)} %collective-permute-done.14.g, f32[256,256]{1,0:T(8,128)S(1)} %bitcast.12, ...), custom_call_target="tpu_custom_call" | custom-call | flops 200000000 | bytes 1000000 | tf_op jit(solution)/shard_map/pallas_call | solution.py:58
  55.0 1.6 %collective-permute-start.15 = (f32[80,256]{1,0:T(8,128)S(1)}, f32[80,256]{1,0:T(8,128)S(1)}, u32[]{:S(2)}, u32[]{:S(2)}) collective-permute-start(f32[80,256]{1,0:T(8,128)S(1)} %get-tuple-element.38), channel_id=1, source_target_pairs={{0,1},{1,0},{2,3},{3,2},{4,5},{5,4},{6,7},{7,6},{8,9},{9,8},{10,11... | collective-permute-start | bytes 245768 | tf_op jit(solution)/shard_map/ppermute | solution.py:33
  56.6 2.6 %collective-permute-start.16 = (f32[80,256]{1,0:T(8,128)S(1)}, f32[80,256]{1,0:T(8,128)S(1)}, u32[]{:S(2)}, u32[]{:S(2)}) collective-permute-start(f32[80,256]{1,0:T(8,128)S(1)} %get-tuple-element.39), channel_id=1, source_target_pairs={{0,2},{1,3},{2,0},{3,1},{4,6},{5,7},{6,4},{7,5},{8,10},{9,11},{10,... | collective-permute-start | bytes 245768 | tf_op jit(solution)/shard_map/ppermute | solution.py:33
  59.2 3.9 %collective-permute-done.16.c = f32[80,256]{1,0:T(8,128)S(1)} collective-permute-done((f32[80,256]{1,0:T(8,128)S(1)}, f32[80,256]{1,0:T(8,128)S(1)}, u32[]{:S(2)}, u32[]{:S(2)}) %collective-permute-start.16) | collective-permute-done | bytes 81952 | tf_op jit(solution)/shard_map/ppermute | solution.py:33
  63.1 2.0 %collective-permute-done.17.d = f32[80,256]{1,0:T(8,128)S(1)} collective-permute-done((f32[80,256]{1,0:T(8,128)S(1)}, f32[80,256]{1,0:T(8,128)S(1)}, u32[]{:S(2)}, u32[]{:S(2)}) %collective-permute-start.17) | collective-permute-done | bytes 81952 | tf_op jit(solution)/shard_map/ppermute | solution.py:33
  65.2 3.1 %collective-permute-start.18 = (f32[48,256]{1,0:T(8,128)S(1)}, f32[48,256]{1,0:T(8,128)S(1)}, u32[]{:S(2)}, u32[]{:S(2)}) collective-permute-start(f32[48,256]{1,0:T(8,128)S(1)} %get-tuple-element.42), channel_id=1, source_target_pairs={{0,4},{1,5},{2,6},{3,7},{4,0},{5,1},{6,2},{7,3},{8,12},{9,13},{10,... | collective-permute-start | bytes 147464 | tf_op jit(solution)/shard_map/ppermute | solution.py:351
  70.0 4.4 %collective-permute-start.19 = (f32[32,256]{1,0:T(8,128)S(1)}, f32[32,256]{1,0:T(8,128)S(1)}, u32[]{:S(2)}, u32[]{:S(2)}) collective-permute-start(f32[32,256]{1,0:T(8,128)S(1)} %slice.45), channel_id=1, source_target_pairs={{0,12},{1,13},{2,14},{3,15},{4,8},{5,9},{6,10},{7,11},{8,4},{9,5},... | collective-permute-start | bytes 98312 | tf_op jit(solution)/shard_map/ppermute | solution.py:355
  75.8 2.7 %collective-permute-done.21 = f32[32,256]{1,0:T(8,128)S(1)} collective-permute-done((f32[32,256]{1,0:T(8,128)S(1)}, f32[32,256]{1,0:T(8,128)S(1)}, u32[]{:S(2)}, u32[]{:S(2)}) %collective-permute-start.21) | collective-permute-done | bytes 32800 | tf_op jit(solution)/shard_map/ppermute | solution.py:356
  78.5 1.5 %collective-permute-start.23 = (f32[80,256]{1,0:T(8,128)S(1)}, f32[80,256]{1,0:T(8,128)S(1)}, u32[]{:S(2)}, u32[]{:S(2)}) collective-permute-start(f32[80,256]{1,0:T(8,128)S(1)} %pad_maximum_fusion.1), channel_id=1, source_target_pairs={{0,64},{16,80},{32,96},{48,112},{64,0},{80,16},{96,32},{112,48},{1... | collective-permute-start | bytes 245768 | tf_op jit(solution)/shard_map/ppermute | solution.py:33
  80.1 2.3 %collective-permute-start.24 = (f32[80,256]{1,0:T(8,128)S(1)}, f32[80,256]{1,0:T(8,128)S(1)}, u32[]{:S(2)}, u32[]{:S(2)}) collective-permute-start(f32[80,256]{1,0:T(8,128)S(1)} %pad_maximum_fusion.1), channel_id=1, source_target_pairs={{0,96},{16,112},{32,64},{48,80},{64,32},{80,48},{96,0},{112,16},{1... | collective-permute-start | bytes 245768 | tf_op jit(solution)/shard_map/ppermute | solution.py:33
  84.6 5.3 %collective-permute-start.25 = (f32[320,256]{1,0:T(8,128)S(1)}, f32[320,256]{1,0:T(8,128)S(1)}, u32[]{:S(2)}, u32[]{:S(2)}) collective-permute-start(f32[320,256]{1,0:T(8,128)S(1)} %constant_dynamic-update-slice_fusion.12.f), channel_id=1, source_target_pairs={{0,16},{16,0},{32,48},{48,32},{64,80},{80,64},{96,112},{112,96},{1... | collective-permute-start | bytes 983048 | tf_op jit(solution)/shard_map/ppermute | solution.py:72
  91.3 3.0 %collective-permute-start.26 = (f32[32,256]{1,0:T(8,128)S(1)}, f32[32,256]{1,0:T(8,128)S(1)}, u32[]{:S(2)}, u32[]{:S(2)}) collective-permute-start(f32[32,256]{1,0:T(8,128)S(1)} %get-tuple-element.44), channel_id=1, source_target_pairs={{0,4},{1,5},{2,6},{3,7},{4,0},{5,1},{6,2},{7,3},{8,12},{9,13},{10,... | collective-permute-start | bytes 98312 | tf_op jit(solution)/shard_map/ppermute | solution.py:359
  94.3 4.5 %shard_map.100 = (f32[128,256]{1,0:T(8,128)S(1)}, f32[128,128]{1,0:T(8,128)S(1)}) custom-call(f32[256,256]{1,0:T(8,128)S(1)} %get-tuple-element.43.a), custom_call_target="tpu_custom_call" | custom-call | flops 4000000000 | bytes 1000000 | tf_op jit(solution)/shard_map/pallas_call | solution.py:58
  99.8 4.8 %shard_map.101.inverse = f32[256,256]{1,0:T(8,128)S(1)} custom-call(f32[256,256]{1,0:T(8,128)S(1)} %get-tuple-element.43.a, f32[128,256]{1,0:T(8,128)S(1)} %get-tuple-element.47.u0, f32[128,128]{1,0:T(8,128)S(1)} %get-tuple-element.48.v0), custom_call_target="tpu_custom_call" | custom-call | flops 4000000000 | bytes 1000000 | tf_op jit(solution)/shard_map/pallas_call | solution.py:58
  105.1 1.7 %collective-permute-start.29 = (f32[32,256]{1,0:T(8,128)S(1)}, f32[32,256]{1,0:T(8,128)S(1)}, u32[]{:S(2)}, u32[]{:S(2)}) collective-permute-start(f32[32,256]{1,0:T(8,128)S(1)} %get-tuple-element.52), channel_id=1, source_target_pairs={{0,2},{1,3},{2,0},{3,1},{4,6},{5,7},{6,4},{7,5},{8,10},{9,11},{10,... | collective-permute-start | bytes 98312 | tf_op jit(solution)/shard_map/ppermute | solution.py:33
  106.8 2.2 %collective-permute-start.30 = (f32[32,256]{1,0:T(8,128)S(1)}, f32[32,256]{1,0:T(8,128)S(1)}, u32[]{:S(2)}, u32[]{:S(2)}) collective-permute-start(f32[32,256]{1,0:T(8,128)S(1)} %get-tuple-element.53), channel_id=1, source_target_pairs={{0,3},{1,2},{2,1},{3,0},{4,7},{5,6},{6,5},{7,4},{8,11},{9,10},{10,... | collective-permute-start | bytes 98312 | tf_op jit(solution)/shard_map/ppermute | solution.py:33
  (77 shorter events, 18.3 us)
Async XLA Ops:
  0.6 6.3 %collective-permute-start = (f32[16,1024]{1,0:T(8,128)}, f32[16,1024]{1,0:T(8,128)S(1)}, u32[]{:S(2)}, u32[]{:S(2)}) collective-permute-start(f32[16,1024]{1,0:T(8,128)} %bitcast.14), channel_id=1, source_target_pairs={{0,128},{16,144},{32,160},{48,176},{64,192},{80,208},{96,224},{112... | collective-permute-start | bytes 196616 | tf_op jit(solution)/shard_map/ppermute | solution.py:303
  7.0 6.0 %collective-permute-start.1 = (f32[32,1024]{1,0:T(8,128)S(1)}, f32[32,1024]{1,0:T(8,128)S(1)}, u32[]{:S(2)}, u32[]{:S(2)}) collective-permute-start(f32[32,1024]{1,0:T(8,128)S(1)} %get-tuple-element.62), channel_id=1, source_target_pairs={{0,32},{16,48},{32,0},{48,16},{64,96},{80,112},{96,64},{112,80},{1... | collective-permute-start | bytes 393224 | tf_op jit(solution)/shard_map/ppermute | solution.py:33
  8.3 7.6 %collective-permute-start.2 = (f32[32,1024]{1,0:T(8,128)S(1)}, f32[32,1024]{1,0:T(8,128)S(1)}, u32[]{:S(2)}, u32[]{:S(2)}) collective-permute-start(f32[32,1024]{1,0:T(8,128)S(1)} %get-tuple-element.62), channel_id=1, source_target_pairs={{0,64},{16,80},{32,96},{48,112},{64,0},{80,16},{96,32},{112,48},{1... | collective-permute-start | bytes 393224 | tf_op jit(solution)/shard_map/ppermute | solution.py:33
  10.7 9.6 %collective-permute-start.4 = (f32[264,256]{1,0:T(8,128)S(1)}, f32[264,256]{1,0:T(8,128)S(1)}, u32[]{:S(2)}, u32[]{:S(2)}) collective-permute-start(f32[264,256]{1,0:T(8,128)S(1)} %get-tuple-element.29.b0), channel_id=1, source_target_pairs={{0,16},{16,0},{32,48},{48,32},{64,80},{80,64},{96,112},{112,96},{1... | collective-permute-start | bytes 811016 | tf_op jit(solution)/shard_map/ppermute | solution.py:314
  12.2 8.0 %collective-permute-start.5 = (f32[256,256]{1,0:T(8,128)S(1)}, f32[256,256]{1,0:T(8,128)S(1)}, u32[]{:S(2)}, u32[]{:S(2)}) collective-permute-start(f32[256,256]{1,0:T(8,128)S(1)} %bitcast.9), channel_id=1, source_target_pairs={{0,16},{16,0},{32,48},{48,32},{64,80},{80,64},{96,112},{112,96},{1... | collective-permute-start | bytes 786440 | tf_op jit(solution)/shard_map/ppermute | solution.py:315
  12.2 8.0 %collective-permute-start.3 = (f32[32,1024]{1,0:T(8,128)S(1)}, f32[32,1024]{1,0:T(8,128)S(1)}, u32[]{:S(2)}, u32[]{:S(2)}) collective-permute-start(f32[32,1024]{1,0:T(8,128)S(1)} %get-tuple-element.62), channel_id=1, source_target_pairs={{0,96},{16,112},{32,64},{48,80},{64,32},{80,48},{96,0},{112,16},{1... | collective-permute-start | bytes 393224 | tf_op jit(solution)/shard_map/ppermute | solution.py:33
  20.3 2.1 %collective-permute-start.6 = (f32[128,1024]{1,0:T(8,128)S(1)}, f32[128,1024]{1,0:T(8,128)S(1)}, u32[]{:S(2)}, u32[]{:S(2)}) collective-permute-start(f32[128,1024]{1,0:T(8,128)S(1)} %constant_dynamic-update-slice_fusion.2.f), channel_id=1, source_target_pairs={{0,16},{16,0},{32,48},{48,32},{64,80},{80,64},{96,112},{112,96},{1... | collective-permute-start | bytes 1572872 | tf_op jit(solution)/shard_map/ppermute | solution.py:326
  24.0 4.8 %collective-permute-start.7 = (f32[32,1024]{1,0:T(8,128)S(1)}, f32[32,1024]{1,0:T(8,128)S(1)}, u32[]{:S(2)}, u32[]{:S(2)}) collective-permute-start(f32[32,1024]{1,0:T(8,128)S(1)} %get-tuple-element.34), channel_id=1, source_target_pairs={{0,32},{16,48},{32,0},{48,16},{64,96},{80,112},{96,64},{112,80},{1... | collective-permute-start | bytes 393224 | tf_op jit(solution)/shard_map/ppermute | solution.py:33
  24.1 7.9 %collective-permute-start.8 = (f32[32,1024]{1,0:T(8,128)S(1)}, f32[32,1024]{1,0:T(8,128)S(1)}, u32[]{:S(2)}, u32[]{:S(2)}) collective-permute-start(f32[32,1024]{1,0:T(8,128)S(1)} %get-tuple-element.35), channel_id=1, source_target_pairs={{0,64},{16,80},{32,96},{48,112},{64,0},{80,16},{96,32},{112,48},{1... | collective-permute-start | bytes 393224 | tf_op jit(solution)/shard_map/ppermute | solution.py:33
  26.0 8.6 %collective-permute-start.9 = (f32[32,1024]{1,0:T(8,128)S(1)}, f32[32,1024]{1,0:T(8,128)S(1)}, u32[]{:S(2)}, u32[]{:S(2)}) collective-permute-start(f32[32,1024]{1,0:T(8,128)S(1)} %get-tuple-element.36), channel_id=1, source_target_pairs={{0,96},{16,112},{32,64},{48,80},{64,32},{80,48},{96,0},{112,16},{1... | collective-permute-start | bytes 393224 | tf_op jit(solution)/shard_map/ppermute | solution.py:33
  34.6 3.9 %collective-permute-start.10 = (f32[32,1024]{1,0:T(8,128)S(1)}, f32[32,1024]{1,0:T(8,128)S(1)}, u32[]{:S(2)}, u32[]{:S(2)}) collective-permute-start(f32[32,1024]{1,0:T(8,128)S(1)} %add_add_fusion), channel_id=1, source_target_pairs={{0,128},{16,144},{32,160},{48,176},{64,192},{80,208},{96,224},{112... | collective-permute-start | bytes 393224 | tf_op jit(solution)/shard_map/ppermute | solution.py:335
  38.6 3.9 %collective-permute-start.11 = (f32[32,1024]{1,0:T(8,128)S(1)}, f32[32,1024]{1,0:T(8,128)S(1)}, u32[]{:S(2)}, u32[]{:S(2)}) collective-permute-start(f32[32,1024]{1,0:T(8,128)S(1)} %pad_maximum_fusion), channel_id=1, source_target_pairs={{0,32},{16,48},{32,0},{48,16},{64,96},{80,112},{96,64},{112,80},{1... | collective-permute-start | bytes 393224 | tf_op jit(solution)/shard_map/ppermute | solution.py:33
  38.7 7.1 %collective-permute-start.12 = (f32[32,1024]{1,0:T(8,128)S(1)}, f32[32,1024]{1,0:T(8,128)S(1)}, u32[]{:S(2)}, u32[]{:S(2)}) collective-permute-start(f32[32,1024]{1,0:T(8,128)S(1)} %pad_maximum_fusion), channel_id=1, source_target_pairs={{0,64},{16,80},{32,96},{48,112},{64,0},{80,16},{96,32},{112,48},{1... | collective-permute-start | bytes 393224 | tf_op jit(solution)/shard_map/ppermute | solution.py:33
  41.8 5.5 %collective-permute-start.13 = (f32[32,1024]{1,0:T(8,128)S(1)}, f32[32,1024]{1,0:T(8,128)S(1)}, u32[]{:S(2)}, u32[]{:S(2)}) collective-permute-start(f32[32,1024]{1,0:T(8,128)S(1)} %pad_maximum_fusion), channel_id=1, source_target_pairs={{0,96},{16,112},{32,64},{48,80},{64,32},{80,48},{96,0},{112,16},{1... | collective-permute-start | bytes 393224 | tf_op jit(solution)/shard_map/ppermute | solution.py:33
  42.5 9.8 %copy-start.2 = (f32[1,1,256,256]{3,2,1,0:T(8,128)S(1)}, f32[1,1,256,256]{3,2,1,0:T(8,128)}, u32[]{:S(2)}) copy-start(f32[1,1,256,256]{3,2,1,0:T(8,128)} %param.9) | copy-start | bytes 786436
  47.3 5.0 %collective-permute-start.14 = (f32[128,1024]{1,0:T(8,128)S(1)}, f32[128,1024]{1,0:T(8,128)S(1)}, u32[]{:S(2)}, u32[]{:S(2)}) collective-permute-start(f32[128,1024]{1,0:T(8,128)S(1)} %constant_dynamic-update-slice_fusion.7.f), channel_id=1, source_target_pairs={{0,16},{16,0},{32,48},{48,32},{64,80},{80,64},{96,112},{112,96},{1... | collective-permute-start | bytes 1572872 | tf_op jit(solution)/shard_map/ppermute | solution.py:72
  55.0 4.2 %collective-permute-start.15 = (f32[80,256]{1,0:T(8,128)S(1)}, f32[80,256]{1,0:T(8,128)S(1)}, u32[]{:S(2)}, u32[]{:S(2)}) collective-permute-start(f32[80,256]{1,0:T(8,128)S(1)} %get-tuple-element.38), channel_id=1, source_target_pairs={{0,1},{1,0},{2,3},{3,2},{4,5},{5,4},{6,7},{7,6},{8,9},{9,8},{10,11... | collective-permute-start | bytes 245768 | tf_op jit(solution)/shard_map/ppermute | solution.py:33
  56.6 6.5 %collective-permute-start.16 = (f32[80,256]{1,0:T(8,128)S(1)}, f32[80,256]{1,0:T(8,128)S(1)}, u32[]{:S(2)}, u32[]{:S(2)}) collective-permute-start(f32[80,256]{1,0:T(8,128)S(1)} %get-tuple-element.39), channel_id=1, source_target_pairs={{0,2},{1,3},{2,0},{3,1},{4,6},{5,7},{6,4},{7,5},{8,10},{9,11},{10,... | collective-permute-start | bytes 245768 | tf_op jit(solution)/shard_map/ppermute | solution.py:33
  59.2 5.9 %collective-permute-start.17 = (f32[80,256]{1,0:T(8,128)S(1)}, f32[80,256]{1,0:T(8,128)S(1)}, u32[]{:S(2)}, u32[]{:S(2)}) collective-permute-start(f32[80,256]{1,0:T(8,128)S(1)} %get-tuple-element.40), channel_id=1, source_target_pairs={{0,3},{1,2},{2,1},{3,0},{4,7},{5,6},{6,5},{7,4},{8,11},{9,10},{10,... | collective-permute-start | bytes 245768 | tf_op jit(solution)/shard_map/ppermute | solution.py:33
  65.2 4.8 %collective-permute-start.18 = (f32[48,256]{1,0:T(8,128)S(1)}, f32[48,256]{1,0:T(8,128)S(1)}, u32[]{:S(2)}, u32[]{:S(2)}) collective-permute-start(f32[48,256]{1,0:T(8,128)S(1)} %get-tuple-element.42), channel_id=1, source_target_pairs={{0,4},{1,5},{2,6},{3,7},{4,0},{5,1},{6,2},{7,3},{8,12},{9,13},{10,... | collective-permute-start | bytes 147464 | tf_op jit(solution)/shard_map/ppermute | solution.py:351
  70.0 5.7 %collective-permute-start.19 = (f32[32,256]{1,0:T(8,128)S(1)}, f32[32,256]{1,0:T(8,128)S(1)}, u32[]{:S(2)}, u32[]{:S(2)}) collective-permute-start(f32[32,256]{1,0:T(8,128)S(1)} %slice.45), channel_id=1, source_target_pairs={{0,12},{1,13},{2,14},{3,15},{4,8},{5,9},{6,10},{7,11},{8,4},{9,5},... | collective-permute-start | bytes 98312 | tf_op jit(solution)/shard_map/ppermute | solution.py:355
  74.4 4.0 %collective-permute-start.21 = (f32[32,256]{1,0:T(8,128)S(1)}, f32[32,256]{1,0:T(8,128)S(1)}, u32[]{:S(2)}, u32[]{:S(2)}) collective-permute-start(f32[32,256]{1,0:T(8,128)S(1)} %slice.45), channel_id=1, source_target_pairs={{0,140},{1,141},{2,142},{3,143},{4,136},{5,137},{6,138},{7,139},{8... | collective-permute-start | bytes 98312 | tf_op jit(solution)/shard_map/ppermute | solution.py:356
  74.4 4.0 %collective-permute-start.20 = (f32[40,256]{1,0:T(8,128)S(1)}, f32[40,256]{1,0:T(8,128)S(1)}, u32[]{:S(2)}, u32[]{:S(2)}) collective-permute-start(f32[40,256]{1,0:T(8,128)S(1)} %pad_maximum_fusion.3), channel_id=1, source_target_pairs={{0,128},{16,144},{32,160},{48,176},{64,192},{80,208},{96,224},{112... | collective-permute-start | bytes 122888 | tf_op jit(solution)/shard_map/ppermute | solution.py:354
  78.4 3.9 %collective-permute-start.22 = (f32[80,256]{1,0:T(8,128)S(1)}, f32[80,256]{1,0:T(8,128)S(1)}, u32[]{:S(2)}, u32[]{:S(2)}) collective-permute-start(f32[80,256]{1,0:T(8,128)S(1)} %pad_maximum_fusion.1), channel_id=1, source_target_pairs={{0,32},{16,48},{32,0},{48,16},{64,96},{80,112},{96,64},{112,80},{1... | collective-permute-start | bytes 245768 | tf_op jit(solution)/shard_map/ppermute | solution.py:33
  78.5 4.9 %collective-permute-start.23 = (f32[80,256]{1,0:T(8,128)S(1)}, f32[80,256]{1,0:T(8,128)S(1)}, u32[]{:S(2)}, u32[]{:S(2)}) collective-permute-start(f32[80,256]{1,0:T(8,128)S(1)} %pad_maximum_fusion.1), channel_id=1, source_target_pairs={{0,64},{16,80},{32,96},{48,112},{64,0},{80,16},{96,32},{112,48},{1... | collective-permute-start | bytes 245768 | tf_op jit(solution)/shard_map/ppermute | solution.py:33
  80.1 4.5 %collective-permute-start.24 = (f32[80,256]{1,0:T(8,128)S(1)}, f32[80,256]{1,0:T(8,128)S(1)}, u32[]{:S(2)}, u32[]{:S(2)}) collective-permute-start(f32[80,256]{1,0:T(8,128)S(1)} %pad_maximum_fusion.1), channel_id=1, source_target_pairs={{0,96},{16,112},{32,64},{48,80},{64,32},{80,48},{96,0},{112,16},{1... | collective-permute-start | bytes 245768 | tf_op jit(solution)/shard_map/ppermute | solution.py:33
  84.6 6.6 %collective-permute-start.25 = (f32[320,256]{1,0:T(8,128)S(1)}, f32[320,256]{1,0:T(8,128)S(1)}, u32[]{:S(2)}, u32[]{:S(2)}) collective-permute-start(f32[320,256]{1,0:T(8,128)S(1)} %constant_dynamic-update-slice_fusion.12.f), channel_id=1, source_target_pairs={{0,16},{16,0},{32,48},{48,32},{64,80},{80,64},{96,112},{112,96},{1... | collective-permute-start | bytes 983048 | tf_op jit(solution)/shard_map/ppermute | solution.py:72
  91.3 7.5 %collective-permute-start.26 = (f32[32,256]{1,0:T(8,128)S(1)}, f32[32,256]{1,0:T(8,128)S(1)}, u32[]{:S(2)}, u32[]{:S(2)}) collective-permute-start(f32[32,256]{1,0:T(8,128)S(1)} %get-tuple-element.44), channel_id=1, source_target_pairs={{0,4},{1,5},{2,6},{3,7},{4,0},{5,1},{6,2},{7,3},{8,12},{9,13},{10,... | collective-permute-start | bytes 98312 | tf_op jit(solution)/shard_map/ppermute | solution.py:359
  98.8 5.9 %collective-permute-start.27 = (f32[64,256]{1,0:T(8,128)S(1)}, f32[64,256]{1,0:T(8,128)S(1)}, u32[]{:S(2)}, u32[]{:S(2)}) collective-permute-start(f32[64,256]{1,0:T(8,128)S(1)} %pad_maximum_fusion.2.near), channel_id=1, source_target_pairs={{0,12},{1,13},{2,14},{3,15},{4,8},{5,9},{6,10},{7,11},{8,4},{9,5},... | collective-permute-start | bytes 196616 | tf_op jit(solution)/shard_map/ppermute | solution.py:362
  105.0 4.9 %collective-permute-start.28 = (f32[32,256]{1,0:T(8,128)S(1)}, f32[32,256]{1,0:T(8,128)S(1)}, u32[]{:S(2)}, u32[]{:S(2)}) collective-permute-start(f32[32,256]{1,0:T(8,128)S(1)} %get-tuple-element.51), channel_id=1, source_target_pairs={{0,1},{1,0},{2,3},{3,2},{4,5},{5,4},{6,7},{7,6},{8,9},{9,8},{10,11... | collective-permute-start | bytes 98312 | tf_op jit(solution)/shard_map/ppermute | solution.py:33
  105.1 4.8 %collective-permute-start.29 = (f32[32,256]{1,0:T(8,128)S(1)}, f32[32,256]{1,0:T(8,128)S(1)}, u32[]{:S(2)}, u32[]{:S(2)}) collective-permute-start(f32[32,256]{1,0:T(8,128)S(1)} %get-tuple-element.52), channel_id=1, source_target_pairs={{0,2},{1,3},{2,0},{3,1},{4,6},{5,7},{6,4},{7,5},{8,10},{9,11},{10,... | collective-permute-start | bytes 98312 | tf_op jit(solution)/shard_map/ppermute | solution.py:33
  106.8 4.0 %collective-permute-start.30 = (f32[32,256]{1,0:T(8,128)S(1)}, f32[32,256]{1,0:T(8,128)S(1)}, u32[]{:S(2)}, u32[]{:S(2)}) collective-permute-start(f32[32,256]{1,0:T(8,128)S(1)} %get-tuple-element.53), channel_id=1, source_target_pairs={{0,3},{1,2},{2,1},{3,0},{4,7},{5,6},{6,5},{7,4},{8,11},{9,10},{10,... | collective-permute-start | bytes 98312 | tf_op jit(solution)/shard_map/ppermute | solution.py:33
  (4 other events, 7.8 us)
